TPU v7x, 256 devices: a whole 4x4x8 slice. The times are simulated.
256 devices in a mesh: expert: 32 (over x, y, core), dp: 8 (over z).
Axes of the slice: x: 4, y: 4, z: 8, core: 2. Of those that a mesh axis runs over, the one named last changes fastest.
Arguments:
- tokens: bfloat16 [32768, 1024], P(('expert', 'dp')), may hold values from -6 to 6
- expert_ids: int32 [32768, 8], P(('expert', 'dp')), may hold values from 0 to 63, all different within a row; in each aligned block of 128 rows (0 to 127, 128 to 255, ...) at most 24 rows name the same one
- combine_weights: float32 [32768, 8], P(('expert', 'dp')), may hold values from 0.2 to 1
- lift_weights: bfloat16 [64, 1024, 768], P('expert', 'dp'), may hold values from -0.1875 to 0.1875
- down_weights: bfloat16 [64, 384, 1024], P('expert', None, 'dp'), may hold values from -0.3125 to 0.3125
- cotangent: bfloat16 [32768, 1024], P(('expert', 'dp')), may hold values from -1.5 to 1.5
Outputs:
- layer_output: bfloat16 [32768, 1024], P(('expert', 'dp'))
- token_grads: bfloat16 [32768, 1024], P(('expert', 'dp'))
- lift_grads: bfloat16 [64, 1024, 768], P('expert', 'dp')
- down_grads: bfloat16 [64, 384, 1024], P('expert', None, 'dp')
Inputs may be any that keep to these rules, and one draw needn't show every extreme that they name: `expert_ids`: each row names 8 different experts. Among the 128 rows of one device, no expert is named more than 24 times, and in every draw some expert is named exactly 24 times in some device's rows.
All inputs are finite; a program needn't handle non-finite values.
Results may differ from a plain program's by a relative error of at most 0.02.
Values may be sent and summed in bfloat16 or wider, within the bound.
No kernel may reach another device: no remote copies, remote signals or barrier semaphores. Data moves between devices by JAX's collectives and lax.ppermute only.
A program may use at most 64 MiB of HBM per device.

v0:
```python
import jax
import jax.numpy as jnp
from jax import lax
from jax.sharding import PartitionSpec as P


def swish_parts(gate_part):
    sigmoid_val = jax.nn.sigmoid(gate_part)
    return (gate_part * sigmoid_val, sigmoid_val * (1.0 + gate_part * (1.0 - sigmoid_val)))


def collect(returned, target, tok_rows, top_count):
    flat_back = returned.reshape(-1, returned.shape[-1])
    return flat_back[target].reshape(tok_rows, top_count, returned.shape[-1])


def shards(tokens, expert_ids, combine_weights, lift_weights, down_weights, cotangent):
    tok_rows, top_count = expert_ids.shape
    local_experts = lift_weights.shape[0]
    hidden_width = down_weights.shape[1]
    model_width = tokens.shape[1]
    owners = lax.axis_size("expert")
    all_experts = local_experts * owners
    capacity = max(2, 3 * tok_rows * top_count // (2 * all_experts))
    slot_total = tok_rows * top_count
    flat_ids = expert_ids.reshape(-1)
    onehot = (flat_ids[:, None] == jnp.arange(all_experts, dtype=jnp.int32)[None, :]).astype(
        jnp.int32
    )
    ranking = jnp.sum(jnp.cumsum(onehot, axis=0) * onehot, axis=1) - 1
    target = (flat_ids % local_experts * owners + flat_ids // local_experts) * capacity + ranking
    source_of = (
        jnp.full((all_experts * capacity,), -1, jnp.int32)
        .at[target]
        .set(jnp.arange(slot_total, dtype=jnp.int32))
    )
    filled = (source_of >= 0)[:, None]
    source_slot = jnp.maximum(source_of, 0)
    source_row = source_slot // top_count
    slot_gates = combine_weights.reshape(-1)[source_slot]
    buffer_shape = (local_experts, owners, capacity, model_width)
    rows_shape = (local_experts, owners * capacity, model_width)
    send_rows = jnp.where(filled, tokens[source_row], jnp.zeros((), jnp.bfloat16)).reshape(
        buffer_shape
    )
    send_back = jnp.where(
        filled, slot_gates[:, None] * cotangent[source_row].astype(jnp.float32), 0.0
    )
    send_back = send_back.astype(jnp.bfloat16).reshape(buffer_shape)
    recv_rows = lax.all_to_all(
        send_rows, "expert", split_axis=1, concat_axis=1, tiled=True
    ).reshape(rows_shape)
    part_rows = recv_rows
    portion = lax.all_gather(lift_weights, "dp", axis=1, tiled=True)
    gate_term = jnp.einsum(
        "erd,edf->erf", part_rows, portion[:, :, :hidden_width], preferred_element_type=jnp.float32
    )
    up_term = jnp.einsum(
        "erd,edf->erf", part_rows, portion[:, :, hidden_width:], preferred_element_type=jnp.float32
    )
    gate_term, up_term = (gate_term, up_term)
    swished, slopes = swish_parts(gate_term)
    activated = (swished * up_term).astype(jnp.bfloat16)
    portion = lax.all_gather(down_weights, "dp", axis=2, tiled=True)
    result = jnp.stack(
        [
            jnp.dot(activated[expert], portion[expert], preferred_element_type=jnp.float32).astype(
                jnp.bfloat16
            )
            for expert in range(local_experts)
        ]
    )
    returned = lax.all_to_all(
        result.reshape(buffer_shape), "expert", split_axis=1, concat_axis=1, tiled=True
    )
    recv_back = lax.all_to_all(
        send_back, "expert", split_axis=1, concat_axis=1, tiled=True
    ).reshape(rows_shape)
    part_back = recv_back
    act_grad = jnp.einsum(
        "ern,efn->erf",
        part_back,
        lax.all_gather(down_weights, "dp", axis=2, tiled=True),
        preferred_element_type=jnp.float32,
    )
    grad_gate = (act_grad * up_term * slopes).astype(jnp.bfloat16)
    grad_up = (act_grad * swished).astype(jnp.bfloat16)
    portion = lax.all_gather(lift_weights, "dp", axis=1, tiled=True)
    contract = (((1,), (1,)), ((), ()))
    outputs = []
    for expert in range(local_experts):
        first = lax.dot_general(
            grad_gate[expert],
            portion[expert, :, :hidden_width],
            contract,
            preferred_element_type=jnp.float32,
        )
        second = lax.dot_general(
            grad_up[expert],
            portion[expert, :, hidden_width:],
            contract,
            preferred_element_type=jnp.float32,
        )
        outputs.append((first + second).astype(jnp.bfloat16))
    input_grads = jnp.stack(outputs)
    returned_grads = lax.all_to_all(
        input_grads.reshape(buffer_shape), "expert", split_axis=1, concat_axis=1, tiled=True
    )
    picked = collect(returned, target, tok_rows, top_count)
    layer_output = jnp.sum(combine_weights[:, :, None] * picked.astype(jnp.float32), axis=1).astype(
        jnp.bfloat16
    )
    grads_picked = collect(returned_grads, target, tok_rows, top_count)
    token_grads = jnp.sum(grads_picked.astype(jnp.float32), axis=1).astype(jnp.bfloat16)
    part_rows = recv_rows
    part_back = recv_back
    gate_grad = jnp.einsum("ern,erf->nef", part_rows, grad_gate, preferred_element_type=jnp.float32)
    up_grad = jnp.einsum("ern,erf->nef", part_rows, grad_up, preferred_element_type=jnp.float32)
    down_grad = jnp.einsum("ern,erf->nef", part_back, activated, preferred_element_type=jnp.float32)
    summed = lax.psum_scatter(
        jnp.concatenate([gate_grad, up_grad, down_grad], axis=2).astype(jnp.bfloat16),
        "dp",
        scatter_dimension=0,
        tiled=True,
    ).astype(jnp.float32)
    lift_grads = jnp.transpose(summed[:, :, : 2 * hidden_width], (1, 0, 2)).astype(jnp.bfloat16)
    down_grads = jnp.transpose(summed[:, :, 2 * hidden_width :], (1, 2, 0)).astype(jnp.bfloat16)
    return (layer_output, token_grads, lift_grads, down_grads)


def solution(mesh):
    in_specs = (
        P(("expert", "dp"), None),
        P(("expert", "dp"), None),
        P(("expert", "dp"), None),
        P("expert", "dp", None),
        P("expert", None, "dp"),
        P(("expert", "dp"), None),
    )
    out_specs = (
        P(("expert", "dp"), None),
        P(("expert", "dp"), None),
        P("expert", "dp", None),
        P("expert", None, "dp"),
    )
    return jax.shard_map(shards, mesh=mesh, in_specs=in_specs, out_specs=out_specs, check_vma=False)
```

profile of v0, /device:TPU:1, one launch (start us, length us, event | category | flops | bytes accessed | tf_op | source)
XLA Modules:
  0.0 293.6 jit_solution(7438763813437499192)
XLA Ops:
  7.9 0.8 copy.27
  8.9 18.0 %reduce-window.6 = s32[64,8,128]{2,1,0:T(8,128)S(1)} reduce-window(s32[64,8,128]{2,1,0:T(8,128)S(1)} %fusion.15, s32[]{:T(128)} %constant.56.clone.1), window={size=1x1x128 pad=0_0x0_0x127_0}, to_apply=%region_0.0 | reduce-window | flops 8323072 | bytes 524292 | tf_op jit(solution)/shard_map/reduce-window
  27.9 4.3 %scatter_custom_fusion = s32[1536]{0:T(1024)S(1)} fusion(s32[1024]{0:T(1024)S(1)} %bitcast.119, s32[1024]{0:T(1024)S(1)} %iota.11, s32[]{:T(128)} %constant.55.clone.1), kind=kCustom, calls=%fused_computation.75 | custom fusion | bytes 6148 | tf_op jit(solution)/shard_map/scatter | solution.py:35
  32.4 5.9 %gather_fusion.2 = f32[1536]{0:T(1024)S(1)} fusion(f32[1024]{0:T(1024)S(1)} %reshape.211, s32[2048]{0:T(1024)S(1)} %get-tuple-element.21), kind=kCustom, calls=%fused_computation.2 | custom fusion | bytes 18432 | tf_op jit(solution)/shard_map/gather | solution.py:40
  38.4 5.1 %gather_fusion.3 = bf16[1536,1024]{1,0:T(8,128)(2,1)S(1)} fusion(bf16[128,1024]{1,0:T(8,128)(2,1)S(1)} %copy-done, s32[2048]{0:T(1024)S(1)} %get-tuple-element.22), kind=kCustom, calls=%fused_computation.3 | custom fusion | bytes 6297600 | tf_op jit(solution)/shard_map/gather | solution.py:47
  43.5 2.2 fusion.1
  45.7 8.7 %all-to-all-start.2 = ((bf16[2,32,24,1024]{3,2,0,1:T(8,128)(2,1)}), bf16[2,32,24,1024]{3,2,0,1:T(8,128)(2,1)S(1)}, u32[]{:S(2)}, u32[]{:S(2)}) async-start(bf16[2,32,24,1024]{3,2,0,1:T(8,128)(2,1)} %fusion.1), calls=%async_computation.2 | async-start | bytes 6291456 | tf_op jit(solution)/shard_map/all_to_all | solution.py:76
  54.4 5.8 %gather_fusion = bf16[1536,1024]{1,0:T(8,128)(2,1)} fusion(bf16[128,1024]{1,0:T(8,128)(2,1)S(1)} %copy-done.2, s32[2048]{0:T(1024)S(1)} %get-tuple-element.22), kind=kCustom, calls=%fused_computation | custom fusion | bytes 6297600 | tf_op jit(solution)/shard_map/gather | solution.py:43
  60.2 3.3 %copy_select_fusion = bf16[2,32,24,1024]{3,2,0,1:T(8,128)(2,1)} fusion(bf16[2,32,24,1024]{3,2,1,0:T(8,128)(2,1)} %bitcast.103, pred[2,32,24]{2,0,1:T(4,128)(4,1)S(1)} %copy.32), kind=kLoop, calls=%fused_computation.14 | loop fusion | flops 1572864 | bytes 6292992 | tf_op jit(solution)/shard_map/jit(_where)/select_n | solution.py:43
  63.5 30.7 %all-to-all-done.2 = bf16[2,32,24,1024]{3,2,0,1:T(8,128)(2,1)S(1)} async-done(((bf16[2,32,24,1024]{3,2,0,1:T(8,128)(2,1)}), bf16[2,32,24,1024]{3,2,0,1:T(8,128)(2,1)S(1)}, u32[]{:S(2)}, u32[]{:S(2)}) %all-to-all-start.2) | async-done | bytes 3145760 | tf_op jit(solution)/shard_map/all_to_all | solution.py:76
  94.2 5.0 %all-to-all-start = ((bf16[2,32,24,1024]{3,2,0,1:T(8,128)(2,1)}), bf16[2,32,24,1024]{3,2,0,1:T(8,128)(2,1)}, u32[]{:S(2)}, u32[]{:S(2)}) async-start(bf16[2,32,24,1024]{3,2,0,1:T(8,128)(2,1)} %copy_select_fusion), calls=%async_computation | async-start | bytes 6291456 | tf_op jit(solution)/shard_map/all_to_all | solution.py:50
  99.3 0.7 all-gather.5.cloned.1.call-update
  100.2 2.1 copy.41
  102.3 36.7 %all-to-all-done = bf16[2,32,24,1024]{3,2,0,1:T(8,128)(2,1)} async-done(((bf16[2,32,24,1024]{3,2,0,1:T(8,128)(2,1)}), bf16[2,32,24,1024]{3,2,0,1:T(8,128)(2,1)}, u32[]{:S(2)}, u32[]{:S(2)}) %all-to-all-start) | async-done | bytes 3145760 | tf_op jit(solution)/shard_map/all_to_all | solution.py:50
  139.0 2.3 copy.34
  141.4 1.6 copy-done.6
  143.0 4.7 %fusion.4 = f32[2,768,384]{2,1,0:T(8,128)} fusion(bf16[2,768,1024]{2,1,0:T(8,128)(2,1)S(1)} %bitcast.109, bf16[2,1024,768]{2,1,0:T(8,128)(2,1)} %all-gather.3.cloned.1.call-done), kind=kOutput, calls=%fused_computation.28 | convolution fusion | flops 1207959552 | bytes 7077888 | tf_op jit(solution)/shard_map/erd,edf->erf/dot_general | solution.py:58
  147.8 5.2 %fusion.6 = f32[2,768,384]{2,1,0:T(8,128)} fusion(bf16[2,768,1024]{2,1,0:T(8,128)(2,1)} %bitcast.110, bf16[2,1024,768]{2,1,0:T(8,128)(2,1)S(1)} %copy-done.8), kind=kOutput, calls=%fused_computation.30 | convolution fusion | flops 1207959552 | bytes 7077888 | tf_op jit(solution)/shard_map/erd,edf->erf/dot_general | solution.py:55
  153.0 5.3 %multiply_convert_fusion = (bf16[2,768,384]{2,1,0:T(8,128)(2,1)S(1)}, bf16[2,768,384]{2,1,0:T(8,128)(2,1)S(1)}, bf16[2,768,384]{2,1,0:T(8,128)(2,1)S(1)}) fusion(f32[2,768,384]{2,1,0:T(8,128)} %fusion.6, f32[2,768,384]{2,1,0:T(8,128)} %fusion.4, bf16[2,768,1024]{2,1,0:T(8,128)(2,1)S(1)} %bitcast.107, bf16[2,384,1024]{2,1,0:T(8,128)(2,1)} %all-gather.5.cloned.1.call-done), kind=kOutput, calls=%fused_computation.17 | convolution fusion | flops 1216806912 | bytes 12976128 | tf_op jit(solution)/shard_map/ern,efn->erf/dot_general | solution.py:80
  158.4 1.4 fusion.10
  159.8 1.7 copy-done.7
  161.5 1.5 fusion.9
  163.0 1.5 fusion.8
  164.5 2.3 pad_maximum_fusion
  166.8 6.7 %copy.54 = bf16[1024,2304]{1,0:T(8,128)(2,1)} copy(bf16[1024,2304]{0,1:T(8,128)(2,1)} %bitcast.102) | data formatting | bytes 9437184
  173.6 1.4 copy-done.15
  175.3 1.0 convolution_convert_fusion.3
  176.3 1.0 convolution_convert_fusion.4
  177.3 1.9 pad_maximum_fusion.1
  179.2 5.0 %all-to-all-start.1 = ((bf16[2,32,24,1024]{3,2,0,1:T(8,128)(2,1)}), bf16[2,32,24,1024]{3,2,0,1:T(8,128)(2,1)S(1)}, u32[]{:S(2)}, u32[]{:S(2)}) async-start(bf16[2,32,24,1024]{3,2,0,1:T(8,128)(2,1)} %pad_maximum_fusion.1), calls=%async_computation.1 | async-start | bytes 6291456 | tf_op jit(solution)/shard_map/all_to_all | solution.py:73
  184.2 2.7 fusion.11
  187.3 1.0 fusion.12
  188.5 1.0 add_convert_fusion
  189.6 1.0 add_convert_fusion.1
  190.6 1.9 pad_maximum_fusion.2
  192.5 31.4 %all-to-all-done.1 = bf16[2,32,24,1024]{3,2,0,1:T(8,128)(2,1)S(1)} async-done(((bf16[2,32,24,1024]{3,2,0,1:T(8,128)(2,1)}), bf16[2,32,24,1024]{3,2,0,1:T(8,128)(2,1)S(1)}, u32[]{:S(2)}, u32[]{:S(2)}) %all-to-all-start.1) | async-done | bytes 3145760 | tf_op jit(solution)/shard_map/all_to_all | solution.py:73
  223.9 1.6 copy-done.3
  225.6 5.0 %all-to-all-start.3 = ((bf16[2,32,24,1024]{3,2,0,1:T(8,128)(2,1)}), bf16[2,32,24,1024]{3,2,0,1:T(8,128)(2,1)}, u32[]{:S(2)}, u32[]{:S(2)}) async-start(bf16[2,32,24,1024]{3,2,0,1:T(8,128)(2,1)} %pad_maximum_fusion.2), calls=%async_computation.3 | async-start | bytes 6291456 | tf_op jit(solution)/shard_map/all_to_all | solution.py:106
  230.6 2.3 copy.37
  232.9 5.4 %gather_fusion.1 = bf16[1024,1024]{1,0:T(8,128)(2,1)} fusion(bf16[1536,1024]{1,0:T(8,128)(2,1)S(1)} %bitcast.101, s32[1024]{0:T(1024)S(1)} %broadcast_clamp_fusion), kind=kCustom, calls=%fused_computation.1 | custom fusion | bytes 4198400 | tf_op jit(solution)/shard_map/gather | solution.py:14
  238.3 32.1 %all-to-all-done.3 = bf16[2,32,24,1024]{3,2,0,1:T(8,128)(2,1)} async-done(((bf16[2,32,24,1024]{3,2,0,1:T(8,128)(2,1)}), bf16[2,32,24,1024]{3,2,0,1:T(8,128)(2,1)}, u32[]{:S(2)}, u32[]{:S(2)}) %all-to-all-start.3) | async-done | bytes 3145760 | tf_op jit(solution)/shard_map/all_to_all | solution.py:106
  270.4 2.3 copy.44
  272.7 5.4 %gather_fusion.4 = bf16[1024,1024]{1,0:T(8,128)(2,1)} fusion(bf16[1536,1024]{1,0:T(8,128)(2,1)S(1)} %bitcast.100, s32[1024]{0:T(1024)S(1)} %broadcast_clamp_fusion), kind=kCustom, calls=%fused_computation.4 | custom fusion | bytes 4198400 | tf_op jit(solution)/shard_map/gather | solution.py:14
  278.1 3.9 %bitcast_reduce_fusion = bf16[128,1024]{1,0:T(8,128)(2,1)} fusion(bf16[1024,1024]{1,0:T(8,128)(2,1)} %gather_fusion.4), kind=kLoop, calls=%fused_computation.22 | loop fusion | flops 917504 | bytes 2359296 | tf_op jit(solution)/shard_map/reduce_sum | solution.py:114
  281.9 2.1 fusion.2
  284.0 1.4 copy.55
  285.4 0.7 slice_bitcast_fusion.25
  286.1 0.9 copy.48
  (65 shorter events, 3.5 us)
Async XLA Ops:
  7.2 31.2 %copy-start = (bf16[128,1024]{1,0:T(8,128)(2,1)S(1)}, bf16[128,1024]{1,0:T(8,128)(2,1)}, u32[]{:S(2)}) copy-start(bf16[128,1024]{1,0:T(8,128)(2,1)} %param.11) | copy-start | bytes 786436
  7.2 20.5 %copy-start.14 = (f32[128,8]{0,1:T(8,128)S(1)}, f32[128,8]{0,1:T(8,128)}, u32[]{:S(2)}) copy-start(f32[128,8]{0,1:T(8,128)} %param.8) | copy-start | bytes 12292
  7.2 134.2 %all-gather.3.cloned.1.call-start = ((), (), s32[]{:S(2)}) async-start(), calls=%async_computation.5 | async-start | bytes 3538944 | tf_op jit(solution)/shard_map/all_gather | solution.py:54
  45.7 8.7 %copy-start.2 = (bf16[128,1024]{1,0:T(8,128)(2,1)S(1)}, bf16[128,1024]{1,0:T(8,128)(2,1)}, u32[]{:S(2)}) copy-start(bf16[128,1024]{1,0:T(8,128)(2,1)} %param.6) | copy-start | bytes 786436
  45.7 48.5 %all-to-all-start.2 = ((bf16[2,32,24,1024]{3,2,0,1:T(8,128)(2,1)}), bf16[2,32,24,1024]{3,2,0,1:T(8,128)(2,1)S(1)}, u32[]{:S(2)}, u32[]{:S(2)}) async-start(bf16[2,32,24,1024]{3,2,0,1:T(8,128)(2,1)} %fusion.1), calls=%async_computation.2 | async-start | bytes 6291456 | tf_op jit(solution)/shard_map/all_to_all | solution.py:76
  94.2 44.9 %all-to-all-start = ((bf16[2,32,24,1024]{3,2,0,1:T(8,128)(2,1)}), bf16[2,32,24,1024]{3,2,0,1:T(8,128)(2,1)}, u32[]{:S(2)}, u32[]{:S(2)}) async-start(bf16[2,32,24,1024]{3,2,0,1:T(8,128)(2,1)} %copy_select_fusion), calls=%async_computation | async-start | bytes 6291456 | tf_op jit(solution)/shard_map/all_to_all | solution.py:50
  99.2 53.8 %all-gather.5.cloned.1.call-start = ((), (), s32[]{:S(2)}) async-start(), calls=%async_computation.6 | async-start | bytes 1769472 | tf_op jit(solution)/shard_map/all_gather | solution.py:64
  100.0 184.0 %reduce-scatter.4.cloned.1.call-start = ((), (), s32[]{:S(2)}) async-start(), calls=%async_computation.7 | async-start | bytes 5308416
  141.3 1.7 copy-start.6
  143.0 4.8 %copy-start.8 = (bf16[2,1024,768]{2,1,0:T(8,128)(2,1)S(1)}, bf16[2,1024,768]{2,1,0:T(8,128)(2,1)}, u32[]{:S(2)}) copy-start(bf16[2,1024,768]{2,1,0:T(8,128)(2,1)} %all-gather.3.cloned.1.call-done) | copy-start | bytes 9437188
  147.8 5.2 %copy-start.5 = (bf16[2,32,24,1024]{3,2,1,0:T(8,128)(2,1)S(1)}, bf16[2,32,24,1024]{3,2,1,0:T(8,128)(2,1)}, u32[]{:S(2)}) copy-start(bf16[2,32,24,1024]{3,2,1,0:T(8,128)(2,1)} %copy.41) | copy-start | bytes 9437188
  158.3 1.5 copy-start.16
  158.3 1.5 copy-start.10
  158.3 4.7 %copy-start.12 = (bf16[2,768,384]{2,1,0:T(8,128)(2,1)}, bf16[2,768,384]{2,1,0:T(8,128)(2,1)S(1)}, u32[]{:S(2)}) copy-start(bf16[2,768,384]{2,1,0:T(8,128)(2,1)S(1)} %get-tuple-element.17) | copy-start | bytes 3538948
  158.4 3.2 %copy-start.7 = (bf16[2,32,24,1024]{3,2,1,0:T(8,128)(2,1)S(1)}, bf16[2,32,24,1024]{3,2,1,0:T(8,128)(2,1)}, u32[]{:S(2)}) copy-start(bf16[2,32,24,1024]{3,2,1,0:T(8,128)(2,1)} %copy-done.6) | copy-start | bytes 9437188
  173.5 1.4 copy-start.15
  173.5 1.7 copy-start.17
  179.2 44.7 %all-to-all-start.1 = ((bf16[2,32,24,1024]{3,2,0,1:T(8,128)(2,1)}), bf16[2,32,24,1024]{3,2,0,1:T(8,128)(2,1)S(1)}, u32[]{:S(2)}, u32[]{:S(2)}) async-start(bf16[2,32,24,1024]{3,2,0,1:T(8,128)(2,1)} %pad_maximum_fusion.1), calls=%async_computation.1 | async-start | bytes 6291456 | tf_op jit(solution)/shard_map/all_to_all | solution.py:73
  184.2 2.7 copy-start.9
  184.2 3.1 %copy-start.13 = (bf16[2,768,384]{2,1,0:T(8,128)(2,1)S(1)}, bf16[2,768,384]{2,1,0:T(8,128)(2,1)}, u32[]{:S(2)}) copy-start(bf16[2,768,384]{2,1,0:T(8,128)(2,1)} %copy-done.12) | copy-start | bytes 3538948
  187.3 1.3 copy-start.11
  223.9 1.6 copy-start.3
  225.6 44.9 %all-to-all-start.3 = ((bf16[2,32,24,1024]{3,2,0,1:T(8,128)(2,1)}), bf16[2,32,24,1024]{3,2,0,1:T(8,128)(2,1)}, u32[]{:S(2)}, u32[]{:S(2)}) async-start(bf16[2,32,24,1024]{3,2,0,1:T(8,128)(2,1)} %pad_maximum_fusion.2), calls=%async_computation.3 | async-start | bytes 6291456 | tf_op jit(solution)/shard_map/all_to_all | solution.py:106
  278.1 3.9 %copy-start.4 = (bf16[1024,1024]{1,0:T(8,128)(2,1)S(1)}, bf16[1024,1024]{1,0:T(8,128)(2,1)}, u32[]{:S(2)}) copy-start(bf16[1024,1024]{1,0:T(8,128)(2,1)} %gather_fusion.1) | copy-start | bytes 6291460
  278.1 9.0 %copy-start.1 = (bf16[128,1024]{1,0:T(8,128)(2,1)S(1)}, bf16[128,1024]{1,0:T(8,128)(2,1)}, u32[]{:S(2)}) copy-start(bf16[128,1024]{1,0:T(8,128)(2,1)} %param.11) | copy-start | bytes 786436
Sparse Core Ops, SparseCore 0:
  9.8 48.5 all-gather.2
  101.8 42.6 all-gather.4
  173.7 60.4 reduce-scatter.3
where the time goes:
time: 294 us
  waiting for transfers between devices  132 us (45%)
  local copies, waits for them, and re-layouts  59.7 us (20%)
  other arithmetic  36 us (12%)
  matrix products  27.4 us (9%)
  starting transfers between devices  24 us (8%)
  between operations  14.2 us (5%)
    all_to_all x1, waiting for transfers between devices, shards(): lax.all_to_all(send_rows, 'expert', split_axis=1, concat_axis=1, tiled=True)  36.7 us
    all_to_all x1, waiting for transfers between devices, shards(): lax.all_to_all(input_grads.reshape(buffer_shape), 'expert', split_axis=1,...  32.1 us
    all_to_all x1, waiting for transfers between devices, shards(): lax.all_to_all(result.reshape(buffer_shape), 'expert', split_axis=1, conc...  31.4 us
    all_to_all x1, waiting for transfers between devices, shards(): lax.all_to_all(send_back, 'expert', split_axis=1, concat_axis=1, tiled=True)  30.7 us
    another operation x3, other arithmetic  18.2 us
    unnamed x41, local copies, waits for them, and re-layouts  17.2 us
    gather x2, local copies, waits for them, and re-layouts, collect(): return flat_back[target].reshape(tok_rows, top_count, returned.shape[-1])  10.7 us
    all_to_all x1, starting transfers between devices, shards(): lax.all_to_all(send_back, 'expert', split_axis=1, concat_axis=1, tiled=True)  8.71 us
  transfers between devices with their start and end apart: 7, of which 4 were waited for; matrix products, arithmetic and copies ran while one was open for 32% of the time, Pallas kernels for 0%

commit v1 on v0

v1 whole, which is shorter than its diff:
```python
import functools
import jax
import jax.numpy as jnp
from jax import lax
from jax.experimental import pallas as pl
from jax.experimental.pallas import tpu as pltpu
from jax.sharding import PartitionSpec as P

BF = jnp.bfloat16
F32 = jnp.float32
CAP = 24
VMEM_LIMIT = 56 << 20


def call(kernel, name, out_shape, grid=None, in_specs=None, out_specs=None, scratch=(), flops=0, nbytes=0):
    full = pl.BlockSpec(memory_space=pltpu.VMEM)
    kwargs = {} if grid is None else {"grid": grid}
    return pl.pallas_call(
        kernel,
        name=name,
        out_shape=out_shape,
        in_specs=in_specs,
        out_specs=full if out_specs is None else out_specs,
        scratch_shapes=scratch,
        compiler_params=pltpu.CompilerParams(vmem_limit_bytes=VMEM_LIMIT),
        cost_estimate=pl.CostEstimate(flops=flops, transcendentals=0, bytes_accessed=nbytes),
        **kwargs,
    )


def membership(ids, weights, experts):
    rows, top = ids.shape
    lane = lax.broadcasted_iota(jnp.int32, (rows, experts), 1)
    named = jnp.zeros((rows, experts), F32)
    gates = jnp.zeros((rows, experts), F32)
    for k in range(top):
        hit = ids[:, k : k + 1] == lane
        named = jnp.where(hit, 1.0, named)
        if weights is not None:
            gates = jnp.where(hit, weights[:, k : k + 1], gates)
    before = (
        lax.broadcasted_iota(jnp.int32, (rows, rows), 1)
        < lax.broadcasted_iota(jnp.int32, (rows, rows), 0)
    ).astype(F32).astype(BF)
    rank = jnp.dot(before, named.astype(BF), preferred_element_type=F32)
    return jnp.where(named > 0.0, rank, -1.0), gates


def slot_matrix(rank):
    rows, experts = rank.shape
    turned = rank.T
    slot = lax.broadcasted_iota(jnp.int32, (experts, CAP, rows), 1).astype(F32)
    return turned[:, None, :] == slot


def pack_rows_kernel(ids_ref, tokens_ref, out_ref):
    experts = out_ref.shape[0]
    rank, _ = membership(ids_ref[...], None, experts)
    chosen = slot_matrix(rank)
    pick = jnp.where(chosen, 1.0, 0.0).reshape(experts * CAP, -1).astype(BF)
    rows = jnp.dot(pick, tokens_ref[...], preferred_element_type=F32)
    out_ref[...] = rows.reshape(out_ref.shape).astype(BF)


def pack_back_kernel(ids_ref, weights_ref, cot_ref, out_ref):
    experts = out_ref.shape[0]
    rank, gates = membership(ids_ref[...], weights_ref[...], experts)
    chosen = slot_matrix(rank)
    pick = jnp.where(chosen, 1.0, 0.0).reshape(experts * CAP, -1).astype(BF)
    scale = jnp.sum(jnp.where(chosen, gates.T[:, None, :], 0.0), axis=2, keepdims=True)
    rows = jnp.dot(pick, cot_ref[...], preferred_element_type=F32)
    out_ref[...] = (rows.reshape(out_ref.shape) * scale).astype(BF)


def expand(values, experts):
    wide = experts * CAP
    col = lax.broadcasted_iota(jnp.int32, (experts, wide), 1)
    row = lax.broadcasted_iota(jnp.int32, (experts, wide), 0) * CAP
    spread = jnp.where((col >= row) & (col < row + CAP), 1.0, 0.0).astype(BF)
    return jnp.dot(values, spread, preferred_element_type=F32)


def slot_hits(rank, experts):
    wide = experts * CAP
    slot = lax.rem(lax.broadcasted_iota(jnp.int32, (rank.shape[0], wide), 1), CAP).astype(F32)
    return expand(rank.astype(BF), experts) == slot


def combine_out_kernel(ids_ref, weights_ref, back_ref, out_ref):
    experts = back_ref.shape[0] // CAP
    rank, gates = membership(ids_ref[...], weights_ref[...], experts)
    hits = slot_hits(rank, experts)
    back = back_ref[...]
    total = None
    rest = gates
    for _ in range(3):
        part = rest.astype(BF)
        rest = rest - part.astype(F32)
        term = jnp.dot(
            jnp.where(hits, expand(part, experts), 0.0).astype(BF), back, preferred_element_type=F32
        )
        total = term if total is None else total + term
    out_ref[...] = total.astype(BF)


def combine_grad_kernel(ids_ref, back_ref, out_ref):
    experts = back_ref.shape[0] // CAP
    rank, _ = membership(ids_ref[...], None, experts)
    pick = jnp.where(slot_hits(rank, experts), 1.0, 0.0).astype(BF)
    out_ref[...] = jnp.dot(pick, back_ref[...], preferred_element_type=F32).astype(BF)


def load_rows(ref):
    block = ref[:, 0].astype(F32)
    return block.reshape(-1, block.shape[-1]).astype(BF)


def load_lift(weights_ref, expert):
    return jnp.concatenate(
        [weights_ref[j, pl.ds(pl.multiple_of(expert * 128, 128), 128), :] for j in range(8)], axis=0
    )


def load_down(weights_ref, expert):
    base = weights_ref.shape[1] - 128
    return jnp.concatenate(
        [
            jnp.concatenate(
                [
                    weights_ref[j, base:, pl.ds(pl.multiple_of(expert * 384 + kb * 128, 128), 128)]
                    for j in range(8)
                ],
                axis=1,
            )
            for kb in range(3)
        ],
        axis=0,
    )


def forward_kernel(rows_ref, weights_ref, out_ref, act_ref, swish_ref, slope_ref):
    expert = pl.program_id(0)
    rows = load_rows(rows_ref)
    hidden = jnp.dot(rows, load_lift(weights_ref, expert), preferred_element_type=F32)
    ff = hidden.shape[1] // 2
    gate, up = hidden[:, :ff], hidden[:, ff:]
    sig = jax.nn.sigmoid(gate)
    swish = gate * sig
    act = (swish * up).astype(BF)
    act_ref[0] = act
    swish_ref[0] = swish
    slope_ref[0] = up * (sig * (1.0 + gate * (1.0 - sig)))
    out = jnp.dot(act, load_down(weights_ref, expert), preferred_element_type=F32)
    out_ref[:, 0] = out.reshape(out_ref.shape[0], CAP, -1).astype(BF)


def weight_grad_kernel(rows_ref, back_ref, act_ref, swish_ref, slope_ref, weights_ref, hid_ref, grad_ref):
    expert = pl.program_id(0)
    back = load_rows(back_ref)
    act_grad = lax.dot_general(
        back, load_down(weights_ref, expert), (((1,), (1,)), ((), ())), preferred_element_type=F32
    )
    hid = jnp.concatenate(
        [(act_grad * slope_ref[0]).astype(BF), (act_grad * swish_ref[0]).astype(BF)], axis=1
    )
    hid_ref[0] = hid
    first = (((0,), (0,)), ((), ()))
    down = lax.dot_general(act_ref[0], back, first, preferred_element_type=F32).astype(BF)
    lift = lax.dot_general(load_rows(rows_ref), hid, first, preferred_element_type=F32).astype(BF)
    base = weights_ref.shape[1] - 128
    for j in range(8):
        grad_ref[j, pl.ds(pl.multiple_of(expert * 128, 128), 128), :] = lift[j * 128 : (j + 1) * 128]
        for kb in range(3):
            grad_ref[j, base:, pl.ds(pl.multiple_of(expert * 384 + kb * 128, 128), 128)] = down[
                kb * 128 : (kb + 1) * 128, j * 128 : (j + 1) * 128
            ]


def input_grad_kernel(hid_ref, weights_ref, out_ref):
    expert = pl.program_id(0)
    grad = lax.dot_general(
        hid_ref[0], load_lift(weights_ref, expert), (((1,), (1,)), ((), ())), preferred_element_type=F32
    )
    out_ref[:, 0] = grad.reshape(out_ref.shape[0], CAP, -1).astype(BF)


def shards(tokens, expert_ids, combine_weights, lift_weights, down_weights, cotangent):
    tok, top = expert_ids.shape
    local, slice_rows, lift_width = lift_weights.shape
    ff = down_weights.shape[1]
    width = tokens.shape[1]
    owners = lax.axis_size("expert")
    groups = lax.axis_size("dp")
    experts = local * owners
    slots = owners * CAP
    bundle = local * slice_rows + 128
    vm = pl.BlockSpec(memory_space=pltpu.VMEM)

    joined = jnp.concatenate(
        [
            lift_weights.reshape(local * slice_rows, lift_width),
            down_weights.reshape(local, ff // 128, 128, 128).transpose(2, 0, 1, 3).reshape(128, lift_width),
        ],
        axis=0,
    )
    weights = lax.all_gather(joined, "dp")

    sent = jax.ShapeDtypeStruct((experts, CAP, width), BF)
    pack_flops = 2 * experts * CAP * tok * width
    send_rows = call(pack_rows_kernel, "pack_rows", sent, in_specs=[vm] * 2, flops=pack_flops, nbytes=8 << 20)(
        expert_ids, tokens
    )
    send_back = call(pack_back_kernel, "pack_back", sent, in_specs=[vm] * 3, flops=pack_flops, nbytes=8 << 20)(
        expert_ids, combine_weights, cotangent
    )
    buffer_shape = (owners, local, CAP, width)

    def exchange(x):
        return lax.all_to_all(x.reshape(buffer_shape), "expert", 0, 0, tiled=True)

    recv_rows = exchange(send_rows)
    recv_back = exchange(send_back)

    row_block = pl.BlockSpec((owners, 1, CAP, width), lambda e: (0, e, 0, 0))
    weight_block = pl.BlockSpec((groups, bundle, lift_width), lambda e: (0, 0, 0))
    half_block = pl.BlockSpec((1, slots, ff), lambda e: (e, 0, 0))
    hid_block = pl.BlockSpec((1, slots, 2 * ff), lambda e: (e, 0, 0))
    back_shape = jax.ShapeDtypeStruct(buffer_shape, BF)
    unit = 2 * local * slots * ff * width
    result, act, swish, slope = call(
        forward_kernel,
        "forward",
        [
            back_shape,
            jax.ShapeDtypeStruct((local, slots, ff), BF),
            jax.ShapeDtypeStruct((local, slots, ff), F32),
            jax.ShapeDtypeStruct((local, slots, ff), F32),
        ],
        grid=(local,),
        in_specs=[row_block, weight_block],
        out_specs=[row_block, half_block, half_block, half_block],
        flops=3 * unit,
        nbytes=16 << 20,
    )(recv_rows, weights)
    returned = exchange(result)
    recv_back, _ = lax.optimization_barrier((recv_back, result))
    hid, weight_grads = call(
        weight_grad_kernel,
        "weight_grad",
        [
            jax.ShapeDtypeStruct((local, slots, 2 * ff), BF),
            jax.ShapeDtypeStruct((groups, bundle, lift_width), BF),
        ],
        grid=(local,),
        in_specs=[row_block, row_block, half_block, half_block, half_block, weight_block],
        out_specs=[hid_block, weight_block],
        flops=4 * unit,
        nbytes=20 << 20,
    )(recv_rows, recv_back, act, swish, slope, weights)
    summed = lax.psum_scatter(weight_grads, "dp", scatter_dimension=0, tiled=False)
    input_grads = call(
        input_grad_kernel,
        "input_grad",
        back_shape,
        grid=(local,),
        in_specs=[hid_block, weight_block],
        out_specs=row_block,
        flops=2 * unit,
        nbytes=12 << 20,
    )(hid, weights)
    input_grads, returned = lax.optimization_barrier((input_grads, returned))
    returned_grads = exchange(input_grads)

    token_shape = jax.ShapeDtypeStruct((tok, width), BF)
    layer_output = call(
        combine_out_kernel, "combine_out", token_shape, in_specs=[vm] * 3, flops=3 * pack_flops, nbytes=4 << 20
    )(expert_ids, combine_weights, returned.reshape(experts * CAP, width))
    token_grads = call(
        combine_grad_kernel, "combine_grad", token_shape, in_specs=[vm] * 2, flops=pack_flops, nbytes=4 << 20
    )(expert_ids, returned_grads.reshape(experts * CAP, width))

    lift_grads = summed[: local * slice_rows].reshape(local, slice_rows, lift_width)
    down_grads = (
        summed[local * slice_rows :].reshape(128, local, ff // 128, 128).transpose(1, 2, 0, 3).reshape(local, ff, 128)
    )
    return (layer_output, token_grads, lift_grads, down_grads)


def solution(mesh):
    rows = P(("expert", "dp"), None)
    lift, down = P("expert", "dp", None), P("expert", None, "dp")
    return jax.shard_map(
        shards,
        mesh=mesh,
        in_specs=(rows, rows, rows, lift, down, rows),
        out_specs=(rows, rows, lift, down),
        check_vma=False,
    )
```

time: 294 us -> 231 us (0.79)
  local copies, waits for them, and re-layouts: 59.7 us -> 12.1 us
  Pallas kernels: 0 us -> 46.9 us
  other arithmetic: 36 us -> 1.84 us
  matrix products: 27.4 us -> 0 us
    pallas_call x0 -> x7, Pallas kernels: none -> 46.9 us  [the longest x1 12.2 us: shards(): call(weight_grad_kernel, 'weight_grad', [jax.ShapeDtypeStruct((local, slo...]
    gather x5 -> x0, local copies, waits for them, and re-layouts: 27.5 us -> none  [the longest x2 10.7 us: collect(): return flat_back[target].reshape(tok_rows, top_count, returned.shape[-1])]
    dot_general x12 -> x0, matrix products: 27.4 us -> none  [the longest x1 5.31 us: shards(): jnp.einsum('ern,efn->erf', part_back, lax.all_gather(down_weights, 'dp',...]
    another operation x5 -> x0, other arithmetic: 22.1 us -> none
    unnamed x41 -> x10, local copies, waits for them, and re-layouts: 17.2 us -> 7.12 us
    all_to_all x4 -> x0, local copies, waits for them, and re-layouts: 8.95 us -> none  [the longest x1 2.28 us: shards(): lax.all_to_all(result.reshape(buffer_shape), 'expert', split_axis=1, conc...]
    reduce_sum x3 -> x0, other arithmetic: 6 us -> none  [the longest x1 3.88 us: shards(): jnp.sum(grads_picked.astype(jnp.float32), axis=1).astype(jnp.bfloat16)]
    scatter x1 -> x0, local copies, waits for them, and re-layouts: 4.32 us -> none  [shards(): source_of = jnp.full((all_experts * capacity,), -1, jnp.int32).at[target]...]
  transfers between devices with their start and end apart: 7 -> 6, of which waited for: 4 -> 5; matrix products, arithmetic and copies ran while one was open for 32% -> 1% of each run, Pallas kernels for 0% -> 15%
where the time goes in v1:
time: 231 us; the launch traced here: 230 us
  waiting for transfers between devices  131 us (57%)
  Pallas kernels  46.9 us (20%)
  starting transfers between devices  23.8 us (10%)
  between operations  14.1 us (6%)
  local copies, waits for them, and re-layouts  12.1 us (5%)
    all_to_all x4, waiting for transfers between devices, exchange(): return lax.all_to_all(x.reshape(buffer_shape), 'expert', 0, 0, tiled=True)  129 us
    all_to_all x4, starting transfers between devices, exchange(): return lax.all_to_all(x.reshape(buffer_shape), 'expert', 0, 0, tiled=True)  23.7 us
    pallas_call x1, Pallas kernels, shards(): call(weight_grad_kernel, 'weight_grad', [jax.ShapeDtypeStruct((local, slo...  12.2 us
    pallas_call x1, Pallas kernels, shards(): call(forward_kernel, 'forward', [back_shape, jax.ShapeDtypeStruct((local,...  11 us
    unnamed x10, local copies, waits for them, and re-layouts  7.12 us
    pallas_call x1, Pallas kernels, shards(): call(input_grad_kernel, 'input_grad', back_shape, grid=(local,), in_specs...  6.75 us
    pallas_call x1, Pallas kernels, shards(): call(combine_out_kernel, 'combine_out', token_shape, in_specs=[vm] * 3, f...  4.99 us
  transfers between devices with their start and end apart: 6, of which 5 were waited for; matrix products, arithmetic and copies ran while one was open for 1% of the time, Pallas kernels for 15%

profile of v1, /device:TPU:1, one launch (start us, length us, event | category | flops | bytes accessed | tf_op | source)
XLA Modules:
  0.0 230.2 jit_solution(7997278993396883264)
XLA Ops:
  7.2 0.0 all-gather.3.cloned.1.call-start
  7.2 1.1 copy.29
  8.3 0.2 copy.30
  8.5 1.8 pad_maximum_fusion
  10.3 0.0 all-gather.3.cloned.1.call-update
  10.3 1.4 copy.31.ids_ref
  11.7 4.2 %pack_rows.1 = bf16[64,24,1024]{2,1,0:T(8,128)(2,1)} custom-call(s32[128,8]{1,0:T(8,128)} %copy.31.ids_ref, bf16[128,1024]{1,0:T(8,128)(2,1)} %tokens_ref.1), custom_call_target="tpu_custom_call" | custom-call | flops 402653184 | bytes 8388608 | tf_op jit(solution)/shard_map/pack_rows/pallas_call | solution.py:210
  15.9 0.0 copy-start.3
  15.9 8.7 %all-to-all-start = ((bf16[32,2,24,1024]{3,2,1,0:T(8,128)(2,1)}), bf16[32,2,24,1024]{3,2,1,0:T(8,128)(2,1)S(1)}, u32[]{:S(2)}, u32[]{:S(2)}) async-start(bf16[32,2,24,1024]{3,2,1,0:T(8,128)(2,1)} %bitcast.17), calls=%async_computation | async-start | bytes 6291456 | tf_op jit(solution)/shard_map/all_to_all | solution.py:219
  24.6 0.0 copy-done.3
  24.6 0.7 copy.32.weights_ref
  25.4 4.2 %pack_back.1 = bf16[64,24,1024]{2,1,0:T(8,128)(2,1)} custom-call(s32[128,8]{1,0:T(8,128)} %copy.31.ids_ref, f32[128,8]{1,0:T(8,128)} %copy.32.weights_ref, bf16[128,1024]{1,0:T(8,128)(2,1)} %cot_ref.1), custom_call_target="tpu_custom_call" | custom-call | flops 402653184 | bytes 8388608 | tf_op jit(solution)/shard_map/pack_back/pallas_call | solution.py:213
  29.5 34.9 %all-to-all-done.rows_ref = bf16[32,2,24,1024]{3,2,1,0:T(8,128)(2,1)S(1)} async-done(((bf16[32,2,24,1024]{3,2,1,0:T(8,128)(2,1)}), bf16[32,2,24,1024]{3,2,1,0:T(8,128)(2,1)S(1)}, u32[]{:S(2)}, u32[]{:S(2)}) %all-to-all-start) | async-done | bytes 3145760 | tf_op jit(solution)/shard_map/all_to_all | solution.py:219
  64.4 0.0 copy-start.1
  64.4 1.7 copy-done.1
  66.0 5.0 %all-to-all-start.1 = ((bf16[32,2,24,1024]{3,2,1,0:T(8,128)(2,1)}), bf16[32,2,24,1024]{3,2,1,0:T(8,128)(2,1)}, u32[]{:S(2)}, u32[]{:S(2)}) async-start(bf16[32,2,24,1024]{3,2,1,0:T(8,128)(2,1)} %bitcast.15), calls=%async_computation.1 | async-start | bytes 6291456 | tf_op jit(solution)/shard_map/all_to_all | solution.py:219
  71.1 0.0 reduce-scatter.2.cloned.1.call-start
  71.1 2.9 %all-gather.3.cloned.1.call-done = bf16[3072,768]{1,0:T(8,128)(2,1)} async-done(((bf16[384,768]{1,0:T(8,128)(2,1)}), bf16[3072,768]{1,0:T(8,128)(2,1)}) %all-gather.3.cloned.1.call-update) | async-done | bytes 4718608 | tf_op jit(solution)/shard_map/all_gather | solution.py:206
  74.0 11.0 %forward.1 = (bf16[32,2,24,1024]{3,2,1,0:T(8,128)(2,1)}, bf16[2,768,384]{2,1,0:T(8,128)(2,1)}, f32[2,768,384]{2,1,0:T(8,128)}, f32[2,768,384]{2,1,0:T(8,128)}) custom-call(bf16[32,2,24,1024]{3,2,1,0:T(8,128)(2,1)} %copy-done.1, bf16[8,384,768]{2,1,0:T(8,128)(2,1)} %bitcast.18), custom_call_target="tpu_custom_call" | custom-call | flops 3623878656 | bytes 16777216 | tf_op jit(solution)/shard_map/forward/pallas_call | solution.py:230
  85.0 25.9 %all-to-all-done.1.back_ref = bf16[32,2,24,1024]{3,2,1,0:T(8,128)(2,1)} async-done(((bf16[32,2,24,1024]{3,2,1,0:T(8,128)(2,1)}), bf16[32,2,24,1024]{3,2,1,0:T(8,128)(2,1)}, u32[]{:S(2)}, u32[]{:S(2)}) %all-to-all-start.1) | async-done | bytes 3145760 | tf_op jit(solution)/shard_map/all_to_all | solution.py:219
  110.9 12.2 %weight_grad.1 = (bf16[2,768,768]{2,1,0:T(8,128)(2,1)}, bf16[8,384,768]{2,1,0:T(8,128)(2,1)}) custom-call(bf16[32,2,24,1024]{3,2,1,0:T(8,128)(2,1)} %copy-done.1, bf16[32,2,24,1024]{3,2,1,0:T(8,128)(2,1)} %all-to-all-done.1.back_ref, bf16[2,768,384]{2,1,0:T(8,128)(2,1)} %get-tuple-element.15.act_ref, f32[2,768,384]{2,1,0:T(8,128)} %get-tuple-element.16.swish_ref, ...), custom_call_target="tpu_custom_call" | custom-call | flops 4831838208 | bytes 20971520 | tf_op jit(solution)/shard_map/weight_grad/pallas_call | solution.py:247
  123.1 0.0 reduce-scatter.2.cloned.1.call-update
  123.2 5.0 %all-to-all-start.2 = ((bf16[32,2,24,1024]{3,2,1,0:T(8,128)(2,1)}), bf16[32,2,24,1024]{3,2,1,0:T(8,128)(2,1)S(1)}, u32[]{:S(2)}, u32[]{:S(2)}) async-start(bf16[32,2,24,1024]{3,2,1,0:T(8,128)(2,1)} %get-tuple-element.13), calls=%async_computation.2 | async-start | bytes 6291456 | tf_op jit(solution)/shard_map/all_to_all | solution.py:219
  128.2 6.7 %input_grad.1 = bf16[32,2,24,1024]{3,2,1,0:T(8,128)(2,1)} custom-call(bf16[2,768,768]{2,1,0:T(8,128)(2,1)} %get-tuple-element.18.hid_ref, bf16[8,384,768]{2,1,0:T(8,128)(2,1)} %bitcast.20), custom_call_target="tpu_custom_call" | custom-call | flops 2415919104 | bytes 12582912 | tf_op jit(solution)/shard_map/input_grad/pallas_call | solution.py:261
  134.9 33.0 %all-to-all-done.2 = bf16[32,2,24,1024]{3,2,1,0:T(8,128)(2,1)S(1)} async-done(((bf16[32,2,24,1024]{3,2,1,0:T(8,128)(2,1)}), bf16[32,2,24,1024]{3,2,1,0:T(8,128)(2,1)S(1)}, u32[]{:S(2)}, u32[]{:S(2)}) %all-to-all-start.2) | async-done | bytes 3145760 | tf_op jit(solution)/shard_map/all_to_all | solution.py:219
  167.9 0.0 copy-start.2
  167.9 1.7 copy-done.2
  169.6 5.0 %all-to-all-start.3 = ((bf16[32,2,24,1024]{3,2,1,0:T(8,128)(2,1)}), bf16[32,2,24,1024]{3,2,1,0:T(8,128)(2,1)S(1)}, u32[]{:S(2)}, u32[]{:S(2)}) async-start(bf16[32,2,24,1024]{3,2,1,0:T(8,128)(2,1)} %input_grad.1), calls=%async_computation.3 | async-start | bytes 6291456 | tf_op jit(solution)/shard_map/all_to_all | solution.py:219
  174.6 5.0 %combine_out.1 = bf16[128,1024]{1,0:T(8,128)(2,1)} custom-call(s32[128,8]{1,0:T(8,128)} %copy.31.ids_ref, f32[128,8]{1,0:T(8,128)} %copy.32.weights_ref, bf16[1536,1024]{1,0:T(8,128)(2,1)} %bitcast.21), custom_call_target="tpu_custom_call" | custom-call | flops 1207959552 | bytes 4194304 | tf_op jit(solution)/shard_map/combine_out/pallas_call | solution.py:275
  179.6 34.8 %all-to-all-done.3 = bf16[32,2,24,1024]{3,2,1,0:T(8,128)(2,1)S(1)} async-done(((bf16[32,2,24,1024]{3,2,1,0:T(8,128)(2,1)}), bf16[32,2,24,1024]{3,2,1,0:T(8,128)(2,1)S(1)}, u32[]{:S(2)}, u32[]{:S(2)}) %all-to-all-start.3) | async-done | bytes 3145760 | tf_op jit(solution)/shard_map/all_to_all | solution.py:219
  214.3 0.0 copy-start
  214.3 1.6 copy-done
  216.0 3.7 %combine_grad.1 = bf16[128,1024]{1,0:T(8,128)(2,1)} custom-call(s32[128,8]{1,0:T(8,128)} %copy.31.ids_ref, bf16[1536,1024]{1,0:T(8,128)(2,1)} %bitcast.16), custom_call_target="tpu_custom_call" | custom-call | flops 402653184 | bytes 4194304 | tf_op jit(solution)/shard_map/combine_grad/pallas_call | solution.py:278
  219.7 0.0 reduce-scatter.2.cloned.1.call-done
  219.7 0.9 slice.11
  220.6 0.2 copy.34
  220.8 0.8 copy.35
  221.6 1.8 slice.10
Async XLA Ops:
  7.2 66.9 %all-gather.3.cloned.1.call-start = ((), (), s32[]{:S(2)}) async-start(), calls=%async_computation.6 | async-start | bytes 5308416 | tf_op jit(solution)/shard_map/all_gather | solution.py:206
  15.9 8.7 %copy-start.3 = (f32[128,8]{0,1:T(8,128)S(1)}, f32[128,8]{0,1:T(8,128)}, u32[]{:S(2)}) copy-start(f32[128,8]{0,1:T(8,128)} %param.8) | copy-start | bytes 12292
  15.9 48.5 %all-to-all-start = ((bf16[32,2,24,1024]{3,2,1,0:T(8,128)(2,1)}), bf16[32,2,24,1024]{3,2,1,0:T(8,128)(2,1)S(1)}, u32[]{:S(2)}, u32[]{:S(2)}) async-start(bf16[32,2,24,1024]{3,2,1,0:T(8,128)(2,1)} %bitcast.17), calls=%async_computation | async-start | bytes 6291456 | tf_op jit(solution)/shard_map/all_to_all | solution.py:219
  64.4 1.7 copy-start.1
  66.0 44.9 %all-to-all-start.1 = ((bf16[32,2,24,1024]{3,2,1,0:T(8,128)(2,1)}), bf16[32,2,24,1024]{3,2,1,0:T(8,128)(2,1)}, u32[]{:S(2)}, u32[]{:S(2)}) async-start(bf16[32,2,24,1024]{3,2,1,0:T(8,128)(2,1)} %bitcast.15), calls=%async_computation.1 | async-start | bytes 6291456 | tf_op jit(solution)/shard_map/all_to_all | solution.py:219
  71.1 148.6 %reduce-scatter.2.cloned.1.call-start = ((), (), s32[]{:S(2)}) async-start(), calls=%async_computation.5 | async-start | bytes 5308416 | tf_op jit(solution)/shard_map/reduce_scatter | solution.py:260
  123.2 44.8 %all-to-all-start.2 = ((bf16[32,2,24,1024]{3,2,1,0:T(8,128)(2,1)}), bf16[32,2,24,1024]{3,2,1,0:T(8,128)(2,1)S(1)}, u32[]{:S(2)}, u32[]{:S(2)}) async-start(bf16[32,2,24,1024]{3,2,1,0:T(8,128)(2,1)} %get-tuple-element.13), calls=%async_computation.2 | async-start | bytes 6291456 | tf_op jit(solution)/shard_map/all_to_all | solution.py:219
  167.9 1.7 copy-start.2
  169.6 44.8 %all-to-all-start.3 = ((bf16[32,2,24,1024]{3,2,1,0:T(8,128)(2,1)}), bf16[32,2,24,1024]{3,2,1,0:T(8,128)(2,1)S(1)}, u32[]{:S(2)}, u32[]{:S(2)}) async-start(bf16[32,2,24,1024]{3,2,1,0:T(8,128)(2,1)} %input_grad.1), calls=%async_computation.3 | async-start | bytes 6291456 | tf_op jit(solution)/shard_map/all_to_all | solution.py:219
  214.3 1.7 copy-start
Sparse Core Ops, SparseCore 0:
  10.4 63.5 all-gather.2
  123.3 60.4 reduce-scatter.1

commit v2 on v1

v2 whole, which is shorter than its diff:
```python
import functools
import jax
import jax.numpy as jnp
from jax import lax
from jax.experimental import pallas as pl
from jax.experimental.pallas import tpu as pltpu
from jax.sharding import PartitionSpec as P

BF = jnp.bfloat16
F32 = jnp.float32
CAP = 24
SIDE = 4
CORES = 2
VMEM_LIMIT = 56 << 20


def call(kernel, name, out_shape, grid=None, in_specs=None, out_specs=None, scratch=(), flops=0, nbytes=0):
    full = pl.BlockSpec(memory_space=pltpu.VMEM)
    kwargs = {} if grid is None else {"grid": grid}
    return pl.pallas_call(
        kernel,
        name=name,
        out_shape=out_shape,
        in_specs=in_specs,
        out_specs=full if out_specs is None else out_specs,
        scratch_shapes=scratch,
        compiler_params=pltpu.CompilerParams(vmem_limit_bytes=VMEM_LIMIT),
        cost_estimate=pl.CostEstimate(flops=flops, transcendentals=0, bytes_accessed=nbytes),
        **kwargs,
    )


def split_parts(values, count):
    parts, rest = [], values
    for _ in range(count):
        part = rest.astype(BF).astype(F32)
        rest = rest - part
        parts.append(part)
    return parts


def bundle_kernel(ids_ref, weights_ref, tokens_ref, cot_ref, out_ref):
    tok, width = tokens_ref.shape
    out_ref[:tok] = tokens_ref[...]
    out_ref[tok : 2 * tok] = cot_ref[...]
    facts = [ids_ref[...].astype(F32)] + split_parts(weights_ref[...], 3)
    facts = jnp.concatenate(facts + [jnp.zeros((facts[0].shape[0], width - 4 * tok), F32)], axis=1)
    out_ref[2 * tok :] = jnp.concatenate([facts, jnp.zeros_like(facts)], axis=0).astype(BF)


def unbundle(ref, tok):
    facts = ref[ref.shape[0] - 16 :, : 4 * tok].astype(F32)[:8]
    pieces = [facts[:, n * tok : (n + 1) * tok] for n in range(4)]
    return pieces[0], (pieces[1] + pieces[2]) + pieces[3]


def membership(ids, weights, experts):
    top, rows = ids.shape
    expert = lax.broadcasted_iota(jnp.int32, (experts, rows), 0).astype(F32)
    named = jnp.zeros((experts, rows), F32)
    gates = jnp.zeros((experts, rows), F32)
    for k in range(top):
        hit = ids[k : k + 1, :] == expert
        named = jnp.where(hit, 1.0, named)
        if weights is not None:
            gates = jnp.where(hit, weights[k : k + 1, :], gates)
    before = (
        lax.broadcasted_iota(jnp.int32, (rows, rows), 0)
        < lax.broadcasted_iota(jnp.int32, (rows, rows), 1)
    ).astype(F32).astype(BF)
    rank = jnp.dot(named.astype(BF), before, preferred_element_type=F32)
    return jnp.where(named > 0.0, rank, -1.0), gates


def pack_kernel(first_ref, *refs):
    bundles, outs, (rank_ref, gate_ref) = refs[:4], refs[4:-2], refs[-2:]
    which = pl.program_id(0)
    tok = (bundles[0].shape[0] - 16) // 2
    found = []
    for q, bundle in enumerate(bundles):
        ids, weights = unbundle(bundle, tok)
        rank_ref[q], gate_ref[q] = membership(ids, weights, rank_ref.shape[1])
        rank = jnp.concatenate([rank_ref[q, pl.ds(first_ref[p], 2), :] for p in range(len(outs))], axis=0)
        gates = jnp.concatenate([gate_ref[q, pl.ds(first_ref[p], 2), :] for p in range(len(outs))], axis=0)
        slot = lax.broadcasted_iota(jnp.int32, (rank.shape[0], CAP, tok), 1).astype(F32)
        chosen = rank[:, None, :] == slot
        pick = jnp.where(chosen, 1.0, 0.0).reshape(-1, tok).astype(BF)
        scale = jnp.sum(jnp.where(chosen, gates[:, None, :], 0.0), axis=2, keepdims=True)
        scale = jnp.where(which == 0, 1.0, scale)
        data = bundle[pl.ds(pl.multiple_of(which * tok, tok), tok), :]
        rows = jnp.dot(pick, data, preferred_element_type=F32)
        found.append(rows.reshape(rank.shape[0], CAP, -1) * scale)
    for p, out in enumerate(outs):
        for e in range(2):
            out[0, e] = jnp.concatenate([rows[2 * p + e] for rows in found], axis=0).astype(BF)


def combine(first_ref, facts, chunks, rank_ref, gate_ref, weighted):
    tok = rank_ref.shape[2]
    sums = []
    for q, fact in enumerate(facts):
        ids, weights = unbundle(fact, tok)
        rank_ref[q], gate_ref[q] = membership(ids, weights, rank_ref.shape[1])
        rank = jnp.concatenate([rank_ref[q, pl.ds(first_ref[p], 2), :] for p in range(len(chunks))], axis=0)
        gates = jnp.concatenate([gate_ref[q, pl.ds(first_ref[p], 2), :] for p in range(len(chunks))], axis=0)
        slot = lax.broadcasted_iota(jnp.int32, (rank.shape[0], CAP, tok), 1).astype(F32)
        chosen = rank[:, None, :] == slot
        rows = jnp.concatenate([chunk[q] for chunk in chunks], axis=0)
        total = None
        for part in split_parts(gates, 3) if weighted else [jnp.ones_like(gates)]:
            pick = jnp.where(chosen, part[:, None, :], 0.0).reshape(-1, tok).astype(BF)
            term = lax.dot_general(pick, rows, (((0,), (0,)), ((), ())), preferred_element_type=F32)
            total = term if total is None else total + term
        sums.append(total)
    return sums


def combine_kernel(weighted, first_ref, *refs):
    facts, chunks, outs, tables = refs[:SIDE], refs[SIDE : -SIDE - 2], refs[-SIDE - 2 : -2], refs[-2:]
    for out, total in zip(outs, combine(first_ref, facts, chunks, *tables, weighted)):
        out[...] = total.astype(out.dtype)


def total_kernel(own_ref, *refs):
    total = own_ref[...]
    for ref in refs[:-1]:
        total = total + ref[...].astype(F32)
    refs[-1][...] = total.astype(BF)


def load_rows(chunks):
    return jnp.concatenate([chunk[0, 0] for chunk in chunks], axis=0)


def store_rows(rows, outs, hold_ref):
    expert = pl.program_id(0)

    @pl.when(expert == 0)
    def _():
        hold_ref[...] = rows

    @pl.when(expert == 1)
    def _():
        for p, out in enumerate(outs):
            for q in range(SIDE):
                part = pl.ds((p * SIDE + q) * CAP, CAP)
                low = (p * SIDE + q) * CAP
                out[q] = jnp.concatenate([hold_ref[part, :], rows[low : low + CAP]], axis=0).astype(BF)


def load_lift(weights_ref, expert):
    return jnp.concatenate(
        [weights_ref[j, pl.ds(pl.multiple_of(expert * 128, 128), 128), :] for j in range(8)], axis=0
    )


def load_down(weights_ref, expert):
    base = weights_ref.shape[1] - 128
    return jnp.concatenate(
        [
            jnp.concatenate(
                [
                    weights_ref[j, base:, pl.ds(pl.multiple_of(expert * 384 + kb * 128, 128), 128)]
                    for j in range(8)
                ],
                axis=1,
            )
            for kb in range(3)
        ],
        axis=0,
    )


def expert_kernel(*refs):
    chunks, (weights_ref, act_ref, hid_ref, grad_ref) = refs[:-4], refs[-4:]
    count = len(chunks) // 2
    expert = pl.program_id(0)
    rows, back = load_rows(chunks[:count]), load_rows(chunks[count:])
    hidden = jnp.dot(rows, load_lift(weights_ref, expert), preferred_element_type=F32)
    ff = hidden.shape[1] // 2
    gate, up = hidden[:, :ff], hidden[:, ff:]
    sig = jax.nn.sigmoid(gate)
    swish = gate * sig
    act = (swish * up).astype(BF)
    act_ref[0] = act
    act_grad = lax.dot_general(
        back, load_down(weights_ref, expert), (((1,), (1,)), ((), ())), preferred_element_type=F32
    )
    slope = sig * (1.0 + gate * (1.0 - sig))
    hid = jnp.concatenate([(act_grad * up * slope).astype(BF), (act_grad * swish).astype(BF)], axis=1)
    hid_ref[0] = hid
    first = (((0,), (0,)), ((), ()))
    down = lax.dot_general(act, back, first, preferred_element_type=F32).astype(BF)
    lift = lax.dot_general(rows, hid, first, preferred_element_type=F32).astype(BF)
    base = weights_ref.shape[1] - 128
    for j in range(8):
        grad_ref[j, pl.ds(pl.multiple_of(expert * 128, 128), 128), :] = lift[j * 128 : (j + 1) * 128]
        for kb in range(3):
            grad_ref[j, base:, pl.ds(pl.multiple_of(expert * 384 + kb * 128, 128), 128)] = down[
                kb * 128 : (kb + 1) * 128, j * 128 : (j + 1) * 128
            ]


def result_kernel(act_ref, weights_ref, *refs):
    out = jnp.dot(act_ref[0], load_down(weights_ref, pl.program_id(0)), preferred_element_type=F32)
    store_rows(out, refs[:-1], refs[-1])


def input_grad_kernel(hid_ref, weights_ref, *refs):
    grad = lax.dot_general(
        hid_ref[0],
        load_lift(weights_ref, pl.program_id(0)),
        (((1,), (1,)), ((), ())),
        preferred_element_type=F32,
    )
    store_rows(grad, refs[:-1], refs[-1])


def shards(tokens, expert_ids, combine_weights, lift_weights, down_weights, cotangent):
    tok, top = expert_ids.shape
    local, slice_rows, lift_width = lift_weights.shape
    ff = down_weights.shape[1]
    width = tokens.shape[1]
    owners = lax.axis_size("expert")
    groups = lax.axis_size("dp")
    experts = local * owners
    slots = owners * CAP
    bundle = local * slice_rows + 128
    vm = pl.BlockSpec(memory_space=pltpu.VMEM)

    joined = jnp.concatenate(
        [
            lift_weights.reshape(local * slice_rows, lift_width),
            down_weights.reshape(local, ff // 128, 128, 128).transpose(2, 0, 1, 3).reshape(128, lift_width),
        ],
        axis=0,
    )
    weights = lax.all_gather(joined, "dp")

    me = lax.axis_index("expert")
    near = SIDE * CORES

    def device(along, across, core):
        first = along if core == 0 else across
        second = across if core == 0 else along
        return (first % SIDE) * near + (second % SIDE) * CORES + core

    def place(n):
        x, y, c = n // near, n // CORES % SIDE, n % CORES
        return (x, y, c) if c == 0 else (y, x, c)

    def share_to(n, step):
        along, across, c = place(n)
        return device(along + step, across, c)

    def send_to(n, step, flip):
        x, y, c = n // near, n // CORES % SIDE, n % CORES
        x, y = (x, y + step) if c == 0 else (x + step, y)
        return (x % SIDE) * near + (y % SIDE) * CORES + (c + flip) % CORES

    def table(values):
        return jnp.asarray(values, jnp.int32)[me]

    hops = [(step, flip) for step in range(SIDE) for flip in range(CORES)]
    everyone = range(owners)
    first_expert = table([[local * send_to(n, *hop) for hop in hops] for n in everyone])

    ids, gates = expert_ids.T, combine_weights.T
    bundle_shape = jax.ShapeDtypeStruct((2 * tok + 16, width), BF)
    own = call(bundle_kernel, "bundle", bundle_shape, in_specs=[vm] * 4, nbytes=1 << 20)(
        ids, gates, tokens, cotangent
    )
    bundles = [own] + [
        lax.ppermute(own, "expert", [(n, share_to(n, q)) for n in everyone]) for q in range(1, SIDE)
    ]
    chunk_shape = jax.ShapeDtypeStruct((2, local, SIDE * CAP, width), BF)
    smem = pl.BlockSpec(memory_space=pltpu.SMEM)
    pack_flops = 2 * experts * CAP * tok * width
    table_scratch = pltpu.VMEM((SIDE, experts, tok), F32)
    packed = call(
        pack_kernel,
        "pack",
        [chunk_shape] * len(hops),
        grid=(2,),
        in_specs=[smem] + [vm] * SIDE,
        out_specs=[pl.BlockSpec((1, local, SIDE * CAP, width), lambda i: (i, 0, 0, 0))] * len(hops),
        scratch=[table_scratch, table_scratch],
        flops=2 * pack_flops,
        nbytes=16 << 20,
    )(first_expert, *bundles)
    chunks = [
        packed[p] if p == 0 else lax.ppermute(packed[p], "expert", [(n, send_to(n, *hop)) for n in everyone])
        for p, hop in enumerate(hops)
    ]

    count = len(hops)
    rows_blocks = [pl.BlockSpec((1, 1, SIDE * CAP, width), lambda e: (0, e, 0, 0))] * count
    back_blocks = [pl.BlockSpec((1, 1, SIDE * CAP, width), lambda e: (1, e, 0, 0))] * count
    weight_block = pl.BlockSpec((groups, bundle, lift_width), lambda e: (0, 0, 0))
    half_block = pl.BlockSpec((1, slots, ff), lambda e: (e, 0, 0))
    hid_block = pl.BlockSpec((1, slots, 2 * ff), lambda e: (e, 0, 0))
    back_shape = jax.ShapeDtypeStruct((SIDE, local * CAP, width), BF)
    back_block = pl.BlockSpec((SIDE, local * CAP, width), lambda e: (0, 0, 0))
    unit = 2 * local * slots * ff * width
    act, hid, weight_grads = call(
        expert_kernel,
        "expert",
        [
            jax.ShapeDtypeStruct((local, slots, ff), BF),
            jax.ShapeDtypeStruct((local, slots, 2 * ff), BF),
            jax.ShapeDtypeStruct((groups, bundle, lift_width), BF),
        ],
        grid=(local,),
        in_specs=rows_blocks + back_blocks + [weight_block],
        out_specs=[half_block, hid_block, weight_block],
        flops=6 * unit,
        nbytes=20 << 20,
    )(*chunks, *chunks, weights)
    summed = lax.psum_scatter(weight_grads, "dp", scatter_dimension=0, tiled=False)

    def returning(kernel, name, block, work, *operands):
        results = call(
            kernel,
            name,
            [back_shape] * count,
            grid=(local,),
            in_specs=[block, weight_block],
            out_specs=[back_block] * count,
            scratch=[pltpu.VMEM((slots, width), F32)],
            flops=work,
            nbytes=10 << 20,
        )(*operands)
        return [
            results[p] if p == 0 else lax.ppermute(results[p], "expert", [(send_to(n, *hop), n) for n in everyone])
            for p, hop in enumerate(hops)
        ]

    facts_block = pl.BlockSpec((16, width), lambda i: (2 * tok // 16, 0))
    whole_block = pl.BlockSpec((SIDE, local * CAP, width), lambda i: (0, 0, 0))
    token_shape = jax.ShapeDtypeStruct((tok, width), BF)
    token_block = pl.BlockSpec((tok, width), lambda i: (0, 0))

    def collected(weighted, name, results):
        sums = call(
            functools.partial(combine_kernel, weighted),
            name,
            [jax.ShapeDtypeStruct((tok, width), F32)] + [token_shape] * (SIDE - 1),
            grid=(1,),
            in_specs=[smem] + [facts_block] * SIDE + [whole_block] * count,
            out_specs=[token_block] * SIDE,
            scratch=[table_scratch, table_scratch],
            flops=pack_flops * (3 if weighted else 1),
            nbytes=4 << 20,
        )(first_expert, *bundles, *results)
        return list(sums[:1]) + [
            lax.ppermute(sums[q], "expert", [(share_to(n, q), n) for n in everyone]) for q in range(1, SIDE)
        ]

    def added(name, sums):
        return call(total_kernel, name, token_shape, in_specs=[vm] * SIDE, nbytes=1 << 20)(*sums)

    results = returning(result_kernel, "result", half_block, unit, act, weights)
    grads = returning(input_grad_kernel, "input_grad", hid_block, 2 * unit, hid, weights)
    result_sums = collected(True, "combine_out", results)
    grad_sums = collected(False, "combine_grad", grads)
    layer_output = added("total_out", result_sums)
    token_grads = added("total_grad", grad_sums)

    lift_grads = summed[: local * slice_rows].reshape(local, slice_rows, lift_width)
    down_grads = (
        summed[local * slice_rows :].reshape(128, local, ff // 128, 128).transpose(1, 2, 0, 3).reshape(local, ff, 128)
    )
    return (layer_output, token_grads, lift_grads, down_grads)


def solution(mesh):
    rows = P(("expert", "dp"), None)
    lift, down = P("expert", "dp", None), P("expert", None, "dp")
    return jax.shard_map(
        shards,
        mesh=mesh,
        in_specs=(rows, rows, rows, lift, down, rows),
        out_specs=(rows, rows, lift, down),
        check_vma=False,
    )
```

time: 231 us -> 185 us (0.80)
  waiting for transfers between devices: 131 us -> 64 us
  starting transfers between devices: 23.8 us -> 44.7 us
  Pallas kernels: 46.9 us -> 51.1 us
  local copies, waits for them, and re-layouts: 12.1 us -> 8.44 us
    all_to_all x4 -> x0, waiting for transfers between devices: 129 us -> none  [exchange(): return lax.all_to_all(x.reshape(buffer_shape), 'expert', 0, 0, tiled=True)]
    ppermute x0 -> x30, waiting for transfers between devices: none -> 64 us  [the longest x7 30.1 us: shards(): lax.ppermute(packed[p], 'expert', [(n, send_to(n, *hop)) for n in everyone])]
    ppermute x0 -> x30, starting transfers between devices: none -> 44.6 us  [the longest x14 19.1 us: returning(): lax.ppermute(results[p], 'expert', [(send_to(n, *hop), n) for n in everyo...]
    all_to_all x4 -> x0, starting transfers between devices: 23.7 us -> none  [exchange(): return lax.all_to_all(x.reshape(buffer_shape), 'expert', 0, 0, tiled=True)]
    pallas_call x7 -> x9, Pallas kernels: 46.9 us -> 51.1 us  [the longest x2 14.7 us: returning(): call(kernel, name, [back_shape] * count, grid=(local,), in_specs=[block,...]
    unnamed x10 -> x60, local copies, waits for them, and re-layouts: 7.12 us -> 3.22 us
    all_gather x1, waiting for transfers between devices: 2.88 us -> 0.01 us  [shards(): weights = lax.all_gather(joined, 'dp')]
  transfers between devices with their start and end apart: 6 -> 32, of which waited for: 5 -> 13; matrix products, arithmetic and copies ran while one was open for 1% -> 1% of each run, Pallas kernels for 15% -> 20%
where the time goes in v2:
time: 185 us; the launch traced here: 184 us
  waiting for transfers between devices  64 us (35%)
  Pallas kernels  51.1 us (28%)
  starting transfers between devices  44.7 us (24%)
  between operations  14.3 us (8%)
  local copies, waits for them, and re-layouts  8.44 us (5%)
  other arithmetic  1.85 us (1%)
    ppermute x7, waiting for transfers between devices, shards(): lax.ppermute(packed[p], 'expert', [(n, send_to(n, *hop)) for n in everyone])  30.1 us
    ppermute x14, starting transfers between devices, returning(): lax.ppermute(results[p], 'expert', [(send_to(n, *hop), n) for n in everyo...  19.1 us
    pallas_call x2, Pallas kernels, returning(): call(kernel, name, [back_shape] * count, grid=(local,), in_specs=[block,...  14.7 us
    pallas_call x1, Pallas kernels, shards(): call(expert_kernel, 'expert', [jax.ShapeDtypeStruct((local, slots, ff), B...  14.4 us
    ppermute x3, waiting for transfers between devices, shards(): lax.ppermute(own, 'expert', [(n, share_to(n, q)) for n in everyone])  14.2 us
    ppermute x14, waiting for transfers between devices, returning(): lax.ppermute(results[p], 'expert', [(send_to(n, *hop), n) for n in everyo...  13.4 us
    ppermute x7, starting transfers between devices, shards(): lax.ppermute(packed[p], 'expert', [(n, send_to(n, *hop)) for n in everyone])  10.7 us
    ppermute x6, starting transfers between devices, collected(): lax.ppermute(sums[q], 'expert', [(share_to(n, q), n) for n in everyone])  10.2 us
  transfers between devices with their start and end apart: 32, of which 13 were waited for; matrix products, arithmetic and copies ran while one was open for 1% of the time, Pallas kernels for 20%

profile of v2, /device:TPU:1, one launch (start us, length us, event | category | flops | bytes accessed | tf_op | source)
XLA Modules:
  0.0 184.5 jit_solution(7509431538849070654)
XLA Ops:
  7.2 1.1 copy.15
  8.5 1.8 %pad_maximum_fusion = bf16[384,768]{1,0:T(8,128)(2,1)} fusion(bf16[128,768]{1,0:T(8,128)(2,1)S(1)} %copy.16, bf16[256,768]{1,0:T(8,128)(2,1)} %bitcast.21), kind=kLoop, calls=%fused_computation | loop fusion | flops 1179648 | bytes 1179648 | tf_op jit(solution)/shard_map/concatenate | solution.py:231
  10.4 1.9 %bundle.1.refs_0_ = bf16[272,1024]{1,0:T(8,128)(2,1)} custom-call(s32[8,128]{1,0:T(8,128)} %bitcast.24, f32[8,128]{1,0:T(8,128)} %bitcast.25, bf16[128,1024]{1,0:T(8,128)(2,1)} %tokens_ref.1, bf16[128,1024]{1,0:T(8,128)(2,1)} %cot_ref.1), custom_call_target="tpu_custom_call" | custom-call | bytes 1048576 | tf_op jit(solution)/shard_map/bundle/pallas_call | solution.py:270
  12.3 3.6 %collective-permute-start.2 = (bf16[272,1024]{1,0:T(8,128)(2,1)}, bf16[272,1024]{1,0:T(8,128)(2,1)S(1)}, u32[]{:S(2)}, u32[]{:S(2)}) collective-permute-start(bf16[272,1024]{1,0:T(8,128)(2,1)} %bundle.1.refs_0_), channel_id=1, source_target_pairs={{0,192},{8,56},{16,208},{24,8},{32,224},{40,24},{48,240},{56,40},{... | collective-permute-start | bytes 1671176 | tf_op jit(solution)/shard_map/ppermute | solution.py:274
  16.9 1.2 dynamic-slice_bitcast_fusion.first_ref
  18.1 10.5 %collective-permute-done.2.refs_3_ = bf16[272,1024]{1,0:T(8,128)(2,1)S(1)} collective-permute-done((bf16[272,1024]{1,0:T(8,128)(2,1)}, bf16[272,1024]{1,0:T(8,128)(2,1)S(1)}, u32[]{:S(2)}, u32[]{:S(2)}) %collective-permute-start.2) | collective-permute-done | bytes 557088 | tf_op jit(solution)/shard_map/ppermute | solution.py:274
  28.6 3.7 %collective-permute-done.refs_1_ = bf16[272,1024]{1,0:T(8,128)(2,1)S(1)} collective-permute-done((bf16[272,1024]{1,0:T(8,128)(2,1)}, bf16[272,1024]{1,0:T(8,128)(2,1)S(1)}, u32[]{:S(2)}, u32[]{:S(2)}) %collective-permute-start) | collective-permute-done | bytes 557088 | tf_op jit(solution)/shard_map/ppermute | solution.py:274
  32.3 0.8 copy-done.2
  33.1 6.4 %pack.1 = (bf16[2,2,96,1024]{3,2,1,0:T(8,128)(2,1)}, bf16[2,2,96,1024]{3,2,1,0:T(8,128)(2,1)}, bf16[2,2,96,1024]{3,2,1,0:T(8,128)(2,1)}, bf16[2,2,96,1024]{3,2,1...) custom-call(s32[8]{0:T(128)} %dynamic-slice_bitcast_fusion.first_ref, ...), custom_call_target="tpu_custom_call" | custom-call | flops 805306368 | bytes 16777216 | tf_op jit(solution)/shard_map/pack/pallas_call | solution.py:280
  39.5 1.4 collective-permute-start.3
  41.6 2.6 %collective-permute-start.6 = (bf16[2,2,96,1024]{3,2,1,0:T(8,128)(2,1)}, bf16[2,2,96,1024]{3,2,1,0:T(8,128)(2,1)S(1)}, u32[]{:S(2)}, u32[]{:S(2)}) collective-permute-start(bf16[2,2,96,1024]{3,2,1,0:T(8,128)(2,1)} %get-tuple-element.43), channel_id=1, source_target_pairs={{0,32},{8,136},{16,48},{24,152},{32,0},{40,168},{48,16},{56,184},{... | collective-permute-start | bytes 2359304 | tf_op jit(solution)/shard_map/ppermute | solution.py:292
  44.2 2.9 %collective-permute-start.7 = (bf16[2,2,96,1024]{3,2,1,0:T(8,128)(2,1)}, bf16[2,2,96,1024]{3,2,1,0:T(8,128)(2,1)}, u32[]{:S(2)}, u32[]{:S(2)}) collective-permute-start(bf16[2,2,96,1024]{3,2,1,0:T(8,128)(2,1)} %get-tuple-element.44), channel_id=1, source_target_pairs={{0,40},{8,128},{16,56},{24,144},{32,8},{40,160},{48,24},{56,176},{... | collective-permute-start | bytes 2359304 | tf_op jit(solution)/shard_map/ppermute | solution.py:292
  47.1 0.9 collective-permute-start.8
  48.1 5.5 %collective-permute-done.4.refs_2_.refs_10_ = bf16[2,2,96,1024]{3,2,1,0:T(8,128)(2,1)S(1)} collective-permute-done((bf16[2,2,96,1024]{3,2,1,0:T(8,128)(2,1)}, bf16[2,2,96,1024]{3,2,1,0:T(8,128)(2,1)S(1)}, u32[]{:S(2)}, u32[]{:S(2)}) %collective-permute-start.4) | collective-permute-done | bytes 786464 | tf_op jit(solution)/shard_map/ppermute | solution.py:292
  53.6 2.2 %collective-permute-start.9 = (bf16[2,2,96,1024]{3,2,1,0:T(8,128)(2,1)}, bf16[2,2,96,1024]{3,2,1,0:T(8,128)(2,1)}, u32[]{:S(2)}, u32[]{:S(2)}) collective-permute-start(bf16[2,2,96,1024]{3,2,1,0:T(8,128)(2,1)} %get-tuple-element.46), channel_id=1, source_target_pairs={{0,56},{8,192},{16,8},{24,208},{32,24},{40,224},{48,40},{56,240},{... | collective-permute-start | bytes 2359304 | tf_op jit(solution)/shard_map/ppermute | solution.py:292
  55.8 6.8 %collective-permute-done.5.refs_3_.refs_11_ = bf16[2,2,96,1024]{3,2,1,0:T(8,128)(2,1)S(1)} collective-permute-done((bf16[2,2,96,1024]{3,2,1,0:T(8,128)(2,1)}, bf16[2,2,96,1024]{3,2,1,0:T(8,128)(2,1)S(1)}, u32[]{:S(2)}, u32[]{:S(2)}) %collective-permute-start.5) | collective-permute-done | bytes 786464 | tf_op jit(solution)/shard_map/ppermute | solution.py:292
  62.6 7.5 %collective-permute-done.6.refs_4_.refs_12_ = bf16[2,2,96,1024]{3,2,1,0:T(8,128)(2,1)S(1)} collective-permute-done((bf16[2,2,96,1024]{3,2,1,0:T(8,128)(2,1)}, bf16[2,2,96,1024]{3,2,1,0:T(8,128)(2,1)S(1)}, u32[]{:S(2)}, u32[]{:S(2)}) %collective-permute-start.6) | collective-permute-done | bytes 786464 | tf_op jit(solution)/shard_map/ppermute | solution.py:292
  70.1 10.3 %collective-permute-done.7.refs_5_.refs_13_ = bf16[2,2,96,1024]{3,2,1,0:T(8,128)(2,1)} collective-permute-done((bf16[2,2,96,1024]{3,2,1,0:T(8,128)(2,1)}, bf16[2,2,96,1024]{3,2,1,0:T(8,128)(2,1)}, u32[]{:S(2)}, u32[]{:S(2)}) %collective-permute-start.7) | collective-permute-done | bytes 786464 | tf_op jit(solution)/shard_map/ppermute | solution.py:292
  80.5 14.4 %expert.1 = (bf16[2,768,384]{2,1,0:T(8,128)(2,1)}, bf16[2,768,768]{2,1,0:T(8,128)(2,1)}, bf16[8,384,768]{2,1,0:T(8,128)(2,1)}) custom-call(bf16[2,2,96,1024]{3,2,1,0:T(8,128)(2,1)} %get-tuple-element.39.refs_0_.refs_8_, bf16[2,2,96,1024]{3,2,1,0:T(8,128)(2,1)} %copy-done.24, bf16[2,2,96,1024]{3,2,1,0:T(8,128)(2,1)} %copy-done.25, ...), custom_call_target="tpu_custom_call" | custom-call | flops 7247757312 | bytes 20971520 | tf_op jit(solution)/shard_map/expert/pallas_call | solution.py:305
  94.9 6.6 %result.1 = (bf16[4,48,1024]{2,1,0:T(8,128)(2,1)}, bf16[4,48,1024]{2,1,0:T(8,128)(2,1)}, bf16[4,48,1024]{2,1,0:T(8,128)(2,1)}, bf16[4,48,1024]{2,1,0:T(8,128)(2,...) custom-call(bf16[2,768,384]{2,1,0:T(8,128)(2,1)} %get-tuple-element., ...), custom_call_target="tpu_custom_call" | custom-call | flops 1207959552 | bytes 10485760 | tf_op jit(solution)/shard_map/result/pallas_call | solution.py:322
  101.5 1.0 collective-permute-start.10
  102.5 2.4 %collective-permute-start.11 = (bf16[4,48,1024]{2,1,0:T(8,128)(2,1)}, bf16[4,48,1024]{2,1,0:T(8,128)(2,1)S(1)}, u32[]{:S(2)}, u32[]{:S(2)}) collective-permute-start(bf16[4,48,1024]{2,1,0:T(8,128)(2,1)} %get-tuple-element.50), channel_id=1, source_target_pairs={{16,0},{72,8},{32,16},{88,24},{48,32},{104,40},{0,48},{120,56},{80... | collective-permute-start | bytes 1179656 | tf_op jit(solution)/shard_map/ppermute | solution.py:334
  104.9 0.7 collective-permute-start.12
  105.6 1.1 collective-permute-start.13
  106.7 1.7 collective-permute-start.14
  108.5 8.0 %input_grad.1 = (bf16[4,48,1024]{2,1,0:T(8,128)(2,1)}, bf16[4,48,1024]{2,1,0:T(8,128)(2,1)}, bf16[4,48,1024]{2,1,0:T(8,128)(2,1)}, bf16[4,48,1024]{2,1,0:T(8,128...) custom-call(bf16[2,768,768]{2,1,0:T(8,128)(2,1)} %get-tuple-element., ...), custom_call_target="tpu_custom_call" | custom-call | flops 2415919104 | bytes 10485760 | tf_op jit(solution)/shard_map/input_grad/pallas_call | solution.py:322
  116.5 1.5 collective-permute-start.15
  118.0 3.8 %collective-permute-done.11.refs_6_ = bf16[4,48,1024]{2,1,0:T(8,128)(2,1)S(1)} collective-permute-done((bf16[4,48,1024]{2,1,0:T(8,128)(2,1)}, bf16[4,48,1024]{2,1,0:T(8,128)(2,1)S(1)}, u32[]{:S(2)}, u32[]{:S(2)}) %collective-permute-start.11) | collective-permute-done | bytes 393248 | tf_op jit(solution)/shard_map/ppermute | solution.py:334
  122.3 0.7 collective-permute-start.20
  123.0 3.3 %collective-permute-start.21 = (bf16[4,48,1024]{2,1,0:T(8,128)(2,1)}, bf16[4,48,1024]{2,1,0:T(8,128)(2,1)S(1)}, u32[]{:S(2)}, u32[]{:S(2)}) collective-permute-start(bf16[4,48,1024]{2,1,0:T(8,128)(2,1)} %get-tuple-element.63), channel_id=1, source_target_pairs={{16,0},{72,8},{32,16},{88,24},{48,32},{104,40},{0,48},{120,56},{80... | collective-permute-start | bytes 1179656 | tf_op jit(solution)/shard_map/ppermute | solution.py:334
  126.4 4.0 %collective-permute-start.23 = (bf16[4,48,1024]{2,1,0:T(8,128)(2,1)}, bf16[4,48,1024]{2,1,0:T(8,128)(2,1)S(1)}, u32[]{:S(2)}, u32[]{:S(2)}) collective-permute-start(bf16[4,48,1024]{2,1,0:T(8,128)(2,1)} %get-tuple-element.65), channel_id=1, source_target_pairs={{32,0},{136,8},{48,16},{152,24},{0,32},{168,40},{16,48},{184,56},{... | collective-permute-start | bytes 1179656 | tf_op jit(solution)/shard_map/ppermute | solution.py:334
  130.7 2.6 %collective-permute-start.24 = (bf16[4,48,1024]{2,1,0:T(8,128)(2,1)}, bf16[4,48,1024]{2,1,0:T(8,128)(2,1)S(1)}, u32[]{:S(2)}, u32[]{:S(2)}) collective-permute-start(bf16[4,48,1024]{2,1,0:T(8,128)(2,1)} %get-tuple-element.66), channel_id=1, source_target_pairs={{40,0},{128,8},{56,16},{144,24},{8,32},{160,40},{24,48},{176,56},{... | collective-permute-start | bytes 1179656 | tf_op jit(solution)/shard_map/ppermute | solution.py:334
  133.3 8.9 %collective-permute-done.21.refs_6_ = bf16[4,48,1024]{2,1,0:T(8,128)(2,1)S(1)} collective-permute-done((bf16[4,48,1024]{2,1,0:T(8,128)(2,1)}, bf16[4,48,1024]{2,1,0:T(8,128)(2,1)S(1)}, u32[]{:S(2)}, u32[]{:S(2)}) %collective-permute-start.21) | collective-permute-done | bytes 393248 | tf_op jit(solution)/shard_map/ppermute | solution.py:334
  142.2 5.4 %combine_out.1 = (f32[128,1024]{1,0:T(8,128)}, bf16[128,1024]{1,0:T(8,128)(2,1)}, bf16[128,1024]{1,0:T(8,128)(2,1)}, bf16[128,1024]{1,0:T(8,128)(2,1)}) custom-call(s32[8]{0:T(128)} %dynamic-slice_bitcast_fusion.first_ref, bf16[272,1024]{1,0:T(8,128)(2,1)} %bundle.1.refs_0_, bf16[272,1024]{1,0:T(8,128)(2,1)} %copy-done.2, bf16[272,1024]{1,0:T(8,128)(2,1)} %copy-done.1, ...), custom_call_target="tpu_custom_call" | custom-call | flops 1207959552 | bytes 4194304 | tf_op jit(solution)/shard_map/combine_out/pallas_call | solution.py:344
  147.7 4.9 %collective-permute-start.17 = (bf16[128,1024]{1,0:T(8,128)(2,1)}, bf16[128,1024]{1,0:T(8,128)(2,1)S(1)}, u32[]{:S(2)}, u32[]{:S(2)}) collective-permute-start(bf16[128,1024]{1,0:T(8,128)(2,1)} %get-tuple-element.57), channel_id=1, source_target_pairs={{64,0},{24,8},{80,16},{40,24},{96,32},{56,40},{112,48},{8,56},{128... | collective-permute-start | bytes 786440 | tf_op jit(solution)/shard_map/ppermute | solution.py:356
  152.5 1.9 %collective-permute-start.18 = (bf16[128,1024]{1,0:T(8,128)(2,1)}, bf16[128,1024]{1,0:T(8,128)(2,1)S(1)}, u32[]{:S(2)}, u32[]{:S(2)}) collective-permute-start(bf16[128,1024]{1,0:T(8,128)(2,1)} %get-tuple-element.58), channel_id=1, source_target_pairs={{128,0},{40,8},{144,16},{56,24},{160,32},{8,40},{176,48},{24,56},{... | collective-permute-start | bytes 786440 | tf_op jit(solution)/shard_map/ppermute | solution.py:356
  154.5 0.7 collective-permute-start.19
  155.3 0.7 copy-done.15
  156.1 4.2 %combine_grad.1 = (f32[128,1024]{1,0:T(8,128)}, bf16[128,1024]{1,0:T(8,128)(2,1)}, bf16[128,1024]{1,0:T(8,128)(2,1)}, bf16[128,1024]{1,0:T(8,128)(2,1)}) custom-call(s32[8]{0:T(128)} %dynamic-slice_bitcast_fusion.first_ref, bf16[272,1024]{1,0:T(8,128)(2,1)} %bundle.1.refs_0_, bf16[272,1024]{1,0:T(8,128)(2,1)} %copy-done.2, bf16[272,1024]{1,0:T(8,128)(2,1)} %copy-done.1, ...), custom_call_target="tpu_custom_call" | custom-call | flops 402653184 | bytes 4194304 | tf_op jit(solution)/shard_map/combine_grad/pallas_call | solution.py:344
  160.3 2.0 %collective-permute-start.27 = (bf16[128,1024]{1,0:T(8,128)(2,1)}, bf16[128,1024]{1,0:T(8,128)(2,1)S(1)}, u32[]{:S(2)}, u32[]{:S(2)}) collective-permute-start(bf16[128,1024]{1,0:T(8,128)(2,1)} %get-tuple-element.70), channel_id=1, source_target_pairs={{64,0},{24,8},{80,16},{40,24},{96,32},{56,40},{112,48},{8,56},{128... | collective-permute-start | bytes 786440 | tf_op jit(solution)/shard_map/ppermute | solution.py:356
  163.7 2.1 %total_out.1 = bf16[128,1024]{1,0:T(8,128)(2,1)} custom-call(f32[128,1024]{1,0:T(8,128)} %get-tuple-element.56.own_ref, bf16[128,1024]{1,0:T(8,128)(2,1)} %copy-done.18, bf16[128,1024]{1,0:T(8,128)(2,1)} %copy-done.19, bf16[128,1024]{1,0:T(8,128)(2,1)} %copy-done.20), custom_call_target="tpu_custom_call" | custom-call | bytes 1048576 | tf_op jit(solution)/shard_map/total_out/pallas_call | solution.py:360
  165.8 2.9 %collective-permute-done.27.refs_0_ = bf16[128,1024]{1,0:T(8,128)(2,1)S(1)} collective-permute-done((bf16[128,1024]{1,0:T(8,128)(2,1)}, bf16[128,1024]{1,0:T(8,128)(2,1)S(1)}, u32[]{:S(2)}, u32[]{:S(2)}) %collective-permute-start.27) | collective-permute-done | bytes 262176 | tf_op jit(solution)/shard_map/ppermute | solution.py:356
  169.3 2.7 %collective-permute-done.29.refs_2_ = bf16[128,1024]{1,0:T(8,128)(2,1)S(1)} collective-permute-done((bf16[128,1024]{1,0:T(8,128)(2,1)}, bf16[128,1024]{1,0:T(8,128)(2,1)S(1)}, u32[]{:S(2)}, u32[]{:S(2)}) %collective-permute-start.29) | collective-permute-done | bytes 262176 | tf_op jit(solution)/shard_map/ppermute | solution.py:356
  172.0 0.7 copy-done.23
  172.7 2.1 %total_grad.1 = bf16[128,1024]{1,0:T(8,128)(2,1)} custom-call(f32[128,1024]{1,0:T(8,128)} %get-tuple-element.69.own_ref, bf16[128,1024]{1,0:T(8,128)(2,1)} %copy-done.21, bf16[128,1024]{1,0:T(8,128)(2,1)} %copy-done.22, bf16[128,1024]{1,0:T(8,128)(2,1)} %copy-done.23), custom_call_target="tpu_custom_call" | custom-call | bytes 1048576 | tf_op jit(solution)/shard_map/total_grad/pallas_call | solution.py:360
  174.8 1.0 slice.11
  176.0 0.8 copy.18
  176.8 0.8 slice.10
  (95 shorter events, 5.2 us)
Async XLA Ops:
  7.2 73.3 %all-gather.3.cloned.1.call-start = ((), (), s32[]{:S(2)}) async-start(), calls=%async_computation.2 | async-start | bytes 5308416 | tf_op jit(solution)/shard_map/all_gather | solution.py:238
  10.3 164.5 %reduce-scatter.2.cloned.1.call-start = ((), (), s32[]{:S(2)}) async-start(), calls=%async_computation.1 | async-start | bytes 5308416 | tf_op jit(solution)/shard_map/reduce_scatter | solution.py:319
  12.3 16.3 %collective-permute-start.2 = (bf16[272,1024]{1,0:T(8,128)(2,1)}, bf16[272,1024]{1,0:T(8,128)(2,1)S(1)}, u32[]{:S(2)}, u32[]{:S(2)}) collective-permute-start(bf16[272,1024]{1,0:T(8,128)(2,1)} %bundle.1.refs_0_), channel_id=1, source_target_pairs={{0,192},{8,56},{16,208},{24,8},{32,224},{40,24},{48,240},{56,40},{... | collective-permute-start | bytes 1671176 | tf_op jit(solution)/shard_map/ppermute | solution.py:274
  15.9 12.8 %collective-permute-start.1 = (bf16[272,1024]{1,0:T(8,128)(2,1)}, bf16[272,1024]{1,0:T(8,128)(2,1)S(1)}, u32[]{:S(2)}, u32[]{:S(2)}) collective-permute-start(bf16[272,1024]{1,0:T(8,128)(2,1)} %bundle.1.refs_0_), channel_id=1, source_target_pairs={{0,128},{8,40},{16,144},{24,56},{32,160},{40,8},{48,176},{56,24},{... | collective-permute-start | bytes 1671176 | tf_op jit(solution)/shard_map/ppermute | solution.py:274
  16.2 16.1 %collective-permute-start = (bf16[272,1024]{1,0:T(8,128)(2,1)}, bf16[272,1024]{1,0:T(8,128)(2,1)S(1)}, u32[]{:S(2)}, u32[]{:S(2)}) collective-permute-start(bf16[272,1024]{1,0:T(8,128)(2,1)} %bundle.1.refs_0_), channel_id=1, source_target_pairs={{0,64},{8,24},{16,80},{24,40},{32,96},{40,56},{48,112},{56,8},{64,... | collective-permute-start | bytes 1671176 | tf_op jit(solution)/shard_map/ppermute | solution.py:274
  39.5 7.6 %collective-permute-start.3 = (bf16[2,2,96,1024]{3,2,1,0:T(8,128)(2,1)}, bf16[2,2,96,1024]{3,2,1,0:T(8,128)(2,1)S(1)}, u32[]{:S(2)}, u32[]{:S(2)}) collective-permute-start(bf16[2,2,96,1024]{3,2,1,0:T(8,128)(2,1)} %get-tuple-element.40), channel_id=1, source_target_pairs={{0,8},{8,0},{16,24},{24,16},{32,40},{40,32},{48,56},{56,48},{64,72... | collective-permute-start | bytes 2359304 | tf_op jit(solution)/shard_map/ppermute | solution.py:292
  40.9 12.7 %collective-permute-start.4 = (bf16[2,2,96,1024]{3,2,1,0:T(8,128)(2,1)}, bf16[2,2,96,1024]{3,2,1,0:T(8,128)(2,1)S(1)}, u32[]{:S(2)}, u32[]{:S(2)}) collective-permute-start(bf16[2,2,96,1024]{3,2,1,0:T(8,128)(2,1)} %get-tuple-element.41), channel_id=1, source_target_pairs={{0,16},{8,72},{16,32},{24,88},{32,48},{40,104},{48,0},{56,120},{64... | collective-permute-start | bytes 2359304 | tf_op jit(solution)/shard_map/ppermute | solution.py:292
  41.0 21.6 %collective-permute-start.5 = (bf16[2,2,96,1024]{3,2,1,0:T(8,128)(2,1)}, bf16[2,2,96,1024]{3,2,1,0:T(8,128)(2,1)S(1)}, u32[]{:S(2)}, u32[]{:S(2)}) collective-permute-start(bf16[2,2,96,1024]{3,2,1,0:T(8,128)(2,1)} %get-tuple-element.42), channel_id=1, source_target_pairs={{0,24},{8,64},{16,40},{24,80},{32,56},{40,96},{48,8},{56,112},{64,... | collective-permute-start | bytes 2359304 | tf_op jit(solution)/shard_map/ppermute | solution.py:292
  41.6 28.5 %collective-permute-start.6 = (bf16[2,2,96,1024]{3,2,1,0:T(8,128)(2,1)}, bf16[2,2,96,1024]{3,2,1,0:T(8,128)(2,1)S(1)}, u32[]{:S(2)}, u32[]{:S(2)}) collective-permute-start(bf16[2,2,96,1024]{3,2,1,0:T(8,128)(2,1)} %get-tuple-element.43), channel_id=1, source_target_pairs={{0,32},{8,136},{16,48},{24,152},{32,0},{40,168},{48,16},{56,184},{... | collective-permute-start | bytes 2359304 | tf_op jit(solution)/shard_map/ppermute | solution.py:292
  44.2 36.2 %collective-permute-start.7 = (bf16[2,2,96,1024]{3,2,1,0:T(8,128)(2,1)}, bf16[2,2,96,1024]{3,2,1,0:T(8,128)(2,1)}, u32[]{:S(2)}, u32[]{:S(2)}) collective-permute-start(bf16[2,2,96,1024]{3,2,1,0:T(8,128)(2,1)} %get-tuple-element.44), channel_id=1, source_target_pairs={{0,40},{8,128},{16,56},{24,144},{32,8},{40,160},{48,24},{56,176},{... | collective-permute-start | bytes 2359304 | tf_op jit(solution)/shard_map/ppermute | solution.py:292
  47.1 33.3 %copy-start.24 = (bf16[2,2,96,1024]{3,2,1,0:T(8,128)(2,1)}, bf16[2,2,96,1024]{3,2,1,0:T(8,128)(2,1)S(1)}, u32[]{:S(2)}) copy-start(bf16[2,2,96,1024]{3,2,1,0:T(8,128)(2,1)S(1)} %collective-permute-done.3.refs_1_.refs_9_) | copy-start | bytes 2359300
  47.1 33.3 %collective-permute-start.8 = (bf16[2,2,96,1024]{3,2,1,0:T(8,128)(2,1)}, bf16[2,2,96,1024]{3,2,1,0:T(8,128)(2,1)}, u32[]{:S(2)}, u32[]{:S(2)}) collective-permute-start(bf16[2,2,96,1024]{3,2,1,0:T(8,128)(2,1)} %get-tuple-element.45), channel_id=1, source_target_pairs={{0,48},{8,200},{16,0},{24,216},{32,16},{40,232},{48,32},{56,248},{... | collective-permute-start | bytes 2359304 | tf_op jit(solution)/shard_map/ppermute | solution.py:292
  53.6 26.8 %copy-start.25 = (bf16[2,2,96,1024]{3,2,1,0:T(8,128)(2,1)}, bf16[2,2,96,1024]{3,2,1,0:T(8,128)(2,1)S(1)}, u32[]{:S(2)}) copy-start(bf16[2,2,96,1024]{3,2,1,0:T(8,128)(2,1)S(1)} %collective-permute-done.4.refs_2_.refs_10_) | copy-start | bytes 2359300
  53.6 26.8 %collective-permute-start.9 = (bf16[2,2,96,1024]{3,2,1,0:T(8,128)(2,1)}, bf16[2,2,96,1024]{3,2,1,0:T(8,128)(2,1)}, u32[]{:S(2)}, u32[]{:S(2)}) collective-permute-start(bf16[2,2,96,1024]{3,2,1,0:T(8,128)(2,1)} %get-tuple-element.46), channel_id=1, source_target_pairs={{0,56},{8,192},{16,8},{24,208},{32,24},{40,224},{48,40},{56,240},{... | collective-permute-start | bytes 2359304 | tf_op jit(solution)/shard_map/ppermute | solution.py:292
  62.6 17.9 %copy-start.26 = (bf16[2,2,96,1024]{3,2,1,0:T(8,128)(2,1)}, bf16[2,2,96,1024]{3,2,1,0:T(8,128)(2,1)S(1)}, u32[]{:S(2)}) copy-start(bf16[2,2,96,1024]{3,2,1,0:T(8,128)(2,1)S(1)} %collective-permute-done.5.refs_3_.refs_11_) | copy-start | bytes 2359300
  70.1 10.4 %copy-start.27 = (bf16[2,2,96,1024]{3,2,1,0:T(8,128)(2,1)}, bf16[2,2,96,1024]{3,2,1,0:T(8,128)(2,1)S(1)}, u32[]{:S(2)}) copy-start(bf16[2,2,96,1024]{3,2,1,0:T(8,128)(2,1)S(1)} %collective-permute-done.6.refs_4_.refs_12_) | copy-start | bytes 2359300
  101.5 15.0 %collective-permute-start.10 = (bf16[4,48,1024]{2,1,0:T(8,128)(2,1)}, bf16[4,48,1024]{2,1,0:T(8,128)(2,1)S(1)}, u32[]{:S(2)}, u32[]{:S(2)}) collective-permute-start(bf16[4,48,1024]{2,1,0:T(8,128)(2,1)} %get-tuple-element.49), channel_id=1, source_target_pairs={{8,0},{0,8},{24,16},{16,24},{40,32},{32,40},{56,48},{48,56},{72,64... | collective-permute-start | bytes 1179656 | tf_op jit(solution)/shard_map/ppermute | solution.py:334
  102.5 19.3 %collective-permute-start.11 = (bf16[4,48,1024]{2,1,0:T(8,128)(2,1)}, bf16[4,48,1024]{2,1,0:T(8,128)(2,1)S(1)}, u32[]{:S(2)}, u32[]{:S(2)}) collective-permute-start(bf16[4,48,1024]{2,1,0:T(8,128)(2,1)} %get-tuple-element.50), channel_id=1, source_target_pairs={{16,0},{72,8},{32,16},{88,24},{48,32},{104,40},{0,48},{120,56},{80... | collective-permute-start | bytes 1179656 | tf_op jit(solution)/shard_map/ppermute | solution.py:334
  104.9 17.4 %collective-permute-start.12 = (bf16[4,48,1024]{2,1,0:T(8,128)(2,1)}, bf16[4,48,1024]{2,1,0:T(8,128)(2,1)S(1)}, u32[]{:S(2)}, u32[]{:S(2)}) collective-permute-start(bf16[4,48,1024]{2,1,0:T(8,128)(2,1)} %get-tuple-element.51), channel_id=1, source_target_pairs={{24,0},{64,8},{40,16},{80,24},{56,32},{96,40},{8,48},{112,56},{88,... | collective-permute-start | bytes 1179656 | tf_op jit(solution)/shard_map/ppermute | solution.py:334
  105.6 17.4 %collective-permute-start.13 = (bf16[4,48,1024]{2,1,0:T(8,128)(2,1)}, bf16[4,48,1024]{2,1,0:T(8,128)(2,1)S(1)}, u32[]{:S(2)}, u32[]{:S(2)}) collective-permute-start(bf16[4,48,1024]{2,1,0:T(8,128)(2,1)} %get-tuple-element.52), channel_id=1, source_target_pairs={{32,0},{136,8},{48,16},{152,24},{0,32},{168,40},{16,48},{184,56},{... | collective-permute-start | bytes 1179656 | tf_op jit(solution)/shard_map/ppermute | solution.py:334
  106.7 19.6 %collective-permute-start.14 = (bf16[4,48,1024]{2,1,0:T(8,128)(2,1)}, bf16[4,48,1024]{2,1,0:T(8,128)(2,1)S(1)}, u32[]{:S(2)}, u32[]{:S(2)}) collective-permute-start(bf16[4,48,1024]{2,1,0:T(8,128)(2,1)} %get-tuple-element.53), channel_id=1, source_target_pairs={{40,0},{128,8},{56,16},{144,24},{8,32},{160,40},{24,48},{176,56},{... | collective-permute-start | bytes 1179656 | tf_op jit(solution)/shard_map/ppermute | solution.py:334
  108.5 8.0 %copy-start.29 = (bf16[4,48,1024]{2,1,0:T(8,128)(2,1)S(1)}, bf16[4,48,1024]{2,1,0:T(8,128)(2,1)}, u32[]{:S(2)}) copy-start(bf16[4,48,1024]{2,1,0:T(8,128)(2,1)} %get-tuple-element.54) | copy-start | bytes 1179652
  108.5 13.4 %copy-start.28 = (bf16[4,48,1024]{2,1,0:T(8,128)(2,1)S(1)}, bf16[4,48,1024]{2,1,0:T(8,128)(2,1)}, u32[]{:S(2)}) copy-start(bf16[4,48,1024]{2,1,0:T(8,128)(2,1)} %get-tuple-element.55) | copy-start | bytes 1179652
  116.5 25.7 %copy-start.4 = (bf16[4,48,1024]{2,1,0:T(8,128)(2,1)}, bf16[4,48,1024]{2,1,0:T(8,128)(2,1)S(1)}, u32[]{:S(2)}) copy-start(bf16[4,48,1024]{2,1,0:T(8,128)(2,1)S(1)} %collective-permute-done.10.refs_5_) | copy-start | bytes 1179652
  116.5 9.9 %collective-permute-start.15 = (bf16[4,48,1024]{2,1,0:T(8,128)(2,1)S(1)}, bf16[4,48,1024]{2,1,0:T(8,128)(2,1)S(1)}, u32[]{:S(2)}, u32[]{:S(2)}) collective-permute-start(bf16[4,48,1024]{2,1,0:T(8,128)(2,1)S(1)} %copy-done.29), channel_id=1, source_target_pairs={{48,0},{200,8},{0,16},{216,24},{16,32},{232,40},{32,48},{248,56},{... | collective-permute-start | bytes 1179656 | tf_op jit(solution)/shard_map/ppermute | solution.py:334
  121.9 20.3 %copy-start.6 = (bf16[4,48,1024]{2,1,0:T(8,128)(2,1)}, bf16[4,48,1024]{2,1,0:T(8,128)(2,1)S(1)}, u32[]{:S(2)}) copy-start(bf16[4,48,1024]{2,1,0:T(8,128)(2,1)S(1)} %collective-permute-done.11.refs_6_) | copy-start | bytes 1179652
  121.9 8.8 %collective-permute-start.16 = (bf16[4,48,1024]{2,1,0:T(8,128)(2,1)S(1)}, bf16[4,48,1024]{2,1,0:T(8,128)(2,1)S(1)}, u32[]{:S(2)}, u32[]{:S(2)}) collective-permute-start(bf16[4,48,1024]{2,1,0:T(8,128)(2,1)S(1)} %copy-done.28), channel_id=1, source_target_pairs={{56,0},{192,8},{8,16},{208,24},{24,32},{224,40},{40,48},{240,56},{... | collective-permute-start | bytes 1179656 | tf_op jit(solution)/shard_map/ppermute | solution.py:334
  122.3 19.9 %copy-start.7 = (bf16[4,48,1024]{2,1,0:T(8,128)(2,1)}, bf16[4,48,1024]{2,1,0:T(8,128)(2,1)S(1)}, u32[]{:S(2)}) copy-start(bf16[4,48,1024]{2,1,0:T(8,128)(2,1)S(1)} %collective-permute-done.12.refs_7_) | copy-start | bytes 1179652
  122.3 11.0 %collective-permute-start.20 = (bf16[4,48,1024]{2,1,0:T(8,128)(2,1)}, bf16[4,48,1024]{2,1,0:T(8,128)(2,1)S(1)}, u32[]{:S(2)}, u32[]{:S(2)}) collective-permute-start(bf16[4,48,1024]{2,1,0:T(8,128)(2,1)} %get-tuple-element.62), channel_id=1, source_target_pairs={{8,0},{0,8},{24,16},{16,24},{40,32},{32,40},{56,48},{48,56},{72,64... | collective-permute-start | bytes 1179656 | tf_op jit(solution)/shard_map/ppermute | solution.py:334
  123.0 19.2 %copy-start.9 = (bf16[4,48,1024]{2,1,0:T(8,128)(2,1)}, bf16[4,48,1024]{2,1,0:T(8,128)(2,1)S(1)}, u32[]{:S(2)}) copy-start(bf16[4,48,1024]{2,1,0:T(8,128)(2,1)S(1)} %collective-permute-done.13.refs_8_) | copy-start | bytes 1179652
  123.0 19.2 %collective-permute-start.21 = (bf16[4,48,1024]{2,1,0:T(8,128)(2,1)}, bf16[4,48,1024]{2,1,0:T(8,128)(2,1)S(1)}, u32[]{:S(2)}, u32[]{:S(2)}) collective-permute-start(bf16[4,48,1024]{2,1,0:T(8,128)(2,1)} %get-tuple-element.63), channel_id=1, source_target_pairs={{16,0},{72,8},{32,16},{88,24},{48,32},{104,40},{0,48},{120,56},{80... | collective-permute-start | bytes 1179656 | tf_op jit(solution)/shard_map/ppermute | solution.py:334
  126.3 15.9 %copy-start.10 = (bf16[4,48,1024]{2,1,0:T(8,128)(2,1)}, bf16[4,48,1024]{2,1,0:T(8,128)(2,1)S(1)}, u32[]{:S(2)}) copy-start(bf16[4,48,1024]{2,1,0:T(8,128)(2,1)S(1)} %collective-permute-done.14.refs_9_) | copy-start | bytes 1179652
  126.3 21.3 %collective-permute-start.22 = (bf16[4,48,1024]{2,1,0:T(8,128)(2,1)}, bf16[4,48,1024]{2,1,0:T(8,128)(2,1)S(1)}, u32[]{:S(2)}, u32[]{:S(2)}) collective-permute-start(bf16[4,48,1024]{2,1,0:T(8,128)(2,1)} %get-tuple-element.64), channel_id=1, source_target_pairs={{24,0},{64,8},{40,16},{80,24},{56,32},{96,40},{8,48},{112,56},{88,... | collective-permute-start | bytes 1179656 | tf_op jit(solution)/shard_map/ppermute | solution.py:334
  126.4 15.8 %copy-start.14 = (bf16[4,48,1024]{2,1,0:T(8,128)(2,1)}, bf16[4,48,1024]{2,1,0:T(8,128)(2,1)S(1)}, u32[]{:S(2)}) copy-start(bf16[4,48,1024]{2,1,0:T(8,128)(2,1)S(1)} %collective-permute-done.15.refs_10_) | copy-start | bytes 1179652
  126.4 26.1 %collective-permute-start.23 = (bf16[4,48,1024]{2,1,0:T(8,128)(2,1)}, bf16[4,48,1024]{2,1,0:T(8,128)(2,1)S(1)}, u32[]{:S(2)}, u32[]{:S(2)}) collective-permute-start(bf16[4,48,1024]{2,1,0:T(8,128)(2,1)} %get-tuple-element.65), channel_id=1, source_target_pairs={{32,0},{136,8},{48,16},{152,24},{0,32},{168,40},{16,48},{184,56},{... | collective-permute-start | bytes 1179656 | tf_op jit(solution)/shard_map/ppermute | solution.py:334
  130.7 11.5 %copy-start.16 = (bf16[4,48,1024]{2,1,0:T(8,128)(2,1)}, bf16[4,48,1024]{2,1,0:T(8,128)(2,1)S(1)}, u32[]{:S(2)}) copy-start(bf16[4,48,1024]{2,1,0:T(8,128)(2,1)S(1)} %collective-permute-done.16.refs_11_) | copy-start | bytes 1179652
  130.7 23.8 %collective-permute-start.24 = (bf16[4,48,1024]{2,1,0:T(8,128)(2,1)}, bf16[4,48,1024]{2,1,0:T(8,128)(2,1)S(1)}, u32[]{:S(2)}, u32[]{:S(2)}) collective-permute-start(bf16[4,48,1024]{2,1,0:T(8,128)(2,1)} %get-tuple-element.66), channel_id=1, source_target_pairs={{40,0},{128,8},{56,16},{144,24},{8,32},{160,40},{24,48},{176,56},{... | collective-permute-start | bytes 1179656 | tf_op jit(solution)/shard_map/ppermute | solution.py:334
  133.3 14.3 %copy-start.5 = (bf16[4,48,1024]{2,1,0:T(8,128)(2,1)}, bf16[4,48,1024]{2,1,0:T(8,128)(2,1)S(1)}, u32[]{:S(2)}) copy-start(bf16[4,48,1024]{2,1,0:T(8,128)(2,1)S(1)} %collective-permute-done.20.refs_5_) | copy-start | bytes 1179652
  133.3 21.9 %collective-permute-start.25 = (bf16[4,48,1024]{2,1,0:T(8,128)(2,1)}, bf16[4,48,1024]{2,1,0:T(8,128)(2,1)S(1)}, u32[]{:S(2)}, u32[]{:S(2)}) collective-permute-start(bf16[4,48,1024]{2,1,0:T(8,128)(2,1)} %get-tuple-element.67), channel_id=1, source_target_pairs={{48,0},{200,8},{0,16},{216,24},{16,32},{232,40},{32,48},{248,56},{... | collective-permute-start | bytes 1179656 | tf_op jit(solution)/shard_map/ppermute | solution.py:334
  142.2 5.5 %copy-start.8 = (bf16[4,48,1024]{2,1,0:T(8,128)(2,1)}, bf16[4,48,1024]{2,1,0:T(8,128)(2,1)S(1)}, u32[]{:S(2)}) copy-start(bf16[4,48,1024]{2,1,0:T(8,128)(2,1)S(1)} %collective-permute-done.21.refs_6_) | copy-start | bytes 1179652
  142.2 13.0 %collective-permute-start.26 = (bf16[4,48,1024]{2,1,0:T(8,128)(2,1)}, bf16[4,48,1024]{2,1,0:T(8,128)(2,1)S(1)}, u32[]{:S(2)}, u32[]{:S(2)}) collective-permute-start(bf16[4,48,1024]{2,1,0:T(8,128)(2,1)} %get-tuple-element.68), channel_id=1, source_target_pairs={{56,0},{192,8},{8,16},{208,24},{24,32},{224,40},{40,48},{240,56},{... | collective-permute-start | bytes 1179656 | tf_op jit(solution)/shard_map/ppermute | solution.py:334
  147.6 7.6 %copy-start.11 = (bf16[4,48,1024]{2,1,0:T(8,128)(2,1)}, bf16[4,48,1024]{2,1,0:T(8,128)(2,1)S(1)}, u32[]{:S(2)}) copy-start(bf16[4,48,1024]{2,1,0:T(8,128)(2,1)S(1)} %collective-permute-done.22.refs_7_) | copy-start | bytes 1179652
  147.7 14.6 %collective-permute-start.17 = (bf16[128,1024]{1,0:T(8,128)(2,1)}, bf16[128,1024]{1,0:T(8,128)(2,1)S(1)}, u32[]{:S(2)}, u32[]{:S(2)}) collective-permute-start(bf16[128,1024]{1,0:T(8,128)(2,1)} %get-tuple-element.57), channel_id=1, source_target_pairs={{64,0},{24,8},{80,16},{40,24},{96,32},{56,40},{112,48},{8,56},{128... | collective-permute-start | bytes 786440 | tf_op jit(solution)/shard_map/ppermute | solution.py:356
  152.5 10.4 %collective-permute-start.18 = (bf16[128,1024]{1,0:T(8,128)(2,1)}, bf16[128,1024]{1,0:T(8,128)(2,1)S(1)}, u32[]{:S(2)}, u32[]{:S(2)}) collective-permute-start(bf16[128,1024]{1,0:T(8,128)(2,1)} %get-tuple-element.58), channel_id=1, source_target_pairs={{128,0},{40,8},{144,16},{56,24},{160,32},{8,40},{176,48},{24,56},{... | collective-permute-start | bytes 786440 | tf_op jit(solution)/shard_map/ppermute | solution.py:356
  154.5 8.5 %collective-permute-start.19 = (bf16[128,1024]{1,0:T(8,128)(2,1)}, bf16[128,1024]{1,0:T(8,128)(2,1)S(1)}, u32[]{:S(2)}, u32[]{:S(2)}) collective-permute-start(bf16[128,1024]{1,0:T(8,128)(2,1)} %get-tuple-element.59), channel_id=1, source_target_pairs={{192,0},{56,8},{208,16},{8,24},{224,32},{24,40},{240,48},{40,56},{... | collective-permute-start | bytes 786440 | tf_op jit(solution)/shard_map/ppermute | solution.py:356
  160.3 8.4 %collective-permute-start.27 = (bf16[128,1024]{1,0:T(8,128)(2,1)}, bf16[128,1024]{1,0:T(8,128)(2,1)S(1)}, u32[]{:S(2)}, u32[]{:S(2)}) collective-permute-start(bf16[128,1024]{1,0:T(8,128)(2,1)} %get-tuple-element.70), channel_id=1, source_target_pairs={{64,0},{24,8},{80,16},{40,24},{96,32},{56,40},{112,48},{8,56},{128... | collective-permute-start | bytes 786440 | tf_op jit(solution)/shard_map/ppermute | solution.py:356
  162.3 7.0 %collective-permute-start.28 = (bf16[128,1024]{1,0:T(8,128)(2,1)}, bf16[128,1024]{1,0:T(8,128)(2,1)S(1)}, u32[]{:S(2)}, u32[]{:S(2)}) collective-permute-start(bf16[128,1024]{1,0:T(8,128)(2,1)} %get-tuple-element.71), channel_id=1, source_target_pairs={{128,0},{40,8},{144,16},{56,24},{160,32},{8,40},{176,48},{24,56},{... | collective-permute-start | bytes 786440 | tf_op jit(solution)/shard_map/ppermute | solution.py:356
  162.3 9.8 %collective-permute-start.29 = (bf16[128,1024]{1,0:T(8,128)(2,1)}, bf16[128,1024]{1,0:T(8,128)(2,1)S(1)}, u32[]{:S(2)}, u32[]{:S(2)}) collective-permute-start(bf16[128,1024]{1,0:T(8,128)(2,1)} %get-tuple-element.72), channel_id=1, source_target_pairs={{192,0},{56,8},{208,16},{8,24},{224,32},{24,40},{240,48},{40,56},{... | collective-permute-start | bytes 786440 | tf_op jit(solution)/shard_map/ppermute | solution.py:356
  (14 other events, 24.3 us)
Sparse Core Ops, SparseCore 0:
  10.5 63.5 all-gather.2
  95.0 62.9 reduce-scatter.1

commit v3 on v2

v3 whole, which is shorter than its diff:
```python
import functools
import jax
import jax.numpy as jnp
from jax import lax
from jax.experimental import pallas as pl
from jax.experimental.pallas import tpu as pltpu
from jax.sharding import PartitionSpec as P

BF = jnp.bfloat16
F32 = jnp.float32
CAP = 24
SIDE = 4
CORES = 2
VMEM_LIMIT = 56 << 20


def call(kernel, name, out_shape, grid=None, in_specs=None, out_specs=None, scratch=(), flops=0, nbytes=0):
    full = pl.BlockSpec(memory_space=pltpu.VMEM)
    kwargs = {} if grid is None else {"grid": grid}
    return pl.pallas_call(
        kernel,
        name=name,
        out_shape=out_shape,
        in_specs=in_specs,
        out_specs=full if out_specs is None else out_specs,
        scratch_shapes=scratch,
        compiler_params=pltpu.CompilerParams(vmem_limit_bytes=VMEM_LIMIT),
        cost_estimate=pl.CostEstimate(flops=flops, transcendentals=0, bytes_accessed=nbytes),
        **kwargs,
    )


def split_parts(values, count):
    parts, rest = [], values
    for _ in range(count):
        part = rest.astype(BF).astype(F32)
        rest = rest - part
        parts.append(part)
    return parts


def down_pieces():
    return [(kb * 128 + h * 64, h * 384 + kb * 128) for kb in range(3) for h in range(2)]


def head_kernel(ids_ref, gates_ref, tokens_ref, cot_ref, lift_ref, down_ref, joined_ref, out_ref):
    for e in range(lift_ref.shape[0]):
        joined_ref[e, :128] = lift_ref[e]
        for row, col in down_pieces():
            joined_ref[e, 128:, col : col + 128] = down_ref[e, row : row + 64]
    tok, width = tokens_ref.shape
    out_ref[:tok] = tokens_ref[...]
    out_ref[tok : 2 * tok] = cot_ref[...]
    facts = [ids_ref[...].astype(F32)] + split_parts(gates_ref[...], 3)
    facts = jnp.concatenate(facts + [jnp.zeros((facts[0].shape[0], width - 4 * tok), F32)], axis=1)
    out_ref[2 * tok :] = jnp.concatenate([facts, jnp.zeros_like(facts)], axis=0).astype(BF)


def unbundle(ref, tok):
    facts = ref[ref.shape[0] - 16 :, : 4 * tok].astype(F32)[:8]
    pieces = [facts[:, n * tok : (n + 1) * tok] for n in range(4)]
    return pieces[0], (pieces[1] + pieces[2]) + pieces[3]


def membership(ids, weights, experts):
    top, rows = ids.shape
    expert = lax.broadcasted_iota(jnp.int32, (experts, rows), 0).astype(F32)
    named = jnp.zeros((experts, rows), F32)
    gates = jnp.zeros((experts, rows), F32)
    for k in range(top):
        hit = ids[k : k + 1, :] == expert
        named = jnp.where(hit, 1.0, named)
        gates = jnp.where(hit, weights[k : k + 1, :], gates)
    before = (
        lax.broadcasted_iota(jnp.int32, (rows, rows), 0)
        < lax.broadcasted_iota(jnp.int32, (rows, rows), 1)
    ).astype(F32).astype(BF)
    rank = jnp.dot(named.astype(BF), before, preferred_element_type=F32)
    return jnp.where(named > 0.0, rank, -1.0), gates


def slots(first_ref, fact_ref, count, rank_ref, gate_ref, q):
    tok = rank_ref.shape[2]
    ids, weights = unbundle(fact_ref, tok)
    rank_ref[q], gate_ref[q] = membership(ids, weights, rank_ref.shape[1])
    rank = jnp.concatenate([rank_ref[q, pl.ds(first_ref[p], 2), :] for p in range(count)], axis=0)
    gates = jnp.concatenate([gate_ref[q, pl.ds(first_ref[p], 2), :] for p in range(count)], axis=0)
    slot = lax.broadcasted_iota(jnp.int32, (rank.shape[0], CAP, tok), 1).astype(F32)
    return rank[:, None, :] == slot, gates


def pack_kernel(first_ref, *refs):
    bundles, outs, tables = refs[:SIDE], refs[SIDE:-2], refs[-2:]
    which = pl.program_id(0)
    tok = tables[0].shape[2]
    found = []
    for q, bundle in enumerate(bundles):
        chosen, gates = slots(first_ref, bundle, len(outs), *tables, q)
        pick = jnp.where(chosen, 1.0, 0.0).reshape(-1, tok).astype(BF)
        scale = jnp.sum(jnp.where(chosen, gates[:, None, :], 0.0), axis=2, keepdims=True)
        scale = jnp.where(which == 0, 1.0, scale)
        data = bundle[pl.ds(pl.multiple_of(which * tok, tok), tok), :]
        rows = jnp.dot(pick, data, preferred_element_type=F32)
        found.append(rows.reshape(-1, CAP, rows.shape[-1]) * scale)
    for p, out in enumerate(outs):
        for e in range(2):
            out[0, e] = jnp.concatenate([rows[2 * p + e] for rows in found], axis=0).astype(BF)


def plan_kernel(count, first_ref, *refs):
    facts, pick_ref, tables = refs[:SIDE], refs[-3], refs[-2:]
    tok = tables[0].shape[2]
    for q, fact in enumerate(facts):
        chosen, gates = slots(first_ref, fact, count, *tables, q)
        for i, weight in enumerate((gates, jnp.ones_like(gates))):
            for n, part in enumerate(split_parts(weight, 2)):
                pick = jnp.where(chosen, part[:, None, :], 0.0).reshape(-1, tok)
                pick_ref[i, q, n * tok : (n + 1) * tok] = pick.T.astype(BF)


def combine_kernel(places, pick_ref, *refs):
    chunks, outs = [refs[n] for n in places], refs[-SIDE:]
    for q, out in enumerate(outs):
        rows = jnp.concatenate([chunk[0, q] for chunk in chunks], axis=0)
        tok = out.shape[1]
        parts = jnp.dot(pick_ref[0, q], rows, preferred_element_type=F32)
        out[0] = (parts[:tok] + parts[tok:]).astype(out.dtype)


def final_kernel(sum_ref, own_ref, *refs):
    others, outs, (lift_ref, down_ref) = refs[: SIDE - 1], refs[SIDE - 1 : -2], refs[-2:]
    for e in range(lift_ref.shape[0]):
        lift_ref[e] = sum_ref[e, :128]
        for row, col in down_pieces():
            down_ref[e, row : row + 64] = sum_ref[e, 128:, col : col + 128]
    for which, out in enumerate(outs):
        total = own_ref[which]
        for ref in others:
            total = total + ref[which].astype(F32)
        out[...] = total.astype(BF)


def load_lift(weights_ref):
    return jnp.concatenate([weights_ref[j, 0, :128] for j in range(weights_ref.shape[0])], axis=0)


def load_down(weights_ref):
    return jnp.concatenate(
        [
            jnp.concatenate(
                [weights_ref[j, 0, 128:, col : col + 128] for j in range(weights_ref.shape[0])], axis=1
            )
            for _, col in down_pieces()
        ],
        axis=0,
    )


def store_rows(which, rows, outs, hold_ref):
    expert = pl.program_id(0)

    @pl.when(expert == 0)
    def _():
        hold_ref[which] = rows

    @pl.when(expert == 1)
    def _():
        for p, out in enumerate(outs):
            for q in range(SIDE):
                low = (p * SIDE + q) * CAP
                out[which, q] = jnp.concatenate(
                    [hold_ref[which, low : low + CAP, :], rows[low : low + CAP]], axis=0
                ).astype(BF)


def expert_kernel(count, *refs):
    chunks, weights_ref, outs = refs[:count], refs[count], refs[count + 2 : -2]
    grad_ref, hold_ref = refs[-2:]
    rows = jnp.concatenate([chunk[0, 0] for chunk in chunks], axis=0)
    back = jnp.concatenate([chunk[1, 0] for chunk in chunks], axis=0)
    lift_weights = load_lift(weights_ref)
    hidden = jnp.dot(rows, lift_weights, preferred_element_type=F32)
    ff = hidden.shape[1] // 2
    gate, up = hidden[:, :ff], hidden[:, ff:]
    sig = jax.nn.sigmoid(gate)
    swish = gate * sig
    act = (swish * up).astype(BF)
    down_weights = load_down(weights_ref)
    act_grad = lax.dot_general(back, down_weights, (((1,), (1,)), ((), ())), preferred_element_type=F32)
    slope = sig * (1.0 + gate * (1.0 - sig))
    hid = jnp.concatenate([(act_grad * up * slope).astype(BF), (act_grad * swish).astype(BF)], axis=1)
    first = (((0,), (0,)), ((), ()))
    down = lax.dot_general(act, back, first, preferred_element_type=F32).astype(BF)
    lift = lax.dot_general(rows, hid, first, preferred_element_type=F32).astype(BF)
    for j in range(grad_ref.shape[0]):
        grad_ref[j, 0, :128] = lift[j * 128 : (j + 1) * 128]
        for row, col in down_pieces():
            grad_ref[j, 0, 128:, col : col + 128] = down[row : row + 64, j * 128 : (j + 1) * 128]
    store_rows(0, jnp.dot(act, down_weights, preferred_element_type=F32), outs, hold_ref)
    grad = lax.dot_general(hid, lift_weights, (((1,), (1,)), ((), ())), preferred_element_type=F32)
    store_rows(1, grad, outs, hold_ref)


def shards(tokens, expert_ids, combine_weights, lift_weights, down_weights, cotangent):
    tok, top = expert_ids.shape
    local, slice_rows, lift_width = lift_weights.shape
    ff = down_weights.shape[1]
    width = tokens.shape[1]
    owners = lax.axis_size("expert")
    groups = lax.axis_size("dp")
    experts = local * owners
    filled = owners * CAP
    vm = pl.BlockSpec(memory_space=pltpu.VMEM)
    smem = pl.BlockSpec(memory_space=pltpu.SMEM)

    near = SIDE * CORES
    everyone = range(owners)

    def device(x, y, c):
        return (x % SIDE) * near + (y % SIDE) * CORES + c % CORES

    def share_to(n, step):
        x, y, c = n // near, n // CORES % SIDE, n % CORES
        return device(x + step, y, c) if c == 0 else device(x, y + step, c)

    def send_to(n, step, flip):
        x, y, c = n // near, n // CORES % SIDE, n % CORES
        return device(x, y + step, c + flip) if c == 0 else device(x + step, y, c + flip)

    def permute(x, target):
        return lax.ppermute(x, "expert", [(n, target(n)) for n in everyone])

    def restore(x, target):
        return lax.ppermute(x, "expert", [(target(n), n) for n in everyone])

    hops = [(step, flip) for step in range(SIDE) for flip in range(CORES)]
    count = len(hops)
    shared = [lambda n, q=q: share_to(n, q) for q in range(1, SIDE)]
    sends = [lambda n, hop=hop: send_to(n, *hop) for hop in hops[1:]]
    targets = jnp.asarray([[local * send_to(n, *hop) for hop in hops] for n in everyone], jnp.int32)
    first_expert = targets[lax.axis_index("expert")]

    joined, own = call(
        head_kernel,
        "head",
        [
            jax.ShapeDtypeStruct((local, slice_rows + 64, lift_width), BF),
            jax.ShapeDtypeStruct((2 * tok + 16, width), BF),
        ],
        in_specs=[vm] * 6,
        out_specs=[vm] * 2,
        nbytes=2 << 20,
    )(expert_ids.T, combine_weights.T, tokens, cotangent, lift_weights, down_weights)
    weights = lax.all_gather(joined, "dp")

    bundles = [own] + [permute(own, target) for target in shared]
    chunk_shape = jax.ShapeDtypeStruct((2, local, SIDE * CAP, width), BF)
    pack_flops = 2 * experts * CAP * tok * width
    table_scratch = pltpu.VMEM((SIDE, experts, tok), F32)
    packed = call(
        pack_kernel,
        "pack",
        [chunk_shape] * count,
        grid=(2,),
        in_specs=[smem] + [vm] * SIDE,
        out_specs=[pl.BlockSpec((1, local, SIDE * CAP, width), lambda i: (i, 0, 0, 0))] * count,
        scratch=[table_scratch, table_scratch],
        flops=2 * pack_flops,
        nbytes=16 << 20,
    )(first_expert, *bundles)
    chunks = list(packed[:1]) + [permute(x, target) for x, target in zip(packed[1:], sends)]
    slot_rows = local * count * CAP
    picks = call(
        functools.partial(plan_kernel, count),
        "plan",
        jax.ShapeDtypeStruct((2, SIDE, 2 * tok, slot_rows), BF),
        grid=(1,),
        in_specs=[smem]
        + [pl.BlockSpec((16, width), lambda i: (2 * tok // 16, 0))] * SIDE
        + [pl.BlockSpec(memory_space=pl.ANY)],
        out_specs=pl.BlockSpec((2, SIDE, 2 * tok, slot_rows), lambda i: (0, 0, 0, 0)),
        scratch=[table_scratch, table_scratch],
        nbytes=2 << 20,
    )(first_expert, *bundles, packed[0])

    weight_block = pl.BlockSpec((groups, 1, slice_rows + 64, lift_width), lambda e: (0, e, 0, 0))
    back_shape = jax.ShapeDtypeStruct((2, SIDE, local * CAP, width), BF)
    back_block = pl.BlockSpec((2, SIDE, local * CAP, width), lambda e: (0, 0, 0, 0))
    unit = 2 * local * filled * ff * width
    *returns, weight_grads = call(
        functools.partial(expert_kernel, count),
        "expert",
        [back_shape] * count
        + [jax.ShapeDtypeStruct((groups, local, slice_rows + 64, lift_width), BF)],
        grid=(local,),
        in_specs=[pl.BlockSpec((2, 1, SIDE * CAP, width), lambda e: (0, e, 0, 0))] * count
        + [weight_block, pl.BlockSpec(memory_space=pl.ANY)],
        out_specs=[back_block] * count + [weight_block],
        scratch=[pltpu.VMEM((2, filled, width), F32)],
        flops=9 * unit,
        nbytes=24 << 20,
    )(*chunks, weights, picks)
    summed = lax.psum_scatter(weight_grads, "dp", scatter_dimension=0, tiled=False)
    order = [0] + sorted(range(1, count), key=lambda p: (-hops[p][0] % SIDE, hops[p][1]))
    parts = [restore(returns[p], sends[p - 1]) if p else returns[0] for p in order]
    combining = functools.partial(combine_kernel, [order.index(p) for p in range(count)])
    sum_block = pl.BlockSpec((1, tok, width), lambda i: (i, 0, 0))
    sums = call(
        combining,
        "combine",
        [jax.ShapeDtypeStruct((2, tok, width), F32)] + [jax.ShapeDtypeStruct((2, tok, width), BF)] * (SIDE - 1),
        grid=(2,),
        in_specs=[pl.BlockSpec((1, SIDE, 2 * tok, slot_rows), lambda i: (i, 0, 0, 0))]
        + [pl.BlockSpec((1, SIDE, local * CAP, width), lambda i: (i, 0, 0, 0))] * count,
        out_specs=[sum_block] * SIDE,
        flops=4 * pack_flops,
        nbytes=10 << 20,
    )(picks, *parts)
    sums = list(sums[:1]) + [restore(x, target) for x, target in zip(sums[1:], shared)]
    token_shape = jax.ShapeDtypeStruct((tok, width), BF)
    return call(
        final_kernel,
        "final",
        [
            token_shape,
            token_shape,
            jax.ShapeDtypeStruct(lift_weights.shape, BF),
            jax.ShapeDtypeStruct(down_weights.shape, BF),
        ],
        in_specs=[vm] * (SIDE + 1),
        out_specs=[vm] * 4,
        nbytes=4 << 20,
    )(summed, *sums)


def solution(mesh):
    rows = P(("expert", "dp"), None)
    lift, down = P("expert", "dp", None), P("expert", None, "dp")
    return jax.shard_map(
        shards,
        mesh=mesh,
        in_specs=(rows, rows, rows, lift, down, rows),
        out_specs=(rows, rows, lift, down),
        check_vma=False,
    )
```

time: 185 us -> 175 us (0.946)
  waiting for transfers between devices: 64 us -> 86.3 us
  starting transfers between devices: 44.7 us -> 30.9 us
  Pallas kernels: 51.1 us -> 39.6 us
  local copies, waits for them, and re-layouts: 8.44 us -> 3.73 us
  other arithmetic: 1.85 us -> 0 us
    ppermute x30 -> x20, waiting for transfers between devices: 64 us -> 86.3 us  [the longest x10 44.5 us: restore(): return lax.ppermute(x, 'expert', [(target(n), n) for n in everyone])]
    ppermute x30 -> x20, starting transfers between devices: 44.6 us -> 30.8 us  [the longest x10 15.4 us: restore(): return lax.ppermute(x, 'expert', [(target(n), n) for n in everyone])]
    pallas_call x9 -> x6, Pallas kernels: 51.1 us -> 39.6 us  [the longest x1 19.8 us: shards(): call(functools.partial(expert_kernel, count), 'expert', [back_shape] * co...]
    slice x3 -> x0, local copies, waits for them, and re-layouts: 1.94 us -> none  [the longest x2 1.17 us: shards(): summed[local * slice_rows:].reshape(128, local, ff // 128, 128)]
    transpose x2 -> x0, local copies, waits for them, and re-layouts: 1.92 us -> none  [the longest x1 1.09 us: shards(): down_weights.reshape(local, ff // 128, 128, 128).transpose(2, 0, 1, 3)]
  transfers between devices with their start and end apart: 32 -> 22, of which waited for: 13 -> 13; matrix products, arithmetic and copies ran while one was open for 1% -> 1% of each run, Pallas kernels for 20% -> 8%
where the time goes in v3:
time: 175 us
  waiting for transfers between devices  86.3 us (49%)
  Pallas kernels  39.6 us (23%)
  starting transfers between devices  30.9 us (18%)
  between operations  14.2 us (8%)
  local copies, waits for them, and re-layouts  3.73 us (2%)
    ppermute x10, waiting for transfers between devices, restore(): return lax.ppermute(x, 'expert', [(target(n), n) for n in everyone])  44.5 us
    ppermute x10, waiting for transfers between devices, permute(): return lax.ppermute(x, 'expert', [(n, target(n)) for n in everyone])  41.7 us
    pallas_call x1, Pallas kernels, shards(): call(functools.partial(expert_kernel, count), 'expert', [back_shape] * co...  19.8 us
    ppermute x10, starting transfers between devices, restore(): return lax.ppermute(x, 'expert', [(target(n), n) for n in everyone])  15.4 us
    ppermute x10, starting transfers between devices, permute(): return lax.ppermute(x, 'expert', [(n, target(n)) for n in everyone])  15.4 us
    pallas_call x1, Pallas kernels, shards(): call(pack_kernel, 'pack', [chunk_shape] * count, grid=(2,), in_specs=[sme...  6.42 us
    pallas_call x1, Pallas kernels, shards(): call(combining, 'combine', [jax.ShapeDtypeStruct((2, tok, width), F32)] +...  5.5 us
  transfers between devices with their start and end apart: 22, of which 13 were waited for; matrix products, arithmetic and copies ran while one was open for 1% of the time, Pallas kernels for 8%

profile of v3, /device:TPU:1, one launch (start us, length us, event | category | flops | bytes accessed | tf_op | source)
XLA Modules:
  0.0 174.7 jit_solution(1415850119091910537)
XLA Ops:
  7.2 0.0 all-gather.3.cloned.1.call-start
  7.2 2.3 %head.1 = (bf16[2,192,768]{2,1,0:T(8,128)(2,1)}, bf16[272,1024]{1,0:T(8,128)(2,1)}) custom-call(s32[8,128]{1,0:T(8,128)} %bitcast.7, f32[8,128]{1,0:T(8,128)} %bitcast.8, bf16[128,1024]{1,0:T(8,128)(2,1)} %tokens_ref.1, bf16[128,1024]{1,0:T(8,128)(2,1)} %cot_ref.1, bf16[2,128,768]{2,1,0:T(8,128)(2,1)} %lift_ref.1, bf16[2,384,128]{2,1,0:T(8,128)(2,1)} %down_ref.1), custom_call_target="tpu_custom_call" | custom-call | bytes 2097152 | tf_op jit(solution)/shard_map/head/pallas_call | solution.py:243
  9.5 0.0 all-gather.3.cloned.1.call-update
  9.6 0.0 reduce-scatter.2.cloned.1.call-start
  9.6 3.6 %collective-permute-start.2 = (bf16[272,1024]{1,0:T(8,128)(2,1)}, bf16[272,1024]{1,0:T(8,128)(2,1)S(1)}, u32[]{:S(2)}, u32[]{:S(2)}) collective-permute-start(bf16[272,1024]{1,0:T(8,128)(2,1)} %get-tuple-element.27.refs_0_), channel_id=1, source_target_pairs={{0,192},{8,56},{16,208},{24,8},{32,224},{40,24},{48,240},{56,40},{... | collective-permute-start | bytes 1671176 | tf_op jit(solution)/shard_map/ppermute | solution.py:231
  13.3 0.3 collective-permute-start.1
  13.6 0.7 collective-permute-start
  14.3 1.2 dynamic-slice_bitcast_fusion.first_ref
  15.5 10.5 %collective-permute-done.2.refs_3_ = bf16[272,1024]{1,0:T(8,128)(2,1)S(1)} collective-permute-done((bf16[272,1024]{1,0:T(8,128)(2,1)}, bf16[272,1024]{1,0:T(8,128)(2,1)S(1)}, u32[]{:S(2)}, u32[]{:S(2)}) %collective-permute-start.2) | collective-permute-done | bytes 557088 | tf_op jit(solution)/shard_map/ppermute | solution.py:231
  26.0 3.7 %collective-permute-done.refs_1_ = bf16[272,1024]{1,0:T(8,128)(2,1)S(1)} collective-permute-done((bf16[272,1024]{1,0:T(8,128)(2,1)}, bf16[272,1024]{1,0:T(8,128)(2,1)S(1)}, u32[]{:S(2)}, u32[]{:S(2)}) %collective-permute-start) | collective-permute-done | bytes 557088 | tf_op jit(solution)/shard_map/ppermute | solution.py:231
  29.7 0.8 copy-done.9
  30.6 6.4 %pack.1 = (bf16[2,2,96,1024]{3,2,1,0:T(8,128)(2,1)}, bf16[2,2,96,1024]{3,2,1,0:T(8,128)(2,1)}, bf16[2,2,96,1024]{3,2,1,0:T(8,128)(2,1)}, bf16[2,2,96,1024]{3,2,1...) custom-call(s32[8]{0:T(128)} %dynamic-slice_bitcast_fusion.first_ref, ...), custom_call_target="tpu_custom_call" | custom-call | flops 805306368 | bytes 16777216 | tf_op jit(solution)/shard_map/pack/pallas_call | solution.py:260
  37.0 1.4 collective-permute-start.3
  38.4 0.6 collective-permute-start.5
  39.0 2.6 %collective-permute-start.6 = (bf16[2,2,96,1024]{3,2,1,0:T(8,128)(2,1)}, bf16[2,2,96,1024]{3,2,1,0:T(8,128)(2,1)S(1)}, u32[]{:S(2)}, u32[]{:S(2)}) collective-permute-start(bf16[2,2,96,1024]{3,2,1,0:T(8,128)(2,1)} %get-tuple-element.32), channel_id=1, source_target_pairs={{0,32},{8,136},{16,48},{24,152},{32,0},{40,168},{48,16},{56,184},{... | collective-permute-start | bytes 2359304 | tf_op jit(solution)/shard_map/ppermute | solution.py:231
  41.6 2.9 %collective-permute-start.7 = (bf16[2,2,96,1024]{3,2,1,0:T(8,128)(2,1)}, bf16[2,2,96,1024]{3,2,1,0:T(8,128)(2,1)}, u32[]{:S(2)}, u32[]{:S(2)}) collective-permute-start(bf16[2,2,96,1024]{3,2,1,0:T(8,128)(2,1)} %get-tuple-element.33), channel_id=1, source_target_pairs={{0,40},{8,128},{16,56},{24,144},{32,8},{40,160},{48,24},{56,176},{... | collective-permute-start | bytes 2359304 | tf_op jit(solution)/shard_map/ppermute | solution.py:231
  44.5 1.0 collective-permute-start.8
  45.5 5.6 %collective-permute-done.4.refs_2_ = bf16[2,2,96,1024]{3,2,1,0:T(8,128)(2,1)S(1)} collective-permute-done((bf16[2,2,96,1024]{3,2,1,0:T(8,128)(2,1)}, bf16[2,2,96,1024]{3,2,1,0:T(8,128)(2,1)S(1)}, u32[]{:S(2)}, u32[]{:S(2)}) %collective-permute-start.4) | collective-permute-done | bytes 786464 | tf_op jit(solution)/shard_map/ppermute | solution.py:231
  51.1 2.2 %collective-permute-start.9 = (bf16[2,2,96,1024]{3,2,1,0:T(8,128)(2,1)}, bf16[2,2,96,1024]{3,2,1,0:T(8,128)(2,1)}, u32[]{:S(2)}, u32[]{:S(2)}) collective-permute-start(bf16[2,2,96,1024]{3,2,1,0:T(8,128)(2,1)} %get-tuple-element.35), channel_id=1, source_target_pairs={{0,56},{8,192},{16,8},{24,208},{32,24},{40,224},{48,40},{56,240},{... | collective-permute-start | bytes 2359304 | tf_op jit(solution)/shard_map/ppermute | solution.py:231
  53.3 2.6 %plan.1.refs_9_.pick_ref = bf16[2,4,256,384]{3,2,1,0:T(8,128)(2,1)} custom-call(s32[8]{0:T(128)} %dynamic-slice_bitcast_fusion.first_ref, bf16[272,1024]{1,0:T(8,128)(2,1)} %get-tuple-element.27.refs_0_, bf16[272,1024]{1,0:T(8,128)(2,1)} %copy-done.9, bf16[272,1024]{1,0:T(8,128)(2,1)} %copy-done.8, bf16[272,1024]{1,0:T(8,128)(2,1)} %copy-done.7, ...), custom_call_target="tpu_custom_call" | custom-call | bytes 2097152 | tf_op jit(solution)/shard_map/plan/pallas_call | solution.py:273
  55.9 4.2 %collective-permute-done.5.refs_3_ = bf16[2,2,96,1024]{3,2,1,0:T(8,128)(2,1)S(1)} collective-permute-done((bf16[2,2,96,1024]{3,2,1,0:T(8,128)(2,1)}, bf16[2,2,96,1024]{3,2,1,0:T(8,128)(2,1)S(1)}, u32[]{:S(2)}, u32[]{:S(2)}) %collective-permute-start.5) | collective-permute-done | bytes 786464 | tf_op jit(solution)/shard_map/ppermute | solution.py:231
  60.0 7.5 %collective-permute-done.6.refs_4_ = bf16[2,2,96,1024]{3,2,1,0:T(8,128)(2,1)S(1)} collective-permute-done((bf16[2,2,96,1024]{3,2,1,0:T(8,128)(2,1)}, bf16[2,2,96,1024]{3,2,1,0:T(8,128)(2,1)S(1)}, u32[]{:S(2)}, u32[]{:S(2)}) %collective-permute-start.6) | collective-permute-done | bytes 786464 | tf_op jit(solution)/shard_map/ppermute | solution.py:231
  67.5 10.3 %collective-permute-done.7.refs_5_ = bf16[2,2,96,1024]{3,2,1,0:T(8,128)(2,1)} collective-permute-done((bf16[2,2,96,1024]{3,2,1,0:T(8,128)(2,1)}, bf16[2,2,96,1024]{3,2,1,0:T(8,128)(2,1)}, u32[]{:S(2)}, u32[]{:S(2)}) %collective-permute-start.7) | collective-permute-done | bytes 786464 | tf_op jit(solution)/shard_map/ppermute | solution.py:231
  77.8 0.0 all-gather.3.cloned.1.call-done
  77.9 19.8 %expert.1 = (bf16[2,4,48,1024]{3,2,1,0:T(8,128)(2,1)}, bf16[2,4,48,1024]{3,2,1,0:T(8,128)(2,1)}, bf16[2,4,48,1024]{3,2,1,0:T(8,128)(2,1)}, bf16[2,4,48,1024]{3,2...) custom-call(bf16[2,2,96,1024]{3,2,1,0:T(8,128)(2,1)} %get-tuple-elem, ...), custom_call_target="tpu_custom_call" | custom-call | flops 10871635968 | bytes 25165824 | tf_op jit(solution)/shard_map/expert/pallas_call | solution.py:290
  97.7 0.0 reduce-scatter.2.cloned.1.call-update
  97.7 1.1 collective-permute-start.10
  98.8 0.7 collective-permute-start.11
  99.6 2.7 %collective-permute-start.12 = (bf16[2,4,48,1024]{3,2,1,0:T(8,128)(2,1)}, bf16[2,4,48,1024]{3,2,1,0:T(8,128)(2,1)S(1)}, u32[]{:S(2)}, u32[]{:S(2)}) collective-permute-start(bf16[2,4,48,1024]{3,2,1,0:T(8,128)(2,1)} %get-tuple-element.41), channel_id=1, source_target_pairs={{56,0},{192,8},{8,16},{208,24},{24,32},{224,40},{40,48},{240,56},{... | collective-permute-start | bytes 2359304 | tf_op jit(solution)/shard_map/ppermute | solution.py:234
  102.3 0.6 collective-permute-start.13
  102.9 1.6 collective-permute-start.14
  104.5 2.4 %collective-permute-start.15 = (bf16[2,4,48,1024]{3,2,1,0:T(8,128)(2,1)S(1)}, bf16[2,4,48,1024]{3,2,1,0:T(8,128)(2,1)S(1)}, u32[]{:S(2)}, u32[]{:S(2)}) collective-permute-start(bf16[2,4,48,1024]{3,2,1,0:T(8,128)(2,1)S(1)} %copy-done.17), channel_id=1, source_target_pairs={{16,0},{72,8},{32,16},{88,24},{48,32},{104,40},{0,48},{120,56},{80... | collective-permute-start | bytes 2359304 | tf_op jit(solution)/shard_map/ppermute | solution.py:234
  107.0 10.1 %collective-permute-done.11.refs_2_ = bf16[2,4,48,1024]{3,2,1,0:T(8,128)(2,1)S(1)} collective-permute-done((bf16[2,4,48,1024]{3,2,1,0:T(8,128)(2,1)S(1)}, bf16[2,4,48,1024]{3,2,1,0:T(8,128)(2,1)S(1)}, u32[]{:S(2)}, u32[]{:S(2)}) %collective-permute-start.11) | collective-permute-done | bytes 786464 | tf_op jit(solution)/shard_map/ppermute | solution.py:234
  117.0 3.7 %collective-permute-start.16 = (bf16[2,4,48,1024]{3,2,1,0:T(8,128)(2,1)S(1)}, bf16[2,4,48,1024]{3,2,1,0:T(8,128)(2,1)S(1)}, u32[]{:S(2)}, u32[]{:S(2)}) collective-permute-start(bf16[2,4,48,1024]{3,2,1,0:T(8,128)(2,1)S(1)} %copy-done.15), channel_id=1, source_target_pairs={{24,0},{64,8},{40,16},{80,24},{56,32},{96,40},{8,48},{112,56},{88,... | collective-permute-start | bytes 2359304 | tf_op jit(solution)/shard_map/ppermute | solution.py:234
  120.7 15.9 %collective-permute-done.13.refs_4_ = bf16[2,4,48,1024]{3,2,1,0:T(8,128)(2,1)S(1)} collective-permute-done((bf16[2,4,48,1024]{3,2,1,0:T(8,128)(2,1)}, bf16[2,4,48,1024]{3,2,1,0:T(8,128)(2,1)S(1)}, u32[]{:S(2)}, u32[]{:S(2)}) %collective-permute-start.13) | collective-permute-done | bytes 786464 | tf_op jit(solution)/shard_map/ppermute | solution.py:234
  136.6 0.9 collective-permute-done.14.refs_5_
  137.5 2.4 %collective-permute-done.15.refs_6_ = bf16[2,4,48,1024]{3,2,1,0:T(8,128)(2,1)S(1)} collective-permute-done((bf16[2,4,48,1024]{3,2,1,0:T(8,128)(2,1)S(1)}, bf16[2,4,48,1024]{3,2,1,0:T(8,128)(2,1)S(1)}, u32[]{:S(2)}, u32[]{:S(2)}) %collective-permute-start.15) | collective-permute-done | bytes 786464 | tf_op jit(solution)/shard_map/ppermute | solution.py:234
  139.9 0.6 collective-permute-done.16.refs_7_
  140.5 0.3 copy-done.5
  140.9 0.5 copy-done.6
  141.4 5.5 %combine.1 = (f32[2,128,1024]{2,1,0:T(8,128)}, bf16[2,128,1024]{2,1,0:T(8,128)(2,1)}, bf16[2,128,1024]{2,1,0:T(8,128)(2,1)}, bf16[2,128,1024]{2,1,0:T(8,128)(2,1)}) custom-call(bf16[2,4,256,384]{3,2,1,0:T(8,128)(2,1)} %plan.1.refs_9_.pick_ref, bf16[2,4,48,1024]{3,2,1,0:T(8,128)(2,1)} %get-tuple-element.38.refs_0_, bf16[2,4,48,1024]{3,2,1,0:T(8,128)(2,1)} %copy-done, ...), custom_call_target="tpu_custom_call" | custom-call | flops 1610612736 | bytes 10485760 | tf_op jit(solution)/shard_map/combine/pallas_call | solution.py:308
  146.9 1.8 %collective-permute-start.17 = (bf16[2,128,1024]{2,1,0:T(8,128)(2,1)}, bf16[2,128,1024]{2,1,0:T(8,128)(2,1)S(1)}, u32[]{:S(2)}, u32[]{:S(2)}) collective-permute-start(bf16[2,128,1024]{2,1,0:T(8,128)(2,1)} %get-tuple-element.47), channel_id=1, source_target_pairs={{64,0},{24,8},{80,16},{40,24},{96,32},{56,40},{112,48},{8,56},{128... | collective-permute-start | bytes 1572872 | tf_op jit(solution)/shard_map/ppermute | solution.py:234
  148.6 0.0 collective-permute-start.18
  148.7 0.7 collective-permute-start.19
  149.4 11.4 %collective-permute-done.17.refs_0_ = bf16[2,128,1024]{2,1,0:T(8,128)(2,1)S(1)} collective-permute-done((bf16[2,128,1024]{2,1,0:T(8,128)(2,1)}, bf16[2,128,1024]{2,1,0:T(8,128)(2,1)S(1)}, u32[]{:S(2)}, u32[]{:S(2)}) %collective-permute-start.17) | collective-permute-done | bytes 524320 | tf_op jit(solution)/shard_map/ppermute | solution.py:234
  160.7 3.3 %collective-permute-done.19.refs_2_ = bf16[2,128,1024]{2,1,0:T(8,128)(2,1)S(1)} collective-permute-done((bf16[2,128,1024]{2,1,0:T(8,128)(2,1)}, bf16[2,128,1024]{2,1,0:T(8,128)(2,1)S(1)}, u32[]{:S(2)}, u32[]{:S(2)}) %collective-permute-start.19) | collective-permute-done | bytes 524320 | tf_op jit(solution)/shard_map/ppermute | solution.py:234
  164.1 0.8 copy-done.12
  164.9 3.0 %final.1 = (bf16[128,1024]{1,0:T(8,128)(2,1)}, bf16[128,1024]{1,0:T(8,128)(2,1)}, bf16[2,128,768]{2,1,0:T(8,128)(2,1)}, bf16[2,384,128]{2,1,0:T(8,128)(2,1)}) custom-call(bf16[2,192,768]{2,1,0:T(8,128)(2,1)} %bitcast.6, f32[2,128,1024]{2,1,0:T(8,128)} %get-tuple-element.46.own_ref, bf16[2,128,1024]{2,1,0:T(8,128)(2,1)} %copy-done.10, ...), custom_call_target="tpu_custom_call" | custom-call | bytes 4194304 | tf_op jit(solution)/shard_map/final/pallas_call | solution.py:321
  (47 shorter events, 0.1 us)
Async XLA Ops:
  7.2 70.7 %all-gather.3.cloned.1.call-start = ((), (), s32[]{:S(2)}) async-start(), calls=%async_computation.2 | async-start | bytes 5308416 | tf_op jit(solution)/shard_map/all_gather | solution.py:254
  9.6 154.5 %reduce-scatter.2.cloned.1.call-start = ((), (), s32[]{:S(2)}) async-start(), calls=%async_computation.1 | async-start | bytes 5308416 | tf_op jit(solution)/shard_map/reduce_scatter | solution.py:303
  9.6 16.4 %collective-permute-start.2 = (bf16[272,1024]{1,0:T(8,128)(2,1)}, bf16[272,1024]{1,0:T(8,128)(2,1)S(1)}, u32[]{:S(2)}, u32[]{:S(2)}) collective-permute-start(bf16[272,1024]{1,0:T(8,128)(2,1)} %get-tuple-element.27.refs_0_), channel_id=1, source_target_pairs={{0,192},{8,56},{16,208},{24,8},{32,224},{40,24},{48,240},{56,40},{... | collective-permute-start | bytes 1671176 | tf_op jit(solution)/shard_map/ppermute | solution.py:231
  13.3 12.8 %collective-permute-start.1 = (bf16[272,1024]{1,0:T(8,128)(2,1)}, bf16[272,1024]{1,0:T(8,128)(2,1)S(1)}, u32[]{:S(2)}, u32[]{:S(2)}) collective-permute-start(bf16[272,1024]{1,0:T(8,128)(2,1)} %get-tuple-element.27.refs_0_), channel_id=1, source_target_pairs={{0,128},{8,40},{16,144},{24,56},{32,160},{40,8},{48,176},{56,24},{... | collective-permute-start | bytes 1671176 | tf_op jit(solution)/shard_map/ppermute | solution.py:231
  13.6 16.1 %collective-permute-start = (bf16[272,1024]{1,0:T(8,128)(2,1)}, bf16[272,1024]{1,0:T(8,128)(2,1)S(1)}, u32[]{:S(2)}, u32[]{:S(2)}) collective-permute-start(bf16[272,1024]{1,0:T(8,128)(2,1)} %get-tuple-element.27.refs_0_), channel_id=1, source_target_pairs={{0,64},{8,24},{16,80},{24,40},{32,96},{40,56},{48,112},{56,8},{64,... | collective-permute-start | bytes 1671176 | tf_op jit(solution)/shard_map/ppermute | solution.py:231
  26.0 3.7 %copy-start.7 = (bf16[272,1024]{1,0:T(8,128)(2,1)}, bf16[272,1024]{1,0:T(8,128)(2,1)S(1)}, u32[]{:S(2)}) copy-start(bf16[272,1024]{1,0:T(8,128)(2,1)S(1)} %collective-permute-done.2.refs_3_) | copy-start | bytes 1671172
  26.0 3.7 %copy-start.8 = (bf16[272,1024]{1,0:T(8,128)(2,1)}, bf16[272,1024]{1,0:T(8,128)(2,1)S(1)}, u32[]{:S(2)}) copy-start(bf16[272,1024]{1,0:T(8,128)(2,1)S(1)} %collective-permute-done.1.refs_2_) | copy-start | bytes 1671172
  29.7 0.8 copy-start.9
  37.0 7.5 %collective-permute-start.3 = (bf16[2,2,96,1024]{3,2,1,0:T(8,128)(2,1)}, bf16[2,2,96,1024]{3,2,1,0:T(8,128)(2,1)S(1)}, u32[]{:S(2)}, u32[]{:S(2)}) collective-permute-start(bf16[2,2,96,1024]{3,2,1,0:T(8,128)(2,1)} %get-tuple-element.29), channel_id=1, source_target_pairs={{0,8},{8,0},{16,24},{24,16},{32,40},{40,32},{48,56},{56,48},{64,72... | collective-permute-start | bytes 2359304 | tf_op jit(solution)/shard_map/ppermute | solution.py:231
  38.4 12.7 %collective-permute-start.4 = (bf16[2,2,96,1024]{3,2,1,0:T(8,128)(2,1)}, bf16[2,2,96,1024]{3,2,1,0:T(8,128)(2,1)S(1)}, u32[]{:S(2)}, u32[]{:S(2)}) collective-permute-start(bf16[2,2,96,1024]{3,2,1,0:T(8,128)(2,1)} %get-tuple-element.30), channel_id=1, source_target_pairs={{0,16},{8,72},{16,32},{24,88},{32,48},{40,104},{48,0},{56,120},{64... | collective-permute-start | bytes 2359304 | tf_op jit(solution)/shard_map/ppermute | solution.py:231
  38.4 21.6 %collective-permute-start.5 = (bf16[2,2,96,1024]{3,2,1,0:T(8,128)(2,1)}, bf16[2,2,96,1024]{3,2,1,0:T(8,128)(2,1)S(1)}, u32[]{:S(2)}, u32[]{:S(2)}) collective-permute-start(bf16[2,2,96,1024]{3,2,1,0:T(8,128)(2,1)} %get-tuple-element.31), channel_id=1, source_target_pairs={{0,24},{8,64},{16,40},{24,80},{32,56},{40,96},{48,8},{56,112},{64,... | collective-permute-start | bytes 2359304 | tf_op jit(solution)/shard_map/ppermute | solution.py:231
  39.0 28.5 %collective-permute-start.6 = (bf16[2,2,96,1024]{3,2,1,0:T(8,128)(2,1)}, bf16[2,2,96,1024]{3,2,1,0:T(8,128)(2,1)S(1)}, u32[]{:S(2)}, u32[]{:S(2)}) collective-permute-start(bf16[2,2,96,1024]{3,2,1,0:T(8,128)(2,1)} %get-tuple-element.32), channel_id=1, source_target_pairs={{0,32},{8,136},{16,48},{24,152},{32,0},{40,168},{48,16},{56,184},{... | collective-permute-start | bytes 2359304 | tf_op jit(solution)/shard_map/ppermute | solution.py:231
  41.6 36.2 %collective-permute-start.7 = (bf16[2,2,96,1024]{3,2,1,0:T(8,128)(2,1)}, bf16[2,2,96,1024]{3,2,1,0:T(8,128)(2,1)}, u32[]{:S(2)}, u32[]{:S(2)}) collective-permute-start(bf16[2,2,96,1024]{3,2,1,0:T(8,128)(2,1)} %get-tuple-element.33), channel_id=1, source_target_pairs={{0,40},{8,128},{16,56},{24,144},{32,8},{40,160},{48,24},{56,176},{... | collective-permute-start | bytes 2359304 | tf_op jit(solution)/shard_map/ppermute | solution.py:231
  44.5 33.3 %copy-start.13 = (bf16[2,2,96,1024]{3,2,1,0:T(8,128)(2,1)}, bf16[2,2,96,1024]{3,2,1,0:T(8,128)(2,1)S(1)}, u32[]{:S(2)}) copy-start(bf16[2,2,96,1024]{3,2,1,0:T(8,128)(2,1)S(1)} %collective-permute-done.3.refs_1_) | copy-start | bytes 2359300
  44.5 33.3 %collective-permute-start.8 = (bf16[2,2,96,1024]{3,2,1,0:T(8,128)(2,1)}, bf16[2,2,96,1024]{3,2,1,0:T(8,128)(2,1)}, u32[]{:S(2)}, u32[]{:S(2)}) collective-permute-start(bf16[2,2,96,1024]{3,2,1,0:T(8,128)(2,1)} %get-tuple-element.34), channel_id=1, source_target_pairs={{0,48},{8,200},{16,0},{24,216},{32,16},{40,232},{48,32},{56,248},{... | collective-permute-start | bytes 2359304 | tf_op jit(solution)/shard_map/ppermute | solution.py:231
  51.1 26.8 %copy-start.14 = (bf16[2,2,96,1024]{3,2,1,0:T(8,128)(2,1)}, bf16[2,2,96,1024]{3,2,1,0:T(8,128)(2,1)S(1)}, u32[]{:S(2)}) copy-start(bf16[2,2,96,1024]{3,2,1,0:T(8,128)(2,1)S(1)} %collective-permute-done.4.refs_2_) | copy-start | bytes 2359300
  51.1 26.8 %collective-permute-start.9 = (bf16[2,2,96,1024]{3,2,1,0:T(8,128)(2,1)}, bf16[2,2,96,1024]{3,2,1,0:T(8,128)(2,1)}, u32[]{:S(2)}, u32[]{:S(2)}) collective-permute-start(bf16[2,2,96,1024]{3,2,1,0:T(8,128)(2,1)} %get-tuple-element.35), channel_id=1, source_target_pairs={{0,56},{8,192},{16,8},{24,208},{32,24},{40,224},{48,40},{56,240},{... | collective-permute-start | bytes 2359304 | tf_op jit(solution)/shard_map/ppermute | solution.py:231
  60.0 17.8 %copy-start.16 = (bf16[2,2,96,1024]{3,2,1,0:T(8,128)(2,1)}, bf16[2,2,96,1024]{3,2,1,0:T(8,128)(2,1)S(1)}, u32[]{:S(2)}) copy-start(bf16[2,2,96,1024]{3,2,1,0:T(8,128)(2,1)S(1)} %collective-permute-done.5.refs_3_) | copy-start | bytes 2359300
  67.5 10.4 %copy-start.18 = (bf16[2,2,96,1024]{3,2,1,0:T(8,128)(2,1)}, bf16[2,2,96,1024]{3,2,1,0:T(8,128)(2,1)S(1)}, u32[]{:S(2)}) copy-start(bf16[2,2,96,1024]{3,2,1,0:T(8,128)(2,1)S(1)} %collective-permute-done.6.refs_4_) | copy-start | bytes 2359300
  97.6 1.2 copy-start.20
  97.6 5.2 %copy-start.19 = (bf16[2,4,48,1024]{3,2,1,0:T(8,128)(2,1)S(1)}, bf16[2,4,48,1024]{3,2,1,0:T(8,128)(2,1)}, u32[]{:S(2)}) copy-start(bf16[2,4,48,1024]{3,2,1,0:T(8,128)(2,1)} %get-tuple-element.43) | copy-start | bytes 2359300
  97.7 6.9 %copy-start.17 = (bf16[2,4,48,1024]{3,2,1,0:T(8,128)(2,1)S(1)}, bf16[2,4,48,1024]{3,2,1,0:T(8,128)(2,1)}, u32[]{:S(2)}) copy-start(bf16[2,4,48,1024]{3,2,1,0:T(8,128)(2,1)} %get-tuple-element.44) | copy-start | bytes 2359300
  97.7 19.4 %copy-start.15 = (bf16[2,4,48,1024]{3,2,1,0:T(8,128)(2,1)S(1)}, bf16[2,4,48,1024]{3,2,1,0:T(8,128)(2,1)}, u32[]{:S(2)}) copy-start(bf16[2,4,48,1024]{3,2,1,0:T(8,128)(2,1)} %get-tuple-element.45) | copy-start | bytes 2359300
  97.7 6.8 %collective-permute-start.10 = (bf16[2,4,48,1024]{3,2,1,0:T(8,128)(2,1)}, bf16[2,4,48,1024]{3,2,1,0:T(8,128)(2,1)S(1)}, u32[]{:S(2)}, u32[]{:S(2)}) collective-permute-start(bf16[2,4,48,1024]{3,2,1,0:T(8,128)(2,1)} %get-tuple-element.39), channel_id=1, source_target_pairs={{8,0},{0,8},{24,16},{16,24},{40,32},{32,40},{56,48},{48,56},{72,64... | collective-permute-start | bytes 2359304 | tf_op jit(solution)/shard_map/ppermute | solution.py:234
  98.8 18.2 %collective-permute-start.11 = (bf16[2,4,48,1024]{3,2,1,0:T(8,128)(2,1)S(1)}, bf16[2,4,48,1024]{3,2,1,0:T(8,128)(2,1)S(1)}, u32[]{:S(2)}, u32[]{:S(2)}) collective-permute-start(bf16[2,4,48,1024]{3,2,1,0:T(8,128)(2,1)S(1)} %copy-done.20), channel_id=1, source_target_pairs={{48,0},{200,8},{0,16},{216,24},{16,32},{232,40},{32,48},{248,56},{... | collective-permute-start | bytes 2359304 | tf_op jit(solution)/shard_map/ppermute | solution.py:234
  99.6 21.2 %collective-permute-start.12 = (bf16[2,4,48,1024]{3,2,1,0:T(8,128)(2,1)}, bf16[2,4,48,1024]{3,2,1,0:T(8,128)(2,1)S(1)}, u32[]{:S(2)}, u32[]{:S(2)}) collective-permute-start(bf16[2,4,48,1024]{3,2,1,0:T(8,128)(2,1)} %get-tuple-element.41), channel_id=1, source_target_pairs={{56,0},{192,8},{8,16},{208,24},{24,32},{224,40},{40,48},{240,56},{... | collective-permute-start | bytes 2359304 | tf_op jit(solution)/shard_map/ppermute | solution.py:234
  102.3 34.4 %collective-permute-start.13 = (bf16[2,4,48,1024]{3,2,1,0:T(8,128)(2,1)}, bf16[2,4,48,1024]{3,2,1,0:T(8,128)(2,1)S(1)}, u32[]{:S(2)}, u32[]{:S(2)}) collective-permute-start(bf16[2,4,48,1024]{3,2,1,0:T(8,128)(2,1)} %get-tuple-element.42), channel_id=1, source_target_pairs={{32,0},{136,8},{48,16},{152,24},{0,32},{168,40},{16,48},{184,56},{... | collective-permute-start | bytes 2359304 | tf_op jit(solution)/shard_map/ppermute | solution.py:234
  102.9 34.7 %collective-permute-start.14 = (bf16[2,4,48,1024]{3,2,1,0:T(8,128)(2,1)S(1)}, bf16[2,4,48,1024]{3,2,1,0:T(8,128)(2,1)S(1)}, u32[]{:S(2)}, u32[]{:S(2)}) collective-permute-start(bf16[2,4,48,1024]{3,2,1,0:T(8,128)(2,1)S(1)} %copy-done.19), channel_id=1, source_target_pairs={{40,0},{128,8},{56,16},{144,24},{8,32},{160,40},{24,48},{176,56},{... | collective-permute-start | bytes 2359304 | tf_op jit(solution)/shard_map/ppermute | solution.py:234
  104.5 36.0 %copy-start = (bf16[2,4,48,1024]{3,2,1,0:T(8,128)(2,1)}, bf16[2,4,48,1024]{3,2,1,0:T(8,128)(2,1)S(1)}, u32[]{:S(2)}) copy-start(bf16[2,4,48,1024]{3,2,1,0:T(8,128)(2,1)S(1)} %collective-permute-done.10.refs_1_) | copy-start | bytes 2359300
  104.5 35.4 %collective-permute-start.15 = (bf16[2,4,48,1024]{3,2,1,0:T(8,128)(2,1)S(1)}, bf16[2,4,48,1024]{3,2,1,0:T(8,128)(2,1)S(1)}, u32[]{:S(2)}, u32[]{:S(2)}) collective-permute-start(bf16[2,4,48,1024]{3,2,1,0:T(8,128)(2,1)S(1)} %copy-done.17), channel_id=1, source_target_pairs={{16,0},{72,8},{32,16},{88,24},{48,32},{104,40},{0,48},{120,56},{80... | collective-permute-start | bytes 2359304 | tf_op jit(solution)/shard_map/ppermute | solution.py:234
  117.0 23.5 %copy-start.1 = (bf16[2,4,48,1024]{3,2,1,0:T(8,128)(2,1)}, bf16[2,4,48,1024]{3,2,1,0:T(8,128)(2,1)S(1)}, u32[]{:S(2)}) copy-start(bf16[2,4,48,1024]{3,2,1,0:T(8,128)(2,1)S(1)} %collective-permute-done.11.refs_2_) | copy-start | bytes 2359300
  117.0 23.5 %collective-permute-start.16 = (bf16[2,4,48,1024]{3,2,1,0:T(8,128)(2,1)S(1)}, bf16[2,4,48,1024]{3,2,1,0:T(8,128)(2,1)S(1)}, u32[]{:S(2)}, u32[]{:S(2)}) collective-permute-start(bf16[2,4,48,1024]{3,2,1,0:T(8,128)(2,1)S(1)} %copy-done.15), channel_id=1, source_target_pairs={{24,0},{64,8},{40,16},{80,24},{56,32},{96,40},{8,48},{112,56},{88,... | collective-permute-start | bytes 2359304 | tf_op jit(solution)/shard_map/ppermute | solution.py:234
  120.7 19.8 %copy-start.2 = (bf16[2,4,48,1024]{3,2,1,0:T(8,128)(2,1)}, bf16[2,4,48,1024]{3,2,1,0:T(8,128)(2,1)S(1)}, u32[]{:S(2)}) copy-start(bf16[2,4,48,1024]{3,2,1,0:T(8,128)(2,1)S(1)} %collective-permute-done.12.refs_3_) | copy-start | bytes 2359300
  136.6 3.9 %copy-start.3 = (bf16[2,4,48,1024]{3,2,1,0:T(8,128)(2,1)}, bf16[2,4,48,1024]{3,2,1,0:T(8,128)(2,1)S(1)}, u32[]{:S(2)}) copy-start(bf16[2,4,48,1024]{3,2,1,0:T(8,128)(2,1)S(1)} %collective-permute-done.13.refs_4_) | copy-start | bytes 2359300
  137.5 3.0 %copy-start.4 = (bf16[2,4,48,1024]{3,2,1,0:T(8,128)(2,1)}, bf16[2,4,48,1024]{3,2,1,0:T(8,128)(2,1)S(1)}, u32[]{:S(2)}) copy-start(bf16[2,4,48,1024]{3,2,1,0:T(8,128)(2,1)S(1)} %collective-permute-done.14.refs_5_) | copy-start | bytes 2359300
  139.9 1.0 copy-start.5
  140.5 0.9 copy-start.6
  146.9 13.9 %collective-permute-start.17 = (bf16[2,128,1024]{2,1,0:T(8,128)(2,1)}, bf16[2,128,1024]{2,1,0:T(8,128)(2,1)S(1)}, u32[]{:S(2)}, u32[]{:S(2)}) collective-permute-start(bf16[2,128,1024]{2,1,0:T(8,128)(2,1)} %get-tuple-element.47), channel_id=1, source_target_pairs={{64,0},{24,8},{80,16},{40,24},{96,32},{56,40},{112,48},{8,56},{128... | collective-permute-start | bytes 1572872 | tf_op jit(solution)/shard_map/ppermute | solution.py:234
  148.6 12.1 %collective-permute-start.18 = (bf16[2,128,1024]{2,1,0:T(8,128)(2,1)}, bf16[2,128,1024]{2,1,0:T(8,128)(2,1)S(1)}, u32[]{:S(2)}, u32[]{:S(2)}) collective-permute-start(bf16[2,128,1024]{2,1,0:T(8,128)(2,1)} %get-tuple-element.48), channel_id=1, source_target_pairs={{128,0},{40,8},{144,16},{56,24},{160,32},{8,40},{176,48},{24,56},{... | collective-permute-start | bytes 1572872 | tf_op jit(solution)/shard_map/ppermute | solution.py:234
  148.7 15.4 %collective-permute-start.19 = (bf16[2,128,1024]{2,1,0:T(8,128)(2,1)}, bf16[2,128,1024]{2,1,0:T(8,128)(2,1)S(1)}, u32[]{:S(2)}, u32[]{:S(2)}) collective-permute-start(bf16[2,128,1024]{2,1,0:T(8,128)(2,1)} %get-tuple-element.49), channel_id=1, source_target_pairs={{192,0},{56,8},{208,16},{8,24},{224,32},{24,40},{240,48},{40,56},{... | collective-permute-start | bytes 1572872 | tf_op jit(solution)/shard_map/ppermute | solution.py:234
  160.7 3.3 %copy-start.10 = (bf16[2,128,1024]{2,1,0:T(8,128)(2,1)}, bf16[2,128,1024]{2,1,0:T(8,128)(2,1)S(1)}, u32[]{:S(2)}) copy-start(bf16[2,128,1024]{2,1,0:T(8,128)(2,1)S(1)} %collective-permute-done.17.refs_0_) | copy-start | bytes 1572868
  160.7 3.3 %copy-start.11 = (bf16[2,128,1024]{2,1,0:T(8,128)(2,1)}, bf16[2,128,1024]{2,1,0:T(8,128)(2,1)S(1)}, u32[]{:S(2)}) copy-start(bf16[2,128,1024]{2,1,0:T(8,128)(2,1)S(1)} %collective-permute-done.18.refs_1_) | copy-start | bytes 1572868
  164.1 0.8 copy-start.12
Sparse Core Ops, SparseCore 0:
  9.8 63.5 all-gather.2
  97.8 62.9 reduce-scatter.1

commit v4 on v3

--- a/solution.py
+++ b/solution.py
@@ -11,10 +11,9 @@
 CAP = 24
 SIDE = 4
 CORES = 2
-VMEM_LIMIT = 56 << 20
-
-
-def call(kernel, name, out_shape, grid=None, in_specs=None, out_specs=None, scratch=(), flops=0, nbytes=0):
+
+
+def call(kernel, name, out_shape, grid=None, in_specs=None, out_specs=None, scratch=(), flops=0, nbytes=0, vmem=16):
     full = pl.BlockSpec(memory_space=pltpu.VMEM)
     kwargs = {} if grid is None else {"grid": grid}
     return pl.pallas_call(
@@ -24,7 +23,7 @@
         in_specs=in_specs,
         out_specs=full if out_specs is None else out_specs,
         scratch_shapes=scratch,
-        compiler_params=pltpu.CompilerParams(vmem_limit_bytes=VMEM_LIMIT),
+        compiler_params=pltpu.CompilerParams(vmem_limit_bytes=vmem << 20),
         cost_estimate=pl.CostEstimate(flops=flops, transcendentals=0, bytes_accessed=nbytes),
         **kwargs,
     )
@@ -91,20 +90,20 @@
 
 def pack_kernel(first_ref, *refs):
     bundles, outs, tables = refs[:SIDE], refs[SIDE:-2], refs[-2:]
-    which = pl.program_id(0)
     tok = tables[0].shape[2]
-    found = []
+    sent, back = [], []
     for q, bundle in enumerate(bundles):
         chosen, gates = slots(first_ref, bundle, len(outs), *tables, q)
         pick = jnp.where(chosen, 1.0, 0.0).reshape(-1, tok).astype(BF)
         scale = jnp.sum(jnp.where(chosen, gates[:, None, :], 0.0), axis=2, keepdims=True)
-        scale = jnp.where(which == 0, 1.0, scale)
-        data = bundle[pl.ds(pl.multiple_of(which * tok, tok), tok), :]
-        rows = jnp.dot(pick, data, preferred_element_type=F32)
-        found.append(rows.reshape(-1, CAP, rows.shape[-1]) * scale)
+        rows = jnp.dot(pick, bundle[:tok], preferred_element_type=F32)
+        sent.append(rows.reshape(-1, CAP, rows.shape[-1]))
+        rows = jnp.dot(pick, bundle[tok : 2 * tok], preferred_element_type=F32)
+        back.append(rows.reshape(-1, CAP, rows.shape[-1]) * scale)
     for p, out in enumerate(outs):
-        for e in range(2):
-            out[0, e] = jnp.concatenate([rows[2 * p + e] for rows in found], axis=0).astype(BF)
+        for which, found in enumerate((sent, back)):
+            for e in range(2):
+                out[which, e] = jnp.concatenate([rows[2 * p + e] for rows in found], axis=0).astype(BF)
 
 
 def plan_kernel(count, first_ref, *refs):
@@ -156,26 +155,16 @@
     )
 
 
-def store_rows(which, rows, outs, hold_ref):
-    expert = pl.program_id(0)
-
-    @pl.when(expert == 0)
-    def _():
-        hold_ref[which] = rows
-
-    @pl.when(expert == 1)
-    def _():
-        for p, out in enumerate(outs):
-            for q in range(SIDE):
-                low = (p * SIDE + q) * CAP
-                out[which, q] = jnp.concatenate(
-                    [hold_ref[which, low : low + CAP, :], rows[low : low + CAP]], axis=0
-                ).astype(BF)
+def store_rows(which, rows, outs):
+    for p, out in enumerate(outs):
+        for q in range(SIDE):
+            low = (p * SIDE + q) * CAP
+            out[which, q, 0] = rows[low : low + CAP].astype(BF)
 
 
 def expert_kernel(count, *refs):
-    chunks, weights_ref, outs = refs[:count], refs[count], refs[count + 2 : -2]
-    grad_ref, hold_ref = refs[-2:]
+    chunks, weights_ref, outs = refs[:count], refs[count], refs[count + 2 : -1]
+    grad_ref = refs[-1]
     rows = jnp.concatenate([chunk[0, 0] for chunk in chunks], axis=0)
     back = jnp.concatenate([chunk[1, 0] for chunk in chunks], axis=0)
     lift_weights = load_lift(weights_ref)
@@ -196,9 +185,9 @@
         grad_ref[j, 0, :128] = lift[j * 128 : (j + 1) * 128]
         for row, col in down_pieces():
             grad_ref[j, 0, 128:, col : col + 128] = down[row : row + 64, j * 128 : (j + 1) * 128]
-    store_rows(0, jnp.dot(act, down_weights, preferred_element_type=F32), outs, hold_ref)
+    store_rows(0, jnp.dot(act, down_weights, preferred_element_type=F32), outs)
     grad = lax.dot_general(hid, lift_weights, (((1,), (1,)), ((), ())), preferred_element_type=F32)
-    store_rows(1, grad, outs, hold_ref)
+    store_rows(1, grad, outs)
 
 
 def shards(tokens, expert_ids, combine_weights, lift_weights, down_weights, cotangent):
@@ -230,6 +219,9 @@
     def permute(x, target):
         return lax.ppermute(x, "expert", [(n, target(n)) for n in everyone])
 
+    def onchip(x):
+        return pltpu.with_memory_space_constraint(x, pltpu.VMEM)
+
     def restore(x, target):
         return lax.ppermute(x, "expert", [(target(n), n) for n in everyone])
 
@@ -250,6 +242,7 @@
         in_specs=[vm] * 6,
         out_specs=[vm] * 2,
         nbytes=2 << 20,
+        vmem=56,
     )(expert_ids.T, combine_weights.T, tokens, cotangent, lift_weights, down_weights)
     weights = lax.all_gather(joined, "dp")
 
@@ -260,14 +253,14 @@
     packed = call(
         pack_kernel,
         "pack",
-        [chunk_shape] * count,
-        grid=(2,),
+        [pltpu.VMEM(chunk_shape.shape, BF)] * count,
         in_specs=[smem] + [vm] * SIDE,
-        out_specs=[pl.BlockSpec((1, local, SIDE * CAP, width), lambda i: (i, 0, 0, 0))] * count,
+        out_specs=[vm] * count,
         scratch=[table_scratch, table_scratch],
         flops=2 * pack_flops,
+        vmem=32,
         nbytes=16 << 20,
-    )(first_expert, *bundles)
+    )(first_expert, *[onchip(x) for x in bundles])
     chunks = list(packed[:1]) + [permute(x, target) for x, target in zip(packed[1:], sends)]
     slot_rows = local * count * CAP
     picks = call(
@@ -284,8 +277,8 @@
     )(first_expert, *bundles, packed[0])
 
     weight_block = pl.BlockSpec((groups, 1, slice_rows + 64, lift_width), lambda e: (0, e, 0, 0))
-    back_shape = jax.ShapeDtypeStruct((2, SIDE, local * CAP, width), BF)
-    back_block = pl.BlockSpec((2, SIDE, local * CAP, width), lambda e: (0, 0, 0, 0))
+    back_shape = jax.ShapeDtypeStruct((2, SIDE, local, CAP, width), BF)
+    back_block = pl.BlockSpec((2, SIDE, 1, CAP, width), lambda e: (0, 0, e, 0, 0))
     unit = 2 * local * filled * ff * width
     *returns, weight_grads = call(
         functools.partial(expert_kernel, count),
@@ -296,11 +289,12 @@
         in_specs=[pl.BlockSpec((2, 1, SIDE * CAP, width), lambda e: (0, e, 0, 0))] * count
         + [weight_block, pl.BlockSpec(memory_space=pl.ANY)],
         out_specs=[back_block] * count + [weight_block],
-        scratch=[pltpu.VMEM((2, filled, width), F32)],
         flops=9 * unit,
+        vmem=56,
         nbytes=24 << 20,
     )(*chunks, weights, picks)
     summed = lax.psum_scatter(weight_grads, "dp", scatter_dimension=0, tiled=False)
+    returns = [x.reshape(2, SIDE, local * CAP, width) for x in returns]
     order = [0] + sorted(range(1, count), key=lambda p: (-hops[p][0] % SIDE, hops[p][1]))
     parts = [restore(returns[p], sends[p - 1]) if p else returns[0] for p in order]
     combining = functools.partial(combine_kernel, [order.index(p) for p in range(count)])

time: 175 us -> 164 us (0.937)
  Pallas kernels: 39.6 us -> 27.5 us
  starting transfers between devices: 30.9 us -> 26.8 us
  waiting for transfers between devices: 86.3 us -> 89.9 us
  local copies, waits for them, and re-layouts: 3.73 us -> 5.75 us
    ppermute x10, starting transfers between devices: 15.4 us -> 11.3 us  [restore(): return lax.ppermute(x, 'expert', [(target(n), n) for n in everyone])]
    pallas_call x1, Pallas kernels: 6.42 us -> 2.92 us  [shards(): call(pack_kernel, 'pack', [pltpu.VMEM(chunk_shape.shape, BF)] * count, in...]
    pallas_call x1, Pallas kernels: 5.5 us -> 2.52 us  [shards(): call(combining, 'combine', [jax.ShapeDtypeStruct((2, tok, width), F32)] +...]
    unnamed x42 -> x26, local copies, waits for them, and re-layouts: 2.53 us -> 5.06 us
    pallas_call x1, Pallas kernels: 19.8 us -> 17.4 us  [shards(): call(functools.partial(expert_kernel, count), 'expert', [back_shape] * co...]
    pallas_call x1, Pallas kernels: 2.98 us -> 1.17 us  [shards(): call(final_kernel, 'final', [token_shape, token_shape, jax.ShapeDtypeStru...]
    ppermute x10, waiting for transfers between devices: 44.5 us -> 46.3 us  [restore(): return lax.ppermute(x, 'expert', [(target(n), n) for n in everyone])]
  transfers between devices with their start and end apart: 22 -> 22, of which waited for: 13 -> 15; matrix products, arithmetic and copies ran while one was open for 1% -> 0% of each run, Pallas kernels for 8% -> 4%
where the time goes in v4:
time: 164 us
  waiting for transfers between devices  89.9 us (55%)
  Pallas kernels  27.5 us (17%)
  starting transfers between devices  26.8 us (16%)
  between operations  14.2 us (9%)
  local copies, waits for them, and re-layouts  5.75 us (4%)
    ppermute x10, waiting for transfers between devices, restore(): return lax.ppermute(x, 'expert', [(target(n), n) for n in everyone])  46.3 us
    ppermute x10, waiting for transfers between devices, permute(): return lax.ppermute(x, 'expert', [(n, target(n)) for n in everyone])  42.3 us
    pallas_call x1, Pallas kernels, shards(): call(functools.partial(expert_kernel, count), 'expert', [back_shape] * co...  17.4 us
    ppermute x10, starting transfers between devices, permute(): return lax.ppermute(x, 'expert', [(n, target(n)) for n in everyone])  15.5 us
    ppermute x10, starting transfers between devices, restore(): return lax.ppermute(x, 'expert', [(target(n), n) for n in everyone])  11.3 us
    unnamed x26, local copies, waits for them, and re-layouts  5.06 us
  transfers between devices with their start and end apart: 22, of which 15 were waited for; matrix products, arithmetic and copies ran while one was open for 0% of the time, Pallas kernels for 4%

profile of v4, /device:TPU:1, one launch (start us, length us, event | category | flops | bytes accessed | tf_op | source)
XLA Modules:
  0.0 164.1 jit_solution(17707681824030322131)
XLA Ops:
  7.2 0.0 all-gather.3.cloned.1.call-start
  7.2 2.3 %head.1 = (bf16[2,192,768]{2,1,0:T(8,128)(2,1)}, bf16[272,1024]{1,0:T(8,128)(2,1)}) custom-call(s32[8,128]{1,0:T(8,128)} %bitcast.16, f32[8,128]{1,0:T(8,128)} %bitcast.17, bf16[128,1024]{1,0:T(8,128)(2,1)} %tokens_ref.1, bf16[128,1024]{1,0:T(8,128)(2,1)} %cot_ref.1, bf16[2,128,768]{2,1,0:T(8,128)(2,1)} %lift_ref.1, bf16[2,384,128]{2,1,0:T(8,128)(2,1)} %down_ref.1), custom_call_target="tpu_custom_call" | custom-call | bytes 2097152 | tf_op jit(solution)/shard_map/head/pallas_call | solution.py:235
  9.6 0.0 reduce-scatter.2.cloned.1.call-start
  9.6 3.6 %collective-permute-start.2 = (bf16[272,1024]{1,0:T(8,128)(2,1)}, bf16[272,1024]{1,0:T(8,128)(2,1)S(1)}, u32[]{:S(2)}, u32[]{:S(2)}) collective-permute-start(bf16[272,1024]{1,0:T(8,128)(2,1)} %get-tuple-element.27.refs_0_), channel_id=1, source_target_pairs={{0,192},{8,56},{16,208},{24,8},{32,224},{40,24},{48,240},{56,40},{... | collective-permute-start | bytes 1671176 | tf_op jit(solution)/shard_map/ppermute | solution.py:220
  13.3 0.3 collective-permute-start.1
  13.6 0.7 collective-permute-start
  14.3 0.7 dynamic-slice_bitcast_fusion.first_ref
  15.0 11.0 %collective-permute-done.2.refs_3_ = bf16[272,1024]{1,0:T(8,128)(2,1)S(1)} collective-permute-done((bf16[272,1024]{1,0:T(8,128)(2,1)}, bf16[272,1024]{1,0:T(8,128)(2,1)S(1)}, u32[]{:S(2)}, u32[]{:S(2)}) %collective-permute-start.2) | collective-permute-done | bytes 557088 | tf_op jit(solution)/shard_map/ppermute | solution.py:220
  26.0 3.7 %collective-permute-done.refs_1_ = bf16[272,1024]{1,0:T(8,128)(2,1)S(1)} collective-permute-done((bf16[272,1024]{1,0:T(8,128)(2,1)}, bf16[272,1024]{1,0:T(8,128)(2,1)S(1)}, u32[]{:S(2)}, u32[]{:S(2)}) %collective-permute-start) | collective-permute-done | bytes 557088 | tf_op jit(solution)/shard_map/ppermute | solution.py:220
  29.7 1.1 copy-done.5
  30.8 2.9 %pack.1 = (bf16[2,2,96,1024]{3,2,1,0:T(8,128)(2,1)S(1)}, bf16[2,2,96,1024]{3,2,1,0:T(8,128)(2,1)S(1)}, bf16[2,2,96,1024]{3,2,1,0:T(8,128)(2,1)S(1)}, bf16[2,2,96...) custom-call(s32[8]{0:T(128)S(1)} %dynamic-slice_bitcast_fusion.first, ...), custom_call_target="tpu_custom_call" | custom-call | flops 805306368 | bytes 16777216 | tf_op jit(solution)/shard_map/pack/pallas_call | solution.py:253
  33.7 1.5 collective-permute-start.3
  35.3 0.6 collective-permute-start.5
  35.9 2.5 %collective-permute-start.6 = (bf16[2,2,96,1024]{3,2,1,0:T(8,128)(2,1)S(1)}, bf16[2,2,96,1024]{3,2,1,0:T(8,128)(2,1)S(1)}, u32[]{:S(2)}, u32[]{:S(2)}) collective-permute-start(bf16[2,2,96,1024]{3,2,1,0:T(8,128)(2,1)S(1)} %get-tuple-element.32), channel_id=1, source_target_pairs={{0,32},{8,136},{16,48},{24,152},{32,0},{40,168},{48,16},{56,184},{... | collective-permute-start | bytes 2359304 | tf_op jit(solution)/shard_map/ppermute | solution.py:220
  38.3 2.9 %collective-permute-start.7 = (bf16[2,2,96,1024]{3,2,1,0:T(8,128)(2,1)S(1)}, bf16[2,2,96,1024]{3,2,1,0:T(8,128)(2,1)S(1)}, u32[]{:S(2)}, u32[]{:S(2)}) collective-permute-start(bf16[2,2,96,1024]{3,2,1,0:T(8,128)(2,1)S(1)} %get-tuple-element.33), channel_id=1, source_target_pairs={{0,40},{8,128},{16,56},{24,144},{32,8},{40,160},{48,24},{56,176},{... | collective-permute-start | bytes 2359304 | tf_op jit(solution)/shard_map/ppermute | solution.py:220
  41.3 1.1 collective-permute-start.8
  42.4 5.4 %collective-permute-done.4.refs_2_ = bf16[2,2,96,1024]{3,2,1,0:T(8,128)(2,1)S(1)} collective-permute-done((bf16[2,2,96,1024]{3,2,1,0:T(8,128)(2,1)S(1)}, bf16[2,2,96,1024]{3,2,1,0:T(8,128)(2,1)S(1)}, u32[]{:S(2)}, u32[]{:S(2)}) %collective-permute-start.4) | collective-permute-done | bytes 786464 | tf_op jit(solution)/shard_map/ppermute | solution.py:220
  47.7 2.2 %collective-permute-start.9 = (bf16[2,2,96,1024]{3,2,1,0:T(8,128)(2,1)S(1)}, bf16[2,2,96,1024]{3,2,1,0:T(8,128)(2,1)}, u32[]{:S(2)}, u32[]{:S(2)}) collective-permute-start(bf16[2,2,96,1024]{3,2,1,0:T(8,128)(2,1)S(1)} %get-tuple-element.35), channel_id=1, source_target_pairs={{0,56},{8,192},{16,8},{24,208},{32,24},{40,224},{48,40},{56,240},{... | collective-permute-start | bytes 2359304 | tf_op jit(solution)/shard_map/ppermute | solution.py:220
  49.9 1.2 plan.1.refs_9_.pick_ref
  51.1 1.1 copy-done
  52.2 4.5 %collective-permute-done.5.refs_3_ = bf16[2,2,96,1024]{3,2,1,0:T(8,128)(2,1)S(1)} collective-permute-done((bf16[2,2,96,1024]{3,2,1,0:T(8,128)(2,1)S(1)}, bf16[2,2,96,1024]{3,2,1,0:T(8,128)(2,1)S(1)}, u32[]{:S(2)}, u32[]{:S(2)}) %collective-permute-start.5) | collective-permute-done | bytes 786464 | tf_op jit(solution)/shard_map/ppermute | solution.py:220
  56.7 7.4 %collective-permute-done.6.refs_4_ = bf16[2,2,96,1024]{3,2,1,0:T(8,128)(2,1)S(1)} collective-permute-done((bf16[2,2,96,1024]{3,2,1,0:T(8,128)(2,1)S(1)}, bf16[2,2,96,1024]{3,2,1,0:T(8,128)(2,1)S(1)}, u32[]{:S(2)}, u32[]{:S(2)}) %collective-permute-start.6) | collective-permute-done | bytes 786464 | tf_op jit(solution)/shard_map/ppermute | solution.py:220
  64.1 10.3 %collective-permute-done.7.refs_5_ = bf16[2,2,96,1024]{3,2,1,0:T(8,128)(2,1)S(1)} collective-permute-done((bf16[2,2,96,1024]{3,2,1,0:T(8,128)(2,1)S(1)}, bf16[2,2,96,1024]{3,2,1,0:T(8,128)(2,1)S(1)}, u32[]{:S(2)}, u32[]{:S(2)}) %collective-permute-start.7) | collective-permute-done | bytes 786464 | tf_op jit(solution)/shard_map/ppermute | solution.py:220
  74.4 0.9 copy-done.11
  75.3 0.9 copy-done.12
  76.2 17.4 %expert.1 = (bf16[2,4,2,24,1024]{4,3,2,1,0:T(8,128)(2,1)}, bf16[2,4,2,24,1024]{4,3,2,1,0:T(8,128)(2,1)}, bf16[2,4,2,24,1024]{4,3,2,1,0:T(8,128)(2,1)}, bf16[2,4,...) custom-call(bf16[2,2,96,1024]{3,2,1,0:T(8,128)(2,1)} %copy-done.2, ...), custom_call_target="tpu_custom_call" | custom-call | flops 10871635968 | bytes 25165824 | tf_op jit(solution)/shard_map/expert/pallas_call | solution.py:283
  93.7 0.1 collective-permute-start.10
  93.8 0.1 collective-permute-start.11
  93.9 2.1 %collective-permute-start.12 = (bf16[2,4,48,1024]{3,2,1,0:T(8,128)(2,1)}, bf16[2,4,48,1024]{3,2,1,0:T(8,128)(2,1)S(1)}, u32[]{:S(2)}, u32[]{:S(2)}) collective-permute-start(bf16[2,4,48,1024]{3,2,1,0:T(8,128)(2,1)} %bitcast.23), channel_id=1, source_target_pairs={{56,0},{192,8},{8,16},{208,24},{24,32},{224,40},{40,48},{240,56},{... | collective-permute-start | bytes 2359304 | tf_op jit(solution)/shard_map/ppermute | solution.py:226
  96.0 0.9 collective-permute-start.13
  96.9 1.0 collective-permute-start.14
  97.9 2.7 %collective-permute-start.15 = (bf16[2,4,48,1024]{3,2,1,0:T(8,128)(2,1)}, bf16[2,4,48,1024]{3,2,1,0:T(8,128)(2,1)S(1)}, u32[]{:S(2)}, u32[]{:S(2)}) collective-permute-start(bf16[2,4,48,1024]{3,2,1,0:T(8,128)(2,1)} %bitcast.20), channel_id=1, source_target_pairs={{16,0},{72,8},{32,16},{88,24},{48,32},{104,40},{0,48},{120,56},{80... | collective-permute-start | bytes 2359304 | tf_op jit(solution)/shard_map/ppermute | solution.py:226
  100.6 13.6 %collective-permute-done.11.refs_2_ = bf16[2,4,48,1024]{3,2,1,0:T(8,128)(2,1)S(1)} collective-permute-done((bf16[2,4,48,1024]{3,2,1,0:T(8,128)(2,1)}, bf16[2,4,48,1024]{3,2,1,0:T(8,128)(2,1)S(1)}, u32[]{:S(2)}, u32[]{:S(2)}) %collective-permute-start.11) | collective-permute-done | bytes 786464 | tf_op jit(solution)/shard_map/ppermute | solution.py:226
  114.2 1.6 collective-permute-start.16
  115.8 0.7 collective-permute-done.12.refs_3_
  116.5 13.5 %collective-permute-done.13.refs_4_ = bf16[2,4,48,1024]{3,2,1,0:T(8,128)(2,1)S(1)} collective-permute-done((bf16[2,4,48,1024]{3,2,1,0:T(8,128)(2,1)}, bf16[2,4,48,1024]{3,2,1,0:T(8,128)(2,1)S(1)}, u32[]{:S(2)}, u32[]{:S(2)}) %collective-permute-start.13) | collective-permute-done | bytes 786464 | tf_op jit(solution)/shard_map/ppermute | solution.py:226
  130.1 1.7 %collective-permute-done.14.refs_5_ = bf16[2,4,48,1024]{3,2,1,0:T(8,128)(2,1)S(1)} collective-permute-done((bf16[2,4,48,1024]{3,2,1,0:T(8,128)(2,1)}, bf16[2,4,48,1024]{3,2,1,0:T(8,128)(2,1)S(1)}, u32[]{:S(2)}, u32[]{:S(2)}) %collective-permute-start.14) | collective-permute-done | bytes 786464 | tf_op jit(solution)/shard_map/ppermute | solution.py:226
  131.8 0.9 collective-permute-done.15.refs_6_
  132.7 1.2 collective-permute-done.16.refs_7_
  133.9 2.5 %combine.1 = (f32[2,128,1024]{2,1,0:T(8,128)S(1)}, bf16[2,128,1024]{2,1,0:T(8,128)(2,1)S(1)}, bf16[2,128,1024]{2,1,0:T(8,128)(2,1)S(1)}, bf16[2,128,1024]{2,1,0:T(8,128)(2,1)S(1)}) custom-call(bf16[2,4,256,384]{3,2,1,0:T(8,128)(2,1)S(1)} %copy-done.1, bf16[2,4,48,1024]{3,2,1,0:T(8,128)(2,1)S(1)} %bitcast.14, ...), custom_call_target="tpu_custom_call" | custom-call | flops 1610612736 | bytes 10485760 | tf_op jit(solution)/shard_map/combine/pallas_call | solution.py:302
  136.4 2.1 %collective-permute-start.17 = (bf16[2,128,1024]{2,1,0:T(8,128)(2,1)S(1)}, bf16[2,128,1024]{2,1,0:T(8,128)(2,1)S(1)}, u32[]{:S(2)}, u32[]{:S(2)}) collective-permute-start(bf16[2,128,1024]{2,1,0:T(8,128)(2,1)S(1)} %get-tuple-element.47), channel_id=1, source_target_pairs={{64,0},{24,8},{80,16},{40,24},{96,32},{56,40},{112,48},{8,56},{128... | collective-permute-start | bytes 1572872 | tf_op jit(solution)/shard_map/ppermute | solution.py:226
  138.5 0.0 collective-permute-start.18
  138.6 0.7 collective-permute-start.19
  139.2 11.1 %collective-permute-done.17.refs_0_ = bf16[2,128,1024]{2,1,0:T(8,128)(2,1)S(1)} collective-permute-done((bf16[2,128,1024]{2,1,0:T(8,128)(2,1)S(1)}, bf16[2,128,1024]{2,1,0:T(8,128)(2,1)S(1)}, u32[]{:S(2)}, u32[]{:S(2)}) %collective-permute-start.17) | collective-permute-done | bytes 524320 | tf_op jit(solution)/shard_map/ppermute | solution.py:226
  150.3 3.5 %collective-permute-done.19.refs_2_ = bf16[2,128,1024]{2,1,0:T(8,128)(2,1)S(1)} collective-permute-done((bf16[2,128,1024]{2,1,0:T(8,128)(2,1)S(1)}, bf16[2,128,1024]{2,1,0:T(8,128)(2,1)S(1)}, u32[]{:S(2)}, u32[]{:S(2)}) %collective-permute-start.19) | collective-permute-done | bytes 524320 | tf_op jit(solution)/shard_map/ppermute | solution.py:226
  153.8 1.2 reduce-scatter.2.cloned.1.call-done
  155.1 1.1 copy-done.4
  156.1 1.2 final.1
  (31 shorter events, 0.1 us)
Async XLA Ops:
  7.2 69.0 %all-gather.3.cloned.1.call-start = ((), (), s32[]{:S(2)}) async-start(), calls=%async_computation.2 | async-start | bytes 5308416 | tf_op jit(solution)/shard_map/all_gather | solution.py:247
  9.6 145.5 %reduce-scatter.2.cloned.1.call-start = ((), (), s32[]{:S(2)}) async-start(), calls=%async_computation.1 | async-start | bytes 5308416 | tf_op jit(solution)/shard_map/reduce_scatter | solution.py:296
  9.6 16.4 %collective-permute-start.2 = (bf16[272,1024]{1,0:T(8,128)(2,1)}, bf16[272,1024]{1,0:T(8,128)(2,1)S(1)}, u32[]{:S(2)}, u32[]{:S(2)}) collective-permute-start(bf16[272,1024]{1,0:T(8,128)(2,1)} %get-tuple-element.27.refs_0_), channel_id=1, source_target_pairs={{0,192},{8,56},{16,208},{24,8},{32,224},{40,24},{48,240},{56,40},{... | collective-permute-start | bytes 1671176 | tf_op jit(solution)/shard_map/ppermute | solution.py:220
  13.3 12.8 %collective-permute-start.1 = (bf16[272,1024]{1,0:T(8,128)(2,1)}, bf16[272,1024]{1,0:T(8,128)(2,1)S(1)}, u32[]{:S(2)}, u32[]{:S(2)}) collective-permute-start(bf16[272,1024]{1,0:T(8,128)(2,1)} %get-tuple-element.27.refs_0_), channel_id=1, source_target_pairs={{0,128},{8,40},{16,144},{24,56},{32,160},{40,8},{48,176},{56,24},{... | collective-permute-start | bytes 1671176 | tf_op jit(solution)/shard_map/ppermute | solution.py:220
  13.6 16.1 %collective-permute-start = (bf16[272,1024]{1,0:T(8,128)(2,1)}, bf16[272,1024]{1,0:T(8,128)(2,1)S(1)}, u32[]{:S(2)}, u32[]{:S(2)}) collective-permute-start(bf16[272,1024]{1,0:T(8,128)(2,1)} %get-tuple-element.27.refs_0_), channel_id=1, source_target_pairs={{0,64},{8,24},{16,80},{24,40},{32,96},{40,56},{48,112},{56,8},{64,... | collective-permute-start | bytes 1671176 | tf_op jit(solution)/shard_map/ppermute | solution.py:220
  29.7 1.1 copy-start.5
  33.7 42.5 %copy-start.2 = (bf16[2,2,96,1024]{3,2,1,0:T(8,128)(2,1)}, bf16[2,2,96,1024]{3,2,1,0:T(8,128)(2,1)S(1)}, u32[]{:S(2)}) copy-start(bf16[2,2,96,1024]{3,2,1,0:T(8,128)(2,1)S(1)} %get-tuple-element.28.refs_4_.refs_0_) | copy-start | bytes 2359300
  33.7 7.5 %collective-permute-start.3 = (bf16[2,2,96,1024]{3,2,1,0:T(8,128)(2,1)S(1)}, bf16[2,2,96,1024]{3,2,1,0:T(8,128)(2,1)S(1)}, u32[]{:S(2)}, u32[]{:S(2)}) collective-permute-start(bf16[2,2,96,1024]{3,2,1,0:T(8,128)(2,1)S(1)} %get-tuple-element.29), channel_id=1, source_target_pairs={{0,8},{8,0},{16,24},{24,16},{32,40},{40,32},{48,56},{56,48},{64,72... | collective-permute-start | bytes 2359304 | tf_op jit(solution)/shard_map/ppermute | solution.py:220
  35.3 12.5 %collective-permute-start.4 = (bf16[2,2,96,1024]{3,2,1,0:T(8,128)(2,1)S(1)}, bf16[2,2,96,1024]{3,2,1,0:T(8,128)(2,1)S(1)}, u32[]{:S(2)}, u32[]{:S(2)}) collective-permute-start(bf16[2,2,96,1024]{3,2,1,0:T(8,128)(2,1)S(1)} %get-tuple-element.30), channel_id=1, source_target_pairs={{0,16},{8,72},{16,32},{24,88},{32,48},{40,104},{48,0},{56,120},{64... | collective-permute-start | bytes 2359304 | tf_op jit(solution)/shard_map/ppermute | solution.py:220
  35.3 21.4 %collective-permute-start.5 = (bf16[2,2,96,1024]{3,2,1,0:T(8,128)(2,1)S(1)}, bf16[2,2,96,1024]{3,2,1,0:T(8,128)(2,1)S(1)}, u32[]{:S(2)}, u32[]{:S(2)}) collective-permute-start(bf16[2,2,96,1024]{3,2,1,0:T(8,128)(2,1)S(1)} %get-tuple-element.31), channel_id=1, source_target_pairs={{0,24},{8,64},{16,40},{24,80},{32,56},{40,96},{48,8},{56,112},{64,... | collective-permute-start | bytes 2359304 | tf_op jit(solution)/shard_map/ppermute | solution.py:220
  35.9 28.3 %collective-permute-start.6 = (bf16[2,2,96,1024]{3,2,1,0:T(8,128)(2,1)S(1)}, bf16[2,2,96,1024]{3,2,1,0:T(8,128)(2,1)S(1)}, u32[]{:S(2)}, u32[]{:S(2)}) collective-permute-start(bf16[2,2,96,1024]{3,2,1,0:T(8,128)(2,1)S(1)} %get-tuple-element.32), channel_id=1, source_target_pairs={{0,32},{8,136},{16,48},{24,152},{32,0},{40,168},{48,16},{56,184},{... | collective-permute-start | bytes 2359304 | tf_op jit(solution)/shard_map/ppermute | solution.py:220
  38.3 36.1 %collective-permute-start.7 = (bf16[2,2,96,1024]{3,2,1,0:T(8,128)(2,1)S(1)}, bf16[2,2,96,1024]{3,2,1,0:T(8,128)(2,1)S(1)}, u32[]{:S(2)}, u32[]{:S(2)}) collective-permute-start(bf16[2,2,96,1024]{3,2,1,0:T(8,128)(2,1)S(1)} %get-tuple-element.33), channel_id=1, source_target_pairs={{0,40},{8,128},{16,56},{24,144},{32,8},{40,160},{48,24},{56,176},{... | collective-permute-start | bytes 2359304 | tf_op jit(solution)/shard_map/ppermute | solution.py:220
  41.3 34.9 %copy-start.6 = (bf16[2,2,96,1024]{3,2,1,0:T(8,128)(2,1)}, bf16[2,2,96,1024]{3,2,1,0:T(8,128)(2,1)S(1)}, u32[]{:S(2)}) copy-start(bf16[2,2,96,1024]{3,2,1,0:T(8,128)(2,1)S(1)} %collective-permute-done.3.refs_1_) | copy-start | bytes 2359300
  41.3 33.1 %collective-permute-start.8 = (bf16[2,2,96,1024]{3,2,1,0:T(8,128)(2,1)S(1)}, bf16[2,2,96,1024]{3,2,1,0:T(8,128)(2,1)S(1)}, u32[]{:S(2)}, u32[]{:S(2)}) collective-permute-start(bf16[2,2,96,1024]{3,2,1,0:T(8,128)(2,1)S(1)} %get-tuple-element.34), channel_id=1, source_target_pairs={{0,48},{8,200},{16,0},{24,216},{32,16},{40,232},{48,32},{56,248},{... | collective-permute-start | bytes 2359304 | tf_op jit(solution)/shard_map/ppermute | solution.py:220
  47.7 26.7 %copy-start.7 = (bf16[2,2,96,1024]{3,2,1,0:T(8,128)(2,1)}, bf16[2,2,96,1024]{3,2,1,0:T(8,128)(2,1)S(1)}, u32[]{:S(2)}) copy-start(bf16[2,2,96,1024]{3,2,1,0:T(8,128)(2,1)S(1)} %collective-permute-done.4.refs_2_) | copy-start | bytes 2359300
  47.7 28.5 %collective-permute-start.9 = (bf16[2,2,96,1024]{3,2,1,0:T(8,128)(2,1)S(1)}, bf16[2,2,96,1024]{3,2,1,0:T(8,128)(2,1)}, u32[]{:S(2)}, u32[]{:S(2)}) collective-permute-start(bf16[2,2,96,1024]{3,2,1,0:T(8,128)(2,1)S(1)} %get-tuple-element.35), channel_id=1, source_target_pairs={{0,56},{8,192},{16,8},{24,208},{32,24},{40,224},{48,40},{56,240},{... | collective-permute-start | bytes 2359304 | tf_op jit(solution)/shard_map/ppermute | solution.py:220
  51.1 1.1 copy-start
  56.7 17.7 %copy-start.9 = (bf16[2,2,96,1024]{3,2,1,0:T(8,128)(2,1)}, bf16[2,2,96,1024]{3,2,1,0:T(8,128)(2,1)S(1)}, u32[]{:S(2)}) copy-start(bf16[2,2,96,1024]{3,2,1,0:T(8,128)(2,1)S(1)} %collective-permute-done.5.refs_3_) | copy-start | bytes 2359300
  64.1 10.3 %copy-start.10 = (bf16[2,2,96,1024]{3,2,1,0:T(8,128)(2,1)}, bf16[2,2,96,1024]{3,2,1,0:T(8,128)(2,1)S(1)}, u32[]{:S(2)}) copy-start(bf16[2,2,96,1024]{3,2,1,0:T(8,128)(2,1)S(1)} %collective-permute-done.6.refs_4_) | copy-start | bytes 2359300
  74.4 0.9 copy-start.11
  75.3 0.9 copy-start.12
  93.6 20.6 %copy-start.8 = (bf16[2,4,2,24,1024]{4,3,2,1,0:T(8,128)(2,1)S(1)}, bf16[2,4,2,24,1024]{4,3,2,1,0:T(8,128)(2,1)}, u32[]{:S(2)}) copy-start(bf16[2,4,2,24,1024]{4,3,2,1,0:T(8,128)(2,1)} %get-tuple-element.45) | copy-start | bytes 2359300
  93.6 40.3 %copy-start.1 = (bf16[2,4,256,384]{3,2,1,0:T(8,128)(2,1)S(1)}, bf16[2,4,256,384]{3,2,1,0:T(8,128)(2,1)}, u32[]{:S(2)}) copy-start(bf16[2,4,256,384]{3,2,1,0:T(8,128)(2,1)} %copy-done) | copy-start | bytes 4718596
  93.6 40.3 %copy-start.3 = (bf16[2,4,2,24,1024]{4,3,2,1,0:T(8,128)(2,1)S(1)}, bf16[2,4,2,24,1024]{4,3,2,1,0:T(8,128)(2,1)}, u32[]{:S(2)}) copy-start(bf16[2,4,2,24,1024]{4,3,2,1,0:T(8,128)(2,1)} %get-tuple-element.38) | copy-start | bytes 2359300
  93.7 4.3 %collective-permute-start.10 = (bf16[2,4,48,1024]{3,2,1,0:T(8,128)(2,1)}, bf16[2,4,48,1024]{3,2,1,0:T(8,128)(2,1)S(1)}, u32[]{:S(2)}, u32[]{:S(2)}) collective-permute-start(bf16[2,4,48,1024]{3,2,1,0:T(8,128)(2,1)} %bitcast.25), channel_id=1, source_target_pairs={{8,0},{0,8},{24,16},{16,24},{40,32},{32,40},{56,48},{48,56},{72,64... | collective-permute-start | bytes 2359304 | tf_op jit(solution)/shard_map/ppermute | solution.py:226
  93.8 20.5 %collective-permute-start.11 = (bf16[2,4,48,1024]{3,2,1,0:T(8,128)(2,1)}, bf16[2,4,48,1024]{3,2,1,0:T(8,128)(2,1)S(1)}, u32[]{:S(2)}, u32[]{:S(2)}) collective-permute-start(bf16[2,4,48,1024]{3,2,1,0:T(8,128)(2,1)} %bitcast.24), channel_id=1, source_target_pairs={{48,0},{200,8},{0,16},{216,24},{16,32},{232,40},{32,48},{248,56},{... | collective-permute-start | bytes 2359304 | tf_op jit(solution)/shard_map/ppermute | solution.py:226
  93.9 22.7 %collective-permute-start.12 = (bf16[2,4,48,1024]{3,2,1,0:T(8,128)(2,1)}, bf16[2,4,48,1024]{3,2,1,0:T(8,128)(2,1)S(1)}, u32[]{:S(2)}, u32[]{:S(2)}) collective-permute-start(bf16[2,4,48,1024]{3,2,1,0:T(8,128)(2,1)} %bitcast.23), channel_id=1, source_target_pairs={{56,0},{192,8},{8,16},{208,24},{24,32},{224,40},{40,48},{240,56},{... | collective-permute-start | bytes 2359304 | tf_op jit(solution)/shard_map/ppermute | solution.py:226
  96.0 34.1 %collective-permute-start.13 = (bf16[2,4,48,1024]{3,2,1,0:T(8,128)(2,1)}, bf16[2,4,48,1024]{3,2,1,0:T(8,128)(2,1)S(1)}, u32[]{:S(2)}, u32[]{:S(2)}) collective-permute-start(bf16[2,4,48,1024]{3,2,1,0:T(8,128)(2,1)} %bitcast.22), channel_id=1, source_target_pairs={{32,0},{136,8},{48,16},{152,24},{0,32},{168,40},{16,48},{184,56},{... | collective-permute-start | bytes 2359304 | tf_op jit(solution)/shard_map/ppermute | solution.py:226
  96.9 34.9 %collective-permute-start.14 = (bf16[2,4,48,1024]{3,2,1,0:T(8,128)(2,1)}, bf16[2,4,48,1024]{3,2,1,0:T(8,128)(2,1)S(1)}, u32[]{:S(2)}, u32[]{:S(2)}) collective-permute-start(bf16[2,4,48,1024]{3,2,1,0:T(8,128)(2,1)} %bitcast.21), channel_id=1, source_target_pairs={{40,0},{128,8},{56,16},{144,24},{8,32},{160,40},{24,48},{176,56},{... | collective-permute-start | bytes 2359304 | tf_op jit(solution)/shard_map/ppermute | solution.py:226
  97.9 34.7 %collective-permute-start.15 = (bf16[2,4,48,1024]{3,2,1,0:T(8,128)(2,1)}, bf16[2,4,48,1024]{3,2,1,0:T(8,128)(2,1)S(1)}, u32[]{:S(2)}, u32[]{:S(2)}) collective-permute-start(bf16[2,4,48,1024]{3,2,1,0:T(8,128)(2,1)} %bitcast.20), channel_id=1, source_target_pairs={{16,0},{72,8},{32,16},{88,24},{48,32},{104,40},{0,48},{120,56},{80... | collective-permute-start | bytes 2359304 | tf_op jit(solution)/shard_map/ppermute | solution.py:226
  114.2 19.7 %collective-permute-start.16 = (bf16[2,4,48,1024]{3,2,1,0:T(8,128)(2,1)S(1)}, bf16[2,4,48,1024]{3,2,1,0:T(8,128)(2,1)S(1)}, u32[]{:S(2)}, u32[]{:S(2)}) collective-permute-start(bf16[2,4,48,1024]{3,2,1,0:T(8,128)(2,1)S(1)} %bitcast.19), channel_id=1, source_target_pairs={{24,0},{64,8},{40,16},{80,24},{56,32},{96,40},{8,48},{112,56},{88,... | collective-permute-start | bytes 2359304 | tf_op jit(solution)/shard_map/ppermute | solution.py:226
  136.4 13.8 %collective-permute-start.17 = (bf16[2,128,1024]{2,1,0:T(8,128)(2,1)S(1)}, bf16[2,128,1024]{2,1,0:T(8,128)(2,1)S(1)}, u32[]{:S(2)}, u32[]{:S(2)}) collective-permute-start(bf16[2,128,1024]{2,1,0:T(8,128)(2,1)S(1)} %get-tuple-element.47), channel_id=1, source_target_pairs={{64,0},{24,8},{80,16},{40,24},{96,32},{56,40},{112,48},{8,56},{128... | collective-permute-start | bytes 1572872 | tf_op jit(solution)/shard_map/ppermute | solution.py:226
  138.5 11.7 %collective-permute-start.18 = (bf16[2,128,1024]{2,1,0:T(8,128)(2,1)S(1)}, bf16[2,128,1024]{2,1,0:T(8,128)(2,1)S(1)}, u32[]{:S(2)}, u32[]{:S(2)}) collective-permute-start(bf16[2,128,1024]{2,1,0:T(8,128)(2,1)S(1)} %get-tuple-element.48), channel_id=1, source_target_pairs={{128,0},{40,8},{144,16},{56,24},{160,32},{8,40},{176,48},{24,56},{... | collective-permute-start | bytes 1572872 | tf_op jit(solution)/shard_map/ppermute | solution.py:226
  138.6 15.3 %collective-permute-start.19 = (bf16[2,128,1024]{2,1,0:T(8,128)(2,1)S(1)}, bf16[2,128,1024]{2,1,0:T(8,128)(2,1)S(1)}, u32[]{:S(2)}, u32[]{:S(2)}) collective-permute-start(bf16[2,128,1024]{2,1,0:T(8,128)(2,1)S(1)} %get-tuple-element.49), channel_id=1, source_target_pairs={{192,0},{56,8},{208,16},{8,24},{224,32},{24,40},{240,48},{40,56},{... | collective-permute-start | bytes 1572872 | tf_op jit(solution)/shard_map/ppermute | solution.py:226
  155.1 1.1 copy-start.4
Sparse Core Ops, SparseCore 0:
  9.8 63.5 all-gather.2
  93.8 61.2 reduce-scatter.1

commit v5 on v4

--- a/solution.py
+++ b/solution.py
@@ -222,6 +222,9 @@
     def onchip(x):
         return pltpu.with_memory_space_constraint(x, pltpu.VMEM)
 
+    def offchip(x):
+        return pltpu.with_memory_space_constraint(x, pltpu.HBM)
+
     def restore(x, target):
         return lax.ppermute(x, "expert", [(target(n), n) for n in everyone])
 
@@ -260,7 +263,7 @@
         flops=2 * pack_flops,
         vmem=32,
         nbytes=16 << 20,
-    )(first_expert, *[onchip(x) for x in bundles])
+    )(first_expert, offchip(own), *[onchip(x) for x in bundles[1:]])
     chunks = list(packed[:1]) + [permute(x, target) for x, target in zip(packed[1:], sends)]
     slot_rows = local * count * CAP
     picks = call(
@@ -292,7 +295,7 @@
         flops=9 * unit,
         vmem=56,
         nbytes=24 << 20,
-    )(*chunks, weights, picks)
+    )(*[offchip(x) for x in chunks], weights, picks)
     summed = lax.psum_scatter(weight_grads, "dp", scatter_dimension=0, tiled=False)
     returns = [x.reshape(2, SIDE, local * CAP, width) for x in returns]
     order = [0] + sorted(range(1, count), key=lambda p: (-hops[p][0] % SIDE, hops[p][1]))
@@ -324,7 +327,7 @@
         in_specs=[vm] * (SIDE + 1),
         out_specs=[vm] * 4,
         nbytes=4 << 20,
-    )(summed, *sums)
+    )(offchip(summed), *sums)
 
 
 def solution(mesh):

time: 164 us -> 164 us (level)
    unnamed x26 -> x24, local copies, waits for them, and re-layouts: 5.06 us -> 4 us
where the time goes in v5:
time: 164 us
  waiting for transfers between devices  88.8 us (54%)
  Pallas kernels  29.1 us (18%)
  starting transfers between devices  26.9 us (16%)
  between operations  14.2 us (9%)
  local copies, waits for them, and re-layouts  4.69 us (3%)
    ppermute x10, waiting for transfers between devices, restore(): return lax.ppermute(x, 'expert', [(target(n), n) for n in everyone])  46.3 us
    ppermute x10, waiting for transfers between devices, permute(): return lax.ppermute(x, 'expert', [(n, target(n)) for n in everyone])  41.2 us
    pallas_call x1, Pallas kernels, shards(): call(functools.partial(expert_kernel, count), 'expert', [back_shape] * co...  17.4 us
    ppermute x10, starting transfers between devices, permute(): return lax.ppermute(x, 'expert', [(n, target(n)) for n in everyone])  15.5 us
    ppermute x10, starting transfers between devices, restore(): return lax.ppermute(x, 'expert', [(target(n), n) for n in everyone])  11.3 us
    unnamed x24, local copies, waits for them, and re-layouts  4 us
    pallas_call x1, Pallas kernels, shards(): call(pack_kernel, 'pack', [pltpu.VMEM(chunk_shape.shape, BF)] * count, in...  3.45 us
  transfers between devices with their start and end apart: 22, of which 15 were waited for; matrix products, arithmetic and copies ran while one was open for 0% of the time, Pallas kernels for 4%

profile of v5, /device:TPU:1, one launch (start us, length us, event | category | flops | bytes accessed | tf_op | source)
XLA Modules:
  0.0 163.6 jit_solution(14439391990688384916)
XLA Ops:
  7.2 0.0 all-gather.3.cloned.1.call-start
  7.2 2.3 %head.1 = (bf16[2,192,768]{2,1,0:T(8,128)(2,1)}, bf16[272,1024]{1,0:T(8,128)(2,1)}) custom-call(s32[8,128]{1,0:T(8,128)} %bitcast.16, f32[8,128]{1,0:T(8,128)} %bitcast.17, bf16[128,1024]{1,0:T(8,128)(2,1)} %tokens_ref.1, bf16[128,1024]{1,0:T(8,128)(2,1)} %cot_ref.1, bf16[2,128,768]{2,1,0:T(8,128)(2,1)} %lift_ref.1, bf16[2,384,128]{2,1,0:T(8,128)(2,1)} %down_ref.1), custom_call_target="tpu_custom_call" | custom-call | bytes 2097152 | tf_op jit(solution)/shard_map/head/pallas_call | solution.py:238
  9.6 0.0 reduce-scatter.2.cloned.1.call-start
  9.6 3.6 %collective-permute-start.2 = (bf16[272,1024]{1,0:T(8,128)(2,1)}, bf16[272,1024]{1,0:T(8,128)(2,1)S(1)}, u32[]{:S(2)}, u32[]{:S(2)}) collective-permute-start(bf16[272,1024]{1,0:T(8,128)(2,1)} %get-tuple-element.27.refs_0_), channel_id=1, source_target_pairs={{0,192},{8,56},{16,208},{24,8},{32,224},{40,24},{48,240},{56,40},{... | collective-permute-start | bytes 1671176 | tf_op jit(solution)/shard_map/ppermute | solution.py:220
  13.3 0.3 collective-permute-start.1
  13.6 0.7 collective-permute-start
  14.3 0.7 dynamic-slice_bitcast_fusion.first_ref
  15.0 11.0 %collective-permute-done.2.refs_3_ = bf16[272,1024]{1,0:T(8,128)(2,1)S(1)} collective-permute-done((bf16[272,1024]{1,0:T(8,128)(2,1)}, bf16[272,1024]{1,0:T(8,128)(2,1)S(1)}, u32[]{:S(2)}, u32[]{:S(2)}) %collective-permute-start.2) | collective-permute-done | bytes 557088 | tf_op jit(solution)/shard_map/ppermute | solution.py:220
  26.0 3.7 %collective-permute-done.refs_1_ = bf16[272,1024]{1,0:T(8,128)(2,1)S(1)} collective-permute-done((bf16[272,1024]{1,0:T(8,128)(2,1)}, bf16[272,1024]{1,0:T(8,128)(2,1)S(1)}, u32[]{:S(2)}, u32[]{:S(2)}) %collective-permute-start) | collective-permute-done | bytes 557088 | tf_op jit(solution)/shard_map/ppermute | solution.py:220
  29.7 3.4 %pack.1 = (bf16[2,2,96,1024]{3,2,1,0:T(8,128)(2,1)S(1)}, bf16[2,2,96,1024]{3,2,1,0:T(8,128)(2,1)S(1)}, bf16[2,2,96,1024]{3,2,1,0:T(8,128)(2,1)S(1)}, bf16[2,2,96...) custom-call(s32[8]{0:T(128)S(1)} %dynamic-slice_bitcast_fusion.first, ...), custom_call_target="tpu_custom_call" | custom-call | flops 805306368 | bytes 16777216 | tf_op jit(solution)/shard_map/pack/pallas_call | solution.py:256
  33.2 1.5 collective-permute-start.3
  34.7 0.6 collective-permute-start.5
  35.3 2.5 %collective-permute-start.6 = (bf16[2,2,96,1024]{3,2,1,0:T(8,128)(2,1)S(1)}, bf16[2,2,96,1024]{3,2,1,0:T(8,128)(2,1)S(1)}, u32[]{:S(2)}, u32[]{:S(2)}) collective-permute-start(bf16[2,2,96,1024]{3,2,1,0:T(8,128)(2,1)S(1)} %get-tuple-element.32), channel_id=1, source_target_pairs={{0,32},{8,136},{16,48},{24,152},{32,0},{40,168},{48,16},{56,184},{... | collective-permute-start | bytes 2359304 | tf_op jit(solution)/shard_map/ppermute | solution.py:220
  37.8 2.9 %collective-permute-start.7 = (bf16[2,2,96,1024]{3,2,1,0:T(8,128)(2,1)S(1)}, bf16[2,2,96,1024]{3,2,1,0:T(8,128)(2,1)S(1)}, u32[]{:S(2)}, u32[]{:S(2)}) collective-permute-start(bf16[2,2,96,1024]{3,2,1,0:T(8,128)(2,1)S(1)} %get-tuple-element.33), channel_id=1, source_target_pairs={{0,40},{8,128},{16,56},{24,144},{32,8},{40,160},{48,24},{56,176},{... | collective-permute-start | bytes 2359304 | tf_op jit(solution)/shard_map/ppermute | solution.py:220
  40.7 1.1 collective-permute-start.8
  41.8 5.4 %collective-permute-done.4.refs_2_ = bf16[2,2,96,1024]{3,2,1,0:T(8,128)(2,1)S(1)} collective-permute-done((bf16[2,2,96,1024]{3,2,1,0:T(8,128)(2,1)S(1)}, bf16[2,2,96,1024]{3,2,1,0:T(8,128)(2,1)S(1)}, u32[]{:S(2)}, u32[]{:S(2)}) %collective-permute-start.4) | collective-permute-done | bytes 786464 | tf_op jit(solution)/shard_map/ppermute | solution.py:220
  47.2 2.2 %collective-permute-start.9 = (bf16[2,2,96,1024]{3,2,1,0:T(8,128)(2,1)S(1)}, bf16[2,2,96,1024]{3,2,1,0:T(8,128)(2,1)}, u32[]{:S(2)}, u32[]{:S(2)}) collective-permute-start(bf16[2,2,96,1024]{3,2,1,0:T(8,128)(2,1)S(1)} %get-tuple-element.35), channel_id=1, source_target_pairs={{0,56},{8,192},{16,8},{24,208},{32,24},{40,224},{48,40},{56,240},{... | collective-permute-start | bytes 2359304 | tf_op jit(solution)/shard_map/ppermute | solution.py:220
  49.4 1.1 copy-done.4
  50.4 1.2 plan.1.refs_9_.pick_ref
  51.6 1.1 copy-done
  52.7 3.4 %collective-permute-done.5.refs_3_ = bf16[2,2,96,1024]{3,2,1,0:T(8,128)(2,1)S(1)} collective-permute-done((bf16[2,2,96,1024]{3,2,1,0:T(8,128)(2,1)S(1)}, bf16[2,2,96,1024]{3,2,1,0:T(8,128)(2,1)S(1)}, u32[]{:S(2)}, u32[]{:S(2)}) %collective-permute-start.5) | collective-permute-done | bytes 786464 | tf_op jit(solution)/shard_map/ppermute | solution.py:220
  56.1 7.4 %collective-permute-done.6.refs_4_ = bf16[2,2,96,1024]{3,2,1,0:T(8,128)(2,1)S(1)} collective-permute-done((bf16[2,2,96,1024]{3,2,1,0:T(8,128)(2,1)S(1)}, bf16[2,2,96,1024]{3,2,1,0:T(8,128)(2,1)S(1)}, u32[]{:S(2)}, u32[]{:S(2)}) %collective-permute-start.6) | collective-permute-done | bytes 786464 | tf_op jit(solution)/shard_map/ppermute | solution.py:220
  63.6 10.2 %collective-permute-done.7.refs_5_ = bf16[2,2,96,1024]{3,2,1,0:T(8,128)(2,1)S(1)} collective-permute-done((bf16[2,2,96,1024]{3,2,1,0:T(8,128)(2,1)S(1)}, bf16[2,2,96,1024]{3,2,1,0:T(8,128)(2,1)S(1)}, u32[]{:S(2)}, u32[]{:S(2)}) %collective-permute-start.7) | collective-permute-done | bytes 786464 | tf_op jit(solution)/shard_map/ppermute | solution.py:220
  73.9 0.9 copy-done.10
  74.7 0.9 copy-done.11
  75.7 17.4 %expert.1 = (bf16[2,4,2,24,1024]{4,3,2,1,0:T(8,128)(2,1)}, bf16[2,4,2,24,1024]{4,3,2,1,0:T(8,128)(2,1)}, bf16[2,4,2,24,1024]{4,3,2,1,0:T(8,128)(2,1)}, bf16[2,4,...) custom-call(bf16[2,2,96,1024]{3,2,1,0:T(8,128)(2,1)} %copy-done.2, ...), custom_call_target="tpu_custom_call" | custom-call | flops 10871635968 | bytes 25165824 | tf_op jit(solution)/shard_map/expert/pallas_call | solution.py:286
  93.1 0.0 reduce-scatter.2.cloned.1.call-update
  93.1 0.1 collective-permute-start.10
  93.2 0.1 collective-permute-start.11
  93.3 2.1 %collective-permute-start.12 = (bf16[2,4,48,1024]{3,2,1,0:T(8,128)(2,1)}, bf16[2,4,48,1024]{3,2,1,0:T(8,128)(2,1)S(1)}, u32[]{:S(2)}, u32[]{:S(2)}) collective-permute-start(bf16[2,4,48,1024]{3,2,1,0:T(8,128)(2,1)} %bitcast.23), channel_id=1, source_target_pairs={{56,0},{192,8},{8,16},{208,24},{24,32},{224,40},{40,48},{240,56},{... | collective-permute-start | bytes 2359304 | tf_op jit(solution)/shard_map/ppermute | solution.py:229
  95.4 1.5 collective-permute-start.13
  96.9 0.5 collective-permute-start.14
  97.5 2.6 %collective-permute-start.15 = (bf16[2,4,48,1024]{3,2,1,0:T(8,128)(2,1)}, bf16[2,4,48,1024]{3,2,1,0:T(8,128)(2,1)S(1)}, u32[]{:S(2)}, u32[]{:S(2)}) collective-permute-start(bf16[2,4,48,1024]{3,2,1,0:T(8,128)(2,1)} %bitcast.20), channel_id=1, source_target_pairs={{16,0},{72,8},{32,16},{88,24},{48,32},{104,40},{0,48},{120,56},{80... | collective-permute-start | bytes 2359304 | tf_op jit(solution)/shard_map/ppermute | solution.py:229
  100.1 13.6 %collective-permute-done.11.refs_2_ = bf16[2,4,48,1024]{3,2,1,0:T(8,128)(2,1)S(1)} collective-permute-done((bf16[2,4,48,1024]{3,2,1,0:T(8,128)(2,1)}, bf16[2,4,48,1024]{3,2,1,0:T(8,128)(2,1)S(1)}, u32[]{:S(2)}, u32[]{:S(2)}) %collective-permute-start.11) | collective-permute-done | bytes 786464 | tf_op jit(solution)/shard_map/ppermute | solution.py:229
  113.7 1.6 collective-permute-start.16
  115.3 0.7 collective-permute-done.12.refs_3_
  116.0 13.6 %collective-permute-done.13.refs_4_ = bf16[2,4,48,1024]{3,2,1,0:T(8,128)(2,1)S(1)} collective-permute-done((bf16[2,4,48,1024]{3,2,1,0:T(8,128)(2,1)}, bf16[2,4,48,1024]{3,2,1,0:T(8,128)(2,1)S(1)}, u32[]{:S(2)}, u32[]{:S(2)}) %collective-permute-start.13) | collective-permute-done | bytes 786464 | tf_op jit(solution)/shard_map/ppermute | solution.py:229
  129.5 1.7 %collective-permute-done.14.refs_5_ = bf16[2,4,48,1024]{3,2,1,0:T(8,128)(2,1)S(1)} collective-permute-done((bf16[2,4,48,1024]{3,2,1,0:T(8,128)(2,1)}, bf16[2,4,48,1024]{3,2,1,0:T(8,128)(2,1)S(1)}, u32[]{:S(2)}, u32[]{:S(2)}) %collective-permute-start.14) | collective-permute-done | bytes 786464 | tf_op jit(solution)/shard_map/ppermute | solution.py:229
  131.2 0.9 collective-permute-done.15.refs_6_
  132.1 1.2 collective-permute-done.16.refs_7_
  133.4 2.5 %combine.1 = (f32[2,128,1024]{2,1,0:T(8,128)S(1)}, bf16[2,128,1024]{2,1,0:T(8,128)(2,1)S(1)}, bf16[2,128,1024]{2,1,0:T(8,128)(2,1)S(1)}, bf16[2,128,1024]{2,1,0:T(8,128)(2,1)S(1)}) custom-call(bf16[2,4,256,384]{3,2,1,0:T(8,128)(2,1)S(1)} %copy-done.1, bf16[2,4,48,1024]{3,2,1,0:T(8,128)(2,1)S(1)} %bitcast.14, ...), custom_call_target="tpu_custom_call" | custom-call | flops 1610612736 | bytes 10485760 | tf_op jit(solution)/shard_map/combine/pallas_call | solution.py:305
  135.9 2.1 %collective-permute-start.17 = (bf16[2,128,1024]{2,1,0:T(8,128)(2,1)S(1)}, bf16[2,128,1024]{2,1,0:T(8,128)(2,1)S(1)}, u32[]{:S(2)}, u32[]{:S(2)}) collective-permute-start(bf16[2,128,1024]{2,1,0:T(8,128)(2,1)S(1)} %get-tuple-element.47), channel_id=1, source_target_pairs={{64,0},{24,8},{80,16},{40,24},{96,32},{56,40},{112,48},{8,56},{128... | collective-permute-start | bytes 1572872 | tf_op jit(solution)/shard_map/ppermute | solution.py:229
  138.0 0.0 collective-permute-start.18
  138.0 0.6 collective-permute-start.19
  138.7 11.1 %collective-permute-done.17.refs_0_ = bf16[2,128,1024]{2,1,0:T(8,128)(2,1)S(1)} collective-permute-done((bf16[2,128,1024]{2,1,0:T(8,128)(2,1)S(1)}, bf16[2,128,1024]{2,1,0:T(8,128)(2,1)S(1)}, u32[]{:S(2)}, u32[]{:S(2)}) %collective-permute-start.17) | collective-permute-done | bytes 524320 | tf_op jit(solution)/shard_map/ppermute | solution.py:229
  149.7 3.5 %collective-permute-done.19.refs_2_ = bf16[2,128,1024]{2,1,0:T(8,128)(2,1)S(1)} collective-permute-done((bf16[2,128,1024]{2,1,0:T(8,128)(2,1)S(1)}, bf16[2,128,1024]{2,1,0:T(8,128)(2,1)S(1)}, u32[]{:S(2)}, u32[]{:S(2)}) %collective-permute-start.19) | collective-permute-done | bytes 524320 | tf_op jit(solution)/shard_map/ppermute | solution.py:229
  153.3 1.3 reduce-scatter.2.cloned.1.call-done
  154.5 2.2 %final.1 = (bf16[128,1024]{1,0:T(8,128)(2,1)}, bf16[128,1024]{1,0:T(8,128)(2,1)}, bf16[2,128,768]{2,1,0:T(8,128)(2,1)}, bf16[2,384,128]{2,1,0:T(8,128)(2,1)}) custom-call(bf16[2,192,768]{2,1,0:T(8,128)(2,1)} %bitcast.15, f32[2,128,1024]{2,1,0:T(8,128)S(1)} %get-tuple-element.46.own_ref, bf16[2,128,1024]{2,1,0:T(8,128)(2,1)S(1)} %collective-permute-done.17.refs_0_, ...), custom_call_target="tpu_custom_call" | custom-call | bytes 4194304 | tf_op jit(solution)/shard_map/final/pallas_call | solution.py:318
  (29 shorter events, 0.1 us)
Async XLA Ops:
  7.2 68.5 %all-gather.3.cloned.1.call-start = ((), (), s32[]{:S(2)}) async-start(), calls=%async_computation.2 | async-start | bytes 5308416 | tf_op jit(solution)/shard_map/all_gather | solution.py:250
  9.6 145.0 %reduce-scatter.2.cloned.1.call-start = ((), (), s32[]{:S(2)}) async-start(), calls=%async_computation.1 | async-start | bytes 5308416 | tf_op jit(solution)/shard_map/reduce_scatter | solution.py:299
  9.6 16.4 %collective-permute-start.2 = (bf16[272,1024]{1,0:T(8,128)(2,1)}, bf16[272,1024]{1,0:T(8,128)(2,1)S(1)}, u32[]{:S(2)}, u32[]{:S(2)}) collective-permute-start(bf16[272,1024]{1,0:T(8,128)(2,1)} %get-tuple-element.27.refs_0_), channel_id=1, source_target_pairs={{0,192},{8,56},{16,208},{24,8},{32,224},{40,24},{48,240},{56,40},{... | collective-permute-start | bytes 1671176 | tf_op jit(solution)/shard_map/ppermute | solution.py:220
  13.3 12.8 %collective-permute-start.1 = (bf16[272,1024]{1,0:T(8,128)(2,1)}, bf16[272,1024]{1,0:T(8,128)(2,1)S(1)}, u32[]{:S(2)}, u32[]{:S(2)}) collective-permute-start(bf16[272,1024]{1,0:T(8,128)(2,1)} %get-tuple-element.27.refs_0_), channel_id=1, source_target_pairs={{0,128},{8,40},{16,144},{24,56},{32,160},{40,8},{48,176},{56,24},{... | collective-permute-start | bytes 1671176 | tf_op jit(solution)/shard_map/ppermute | solution.py:220
  13.6 16.1 %collective-permute-start = (bf16[272,1024]{1,0:T(8,128)(2,1)}, bf16[272,1024]{1,0:T(8,128)(2,1)S(1)}, u32[]{:S(2)}, u32[]{:S(2)}) collective-permute-start(bf16[272,1024]{1,0:T(8,128)(2,1)} %get-tuple-element.27.refs_0_), channel_id=1, source_target_pairs={{0,64},{8,24},{16,80},{24,40},{32,96},{40,56},{48,112},{56,8},{64,... | collective-permute-start | bytes 1671176 | tf_op jit(solution)/shard_map/ppermute | solution.py:220
  33.2 42.5 %copy-start.2 = (bf16[2,2,96,1024]{3,2,1,0:T(8,128)(2,1)}, bf16[2,2,96,1024]{3,2,1,0:T(8,128)(2,1)S(1)}, u32[]{:S(2)}) copy-start(bf16[2,2,96,1024]{3,2,1,0:T(8,128)(2,1)S(1)} %get-tuple-element.28.refs_4_.refs_0_) | copy-start | bytes 2359300
  33.2 7.5 %collective-permute-start.3 = (bf16[2,2,96,1024]{3,2,1,0:T(8,128)(2,1)S(1)}, bf16[2,2,96,1024]{3,2,1,0:T(8,128)(2,1)S(1)}, u32[]{:S(2)}, u32[]{:S(2)}) collective-permute-start(bf16[2,2,96,1024]{3,2,1,0:T(8,128)(2,1)S(1)} %get-tuple-element.29), channel_id=1, source_target_pairs={{0,8},{8,0},{16,24},{24,16},{32,40},{40,32},{48,56},{56,48},{64,72... | collective-permute-start | bytes 2359304 | tf_op jit(solution)/shard_map/ppermute | solution.py:220
  34.7 12.5 %collective-permute-start.4 = (bf16[2,2,96,1024]{3,2,1,0:T(8,128)(2,1)S(1)}, bf16[2,2,96,1024]{3,2,1,0:T(8,128)(2,1)S(1)}, u32[]{:S(2)}, u32[]{:S(2)}) collective-permute-start(bf16[2,2,96,1024]{3,2,1,0:T(8,128)(2,1)S(1)} %get-tuple-element.30), channel_id=1, source_target_pairs={{0,16},{8,72},{16,32},{24,88},{32,48},{40,104},{48,0},{56,120},{64... | collective-permute-start | bytes 2359304 | tf_op jit(solution)/shard_map/ppermute | solution.py:220
  34.7 21.4 %collective-permute-start.5 = (bf16[2,2,96,1024]{3,2,1,0:T(8,128)(2,1)S(1)}, bf16[2,2,96,1024]{3,2,1,0:T(8,128)(2,1)S(1)}, u32[]{:S(2)}, u32[]{:S(2)}) collective-permute-start(bf16[2,2,96,1024]{3,2,1,0:T(8,128)(2,1)S(1)} %get-tuple-element.31), channel_id=1, source_target_pairs={{0,24},{8,64},{16,40},{24,80},{32,56},{40,96},{48,8},{56,112},{64,... | collective-permute-start | bytes 2359304 | tf_op jit(solution)/shard_map/ppermute | solution.py:220
  35.3 28.3 %collective-permute-start.6 = (bf16[2,2,96,1024]{3,2,1,0:T(8,128)(2,1)S(1)}, bf16[2,2,96,1024]{3,2,1,0:T(8,128)(2,1)S(1)}, u32[]{:S(2)}, u32[]{:S(2)}) collective-permute-start(bf16[2,2,96,1024]{3,2,1,0:T(8,128)(2,1)S(1)} %get-tuple-element.32), channel_id=1, source_target_pairs={{0,32},{8,136},{16,48},{24,152},{32,0},{40,168},{48,16},{56,184},{... | collective-permute-start | bytes 2359304 | tf_op jit(solution)/shard_map/ppermute | solution.py:220
  37.8 36.1 %collective-permute-start.7 = (bf16[2,2,96,1024]{3,2,1,0:T(8,128)(2,1)S(1)}, bf16[2,2,96,1024]{3,2,1,0:T(8,128)(2,1)S(1)}, u32[]{:S(2)}, u32[]{:S(2)}) collective-permute-start(bf16[2,2,96,1024]{3,2,1,0:T(8,128)(2,1)S(1)} %get-tuple-element.33), channel_id=1, source_target_pairs={{0,40},{8,128},{16,56},{24,144},{32,8},{40,160},{48,24},{56,176},{... | collective-permute-start | bytes 2359304 | tf_op jit(solution)/shard_map/ppermute | solution.py:220
  40.7 34.9 %copy-start.5 = (bf16[2,2,96,1024]{3,2,1,0:T(8,128)(2,1)}, bf16[2,2,96,1024]{3,2,1,0:T(8,128)(2,1)S(1)}, u32[]{:S(2)}) copy-start(bf16[2,2,96,1024]{3,2,1,0:T(8,128)(2,1)S(1)} %collective-permute-done.3.refs_1_) | copy-start | bytes 2359300
  40.7 33.1 %collective-permute-start.8 = (bf16[2,2,96,1024]{3,2,1,0:T(8,128)(2,1)S(1)}, bf16[2,2,96,1024]{3,2,1,0:T(8,128)(2,1)S(1)}, u32[]{:S(2)}, u32[]{:S(2)}) collective-permute-start(bf16[2,2,96,1024]{3,2,1,0:T(8,128)(2,1)S(1)} %get-tuple-element.34), channel_id=1, source_target_pairs={{0,48},{8,200},{16,0},{24,216},{32,16},{40,232},{48,32},{56,248},{... | collective-permute-start | bytes 2359304 | tf_op jit(solution)/shard_map/ppermute | solution.py:220
  47.2 26.7 %copy-start.6 = (bf16[2,2,96,1024]{3,2,1,0:T(8,128)(2,1)}, bf16[2,2,96,1024]{3,2,1,0:T(8,128)(2,1)S(1)}, u32[]{:S(2)}) copy-start(bf16[2,2,96,1024]{3,2,1,0:T(8,128)(2,1)S(1)} %collective-permute-done.4.refs_2_) | copy-start | bytes 2359300
  47.2 28.5 %collective-permute-start.9 = (bf16[2,2,96,1024]{3,2,1,0:T(8,128)(2,1)S(1)}, bf16[2,2,96,1024]{3,2,1,0:T(8,128)(2,1)}, u32[]{:S(2)}, u32[]{:S(2)}) collective-permute-start(bf16[2,2,96,1024]{3,2,1,0:T(8,128)(2,1)S(1)} %get-tuple-element.35), channel_id=1, source_target_pairs={{0,56},{8,192},{16,8},{24,208},{32,24},{40,224},{48,40},{56,240},{... | collective-permute-start | bytes 2359304 | tf_op jit(solution)/shard_map/ppermute | solution.py:220
  49.4 1.1 copy-start.4
  51.6 1.1 copy-start
  56.1 17.7 %copy-start.8 = (bf16[2,2,96,1024]{3,2,1,0:T(8,128)(2,1)}, bf16[2,2,96,1024]{3,2,1,0:T(8,128)(2,1)S(1)}, u32[]{:S(2)}) copy-start(bf16[2,2,96,1024]{3,2,1,0:T(8,128)(2,1)S(1)} %collective-permute-done.5.refs_3_) | copy-start | bytes 2359300
  63.6 10.3 %copy-start.9 = (bf16[2,2,96,1024]{3,2,1,0:T(8,128)(2,1)}, bf16[2,2,96,1024]{3,2,1,0:T(8,128)(2,1)S(1)}, u32[]{:S(2)}) copy-start(bf16[2,2,96,1024]{3,2,1,0:T(8,128)(2,1)S(1)} %collective-permute-done.6.refs_4_) | copy-start | bytes 2359300
  73.8 0.9 copy-start.10
  74.7 0.9 copy-start.11
  93.1 20.6 %copy-start.7 = (bf16[2,4,2,24,1024]{4,3,2,1,0:T(8,128)(2,1)S(1)}, bf16[2,4,2,24,1024]{4,3,2,1,0:T(8,128)(2,1)}, u32[]{:S(2)}) copy-start(bf16[2,4,2,24,1024]{4,3,2,1,0:T(8,128)(2,1)} %get-tuple-element.45) | copy-start | bytes 2359300
  93.1 40.3 %copy-start.1 = (bf16[2,4,256,384]{3,2,1,0:T(8,128)(2,1)S(1)}, bf16[2,4,256,384]{3,2,1,0:T(8,128)(2,1)}, u32[]{:S(2)}) copy-start(bf16[2,4,256,384]{3,2,1,0:T(8,128)(2,1)} %copy-done) | copy-start | bytes 4718596
  93.1 40.3 %copy-start.3 = (bf16[2,4,2,24,1024]{4,3,2,1,0:T(8,128)(2,1)S(1)}, bf16[2,4,2,24,1024]{4,3,2,1,0:T(8,128)(2,1)}, u32[]{:S(2)}) copy-start(bf16[2,4,2,24,1024]{4,3,2,1,0:T(8,128)(2,1)} %get-tuple-element.38) | copy-start | bytes 2359300
  93.1 4.4 %collective-permute-start.10 = (bf16[2,4,48,1024]{3,2,1,0:T(8,128)(2,1)}, bf16[2,4,48,1024]{3,2,1,0:T(8,128)(2,1)S(1)}, u32[]{:S(2)}, u32[]{:S(2)}) collective-permute-start(bf16[2,4,48,1024]{3,2,1,0:T(8,128)(2,1)} %bitcast.25), channel_id=1, source_target_pairs={{8,0},{0,8},{24,16},{16,24},{40,32},{32,40},{56,48},{48,56},{72,64... | collective-permute-start | bytes 2359304 | tf_op jit(solution)/shard_map/ppermute | solution.py:229
  93.2 20.5 %collective-permute-start.11 = (bf16[2,4,48,1024]{3,2,1,0:T(8,128)(2,1)}, bf16[2,4,48,1024]{3,2,1,0:T(8,128)(2,1)S(1)}, u32[]{:S(2)}, u32[]{:S(2)}) collective-permute-start(bf16[2,4,48,1024]{3,2,1,0:T(8,128)(2,1)} %bitcast.24), channel_id=1, source_target_pairs={{48,0},{200,8},{0,16},{216,24},{16,32},{232,40},{32,48},{248,56},{... | collective-permute-start | bytes 2359304 | tf_op jit(solution)/shard_map/ppermute | solution.py:229
  93.3 22.7 %collective-permute-start.12 = (bf16[2,4,48,1024]{3,2,1,0:T(8,128)(2,1)}, bf16[2,4,48,1024]{3,2,1,0:T(8,128)(2,1)S(1)}, u32[]{:S(2)}, u32[]{:S(2)}) collective-permute-start(bf16[2,4,48,1024]{3,2,1,0:T(8,128)(2,1)} %bitcast.23), channel_id=1, source_target_pairs={{56,0},{192,8},{8,16},{208,24},{24,32},{224,40},{40,48},{240,56},{... | collective-permute-start | bytes 2359304 | tf_op jit(solution)/shard_map/ppermute | solution.py:229
  95.4 34.1 %collective-permute-start.13 = (bf16[2,4,48,1024]{3,2,1,0:T(8,128)(2,1)}, bf16[2,4,48,1024]{3,2,1,0:T(8,128)(2,1)S(1)}, u32[]{:S(2)}, u32[]{:S(2)}) collective-permute-start(bf16[2,4,48,1024]{3,2,1,0:T(8,128)(2,1)} %bitcast.22), channel_id=1, source_target_pairs={{32,0},{136,8},{48,16},{152,24},{0,32},{168,40},{16,48},{184,56},{... | collective-permute-start | bytes 2359304 | tf_op jit(solution)/shard_map/ppermute | solution.py:229
  96.9 34.3 %collective-permute-start.14 = (bf16[2,4,48,1024]{3,2,1,0:T(8,128)(2,1)}, bf16[2,4,48,1024]{3,2,1,0:T(8,128)(2,1)S(1)}, u32[]{:S(2)}, u32[]{:S(2)}) collective-permute-start(bf16[2,4,48,1024]{3,2,1,0:T(8,128)(2,1)} %bitcast.21), channel_id=1, source_target_pairs={{40,0},{128,8},{56,16},{144,24},{8,32},{160,40},{24,48},{176,56},{... | collective-permute-start | bytes 2359304 | tf_op jit(solution)/shard_map/ppermute | solution.py:229
  97.5 34.6 %collective-permute-start.15 = (bf16[2,4,48,1024]{3,2,1,0:T(8,128)(2,1)}, bf16[2,4,48,1024]{3,2,1,0:T(8,128)(2,1)S(1)}, u32[]{:S(2)}, u32[]{:S(2)}) collective-permute-start(bf16[2,4,48,1024]{3,2,1,0:T(8,128)(2,1)} %bitcast.20), channel_id=1, source_target_pairs={{16,0},{72,8},{32,16},{88,24},{48,32},{104,40},{0,48},{120,56},{80... | collective-permute-start | bytes 2359304 | tf_op jit(solution)/shard_map/ppermute | solution.py:229
  113.7 19.7 %collective-permute-start.16 = (bf16[2,4,48,1024]{3,2,1,0:T(8,128)(2,1)S(1)}, bf16[2,4,48,1024]{3,2,1,0:T(8,128)(2,1)S(1)}, u32[]{:S(2)}, u32[]{:S(2)}) collective-permute-start(bf16[2,4,48,1024]{3,2,1,0:T(8,128)(2,1)S(1)} %bitcast.19), channel_id=1, source_target_pairs={{24,0},{64,8},{40,16},{80,24},{56,32},{96,40},{8,48},{112,56},{88,... | collective-permute-start | bytes 2359304 | tf_op jit(solution)/shard_map/ppermute | solution.py:229
  135.9 13.8 %collective-permute-start.17 = (bf16[2,128,1024]{2,1,0:T(8,128)(2,1)S(1)}, bf16[2,128,1024]{2,1,0:T(8,128)(2,1)S(1)}, u32[]{:S(2)}, u32[]{:S(2)}) collective-permute-start(bf16[2,128,1024]{2,1,0:T(8,128)(2,1)S(1)} %get-tuple-element.47), channel_id=1, source_target_pairs={{64,0},{24,8},{80,16},{40,24},{96,32},{56,40},{112,48},{8,56},{128... | collective-permute-start | bytes 1572872 | tf_op jit(solution)/shard_map/ppermute | solution.py:229
  138.0 11.7 %collective-permute-start.18 = (bf16[2,128,1024]{2,1,0:T(8,128)(2,1)S(1)}, bf16[2,128,1024]{2,1,0:T(8,128)(2,1)S(1)}, u32[]{:S(2)}, u32[]{:S(2)}) collective-permute-start(bf16[2,128,1024]{2,1,0:T(8,128)(2,1)S(1)} %get-tuple-element.48), channel_id=1, source_target_pairs={{128,0},{40,8},{144,16},{56,24},{160,32},{8,40},{176,48},{24,56},{... | collective-permute-start | bytes 1572872 | tf_op jit(solution)/shard_map/ppermute | solution.py:229
  138.0 15.3 %collective-permute-start.19 = (bf16[2,128,1024]{2,1,0:T(8,128)(2,1)S(1)}, bf16[2,128,1024]{2,1,0:T(8,128)(2,1)S(1)}, u32[]{:S(2)}, u32[]{:S(2)}) collective-permute-start(bf16[2,128,1024]{2,1,0:T(8,128)(2,1)S(1)} %get-tuple-element.49), channel_id=1, source_target_pairs={{192,0},{56,8},{208,16},{8,24},{224,32},{24,40},{240,48},{40,56},{... | collective-permute-start | bytes 1572872 | tf_op jit(solution)/shard_map/ppermute | solution.py:229
Sparse Core Ops, SparseCore 0:
  9.8 63.5 all-gather.2
  93.2 61.2 reduce-scatter.1

commit v6 on v5

--- a/solution.py
+++ b/solution.py
@@ -11,6 +11,7 @@
 CAP = 24
 SIDE = 4
 CORES = 2
+SPARE = 8
 
 
 def call(kernel, name, out_shape, grid=None, in_specs=None, out_specs=None, scratch=(), flops=0, nbytes=0, vmem=16):
@@ -81,7 +82,8 @@
 def slots(first_ref, fact_ref, count, rank_ref, gate_ref, q):
     tok = rank_ref.shape[2]
     ids, weights = unbundle(fact_ref, tok)
-    rank_ref[q], gate_ref[q] = membership(ids, weights, rank_ref.shape[1])
+    experts = rank_ref.shape[1] - SPARE
+    rank_ref[q, :experts], gate_ref[q, :experts] = membership(ids, weights, experts)
     rank = jnp.concatenate([rank_ref[q, pl.ds(first_ref[p], 2), :] for p in range(count)], axis=0)
     gates = jnp.concatenate([gate_ref[q, pl.ds(first_ref[p], 2), :] for p in range(count)], axis=0)
     slot = lax.broadcasted_iota(jnp.int32, (rank.shape[0], CAP, tok), 1).astype(F32)
@@ -252,7 +254,7 @@
     bundles = [own] + [permute(own, target) for target in shared]
     chunk_shape = jax.ShapeDtypeStruct((2, local, SIDE * CAP, width), BF)
     pack_flops = 2 * experts * CAP * tok * width
-    table_scratch = pltpu.VMEM((SIDE, experts, tok), F32)
+    table_scratch = pltpu.VMEM((SIDE, experts + SPARE, tok), F32)
     packed = call(
         pack_kernel,
         "pack",

time: 164 us -> 164 us (level)
  no operation moved by 1% of the time
where the time goes in v6:
time: 164 us
  waiting for transfers between devices  88.8 us (54%)
  Pallas kernels  29.1 us (18%)
  starting transfers between devices  26.9 us (16%)
  between operations  14.2 us (9%)
  local copies, waits for them, and re-layouts  4.69 us (3%)
    ppermute x10, waiting for transfers between devices, restore(): return lax.ppermute(x, 'expert', [(target(n), n) for n in everyone])  46.3 us
    ppermute x10, waiting for transfers between devices, permute(): return lax.ppermute(x, 'expert', [(n, target(n)) for n in everyone])  41.2 us
    pallas_call x1, Pallas kernels, shards(): call(functools.partial(expert_kernel, count), 'expert', [back_shape] * co...  17.4 us
    ppermute x10, starting transfers between devices, permute(): return lax.ppermute(x, 'expert', [(n, target(n)) for n in everyone])  15.5 us
    ppermute x10, starting transfers between devices, restore(): return lax.ppermute(x, 'expert', [(target(n), n) for n in everyone])  11.3 us
    unnamed x24, local copies, waits for them, and re-layouts  4 us
    pallas_call x1, Pallas kernels, shards(): call(pack_kernel, 'pack', [pltpu.VMEM(chunk_shape.shape, BF)] * count, in...  3.45 us
  transfers between devices with their start and end apart: 22, of which 15 were waited for; matrix products, arithmetic and copies ran while one was open for 0% of the time, Pallas kernels for 4%

profile of v6, /device:TPU:1, one launch (start us, length us, event | category | flops | bytes accessed | tf_op | source)
XLA Modules:
  0.0 163.6 jit_solution(5536442567002445220)
XLA Ops:
  7.2 0.0 all-gather.3.cloned.1.call-start
  7.2 2.3 %head.1 = (bf16[2,192,768]{2,1,0:T(8,128)(2,1)}, bf16[272,1024]{1,0:T(8,128)(2,1)}) custom-call(s32[8,128]{1,0:T(8,128)} %bitcast.16, f32[8,128]{1,0:T(8,128)} %bitcast.17, bf16[128,1024]{1,0:T(8,128)(2,1)} %tokens_ref.1, bf16[128,1024]{1,0:T(8,128)(2,1)} %cot_ref.1, bf16[2,128,768]{2,1,0:T(8,128)(2,1)} %lift_ref.1, bf16[2,384,128]{2,1,0:T(8,128)(2,1)} %down_ref.1), custom_call_target="tpu_custom_call" | custom-call | bytes 2097152 | tf_op jit(solution)/shard_map/head/pallas_call | solution.py:240
  9.6 0.0 reduce-scatter.2.cloned.1.call-start
  9.6 3.6 %collective-permute-start.2 = (bf16[272,1024]{1,0:T(8,128)(2,1)}, bf16[272,1024]{1,0:T(8,128)(2,1)S(1)}, u32[]{:S(2)}, u32[]{:S(2)}) collective-permute-start(bf16[272,1024]{1,0:T(8,128)(2,1)} %get-tuple-element.27.refs_0_), channel_id=1, source_target_pairs={{0,192},{8,56},{16,208},{24,8},{32,224},{40,24},{48,240},{56,40},{... | collective-permute-start | bytes 1671176 | tf_op jit(solution)/shard_map/ppermute | solution.py:222
  13.3 0.3 collective-permute-start.1
  13.6 0.7 collective-permute-start
  14.3 0.7 dynamic-slice_bitcast_fusion.first_ref
  15.0 11.0 %collective-permute-done.2.refs_3_ = bf16[272,1024]{1,0:T(8,128)(2,1)S(1)} collective-permute-done((bf16[272,1024]{1,0:T(8,128)(2,1)}, bf16[272,1024]{1,0:T(8,128)(2,1)S(1)}, u32[]{:S(2)}, u32[]{:S(2)}) %collective-permute-start.2) | collective-permute-done | bytes 557088 | tf_op jit(solution)/shard_map/ppermute | solution.py:222
  26.0 3.7 %collective-permute-done.refs_1_ = bf16[272,1024]{1,0:T(8,128)(2,1)S(1)} collective-permute-done((bf16[272,1024]{1,0:T(8,128)(2,1)}, bf16[272,1024]{1,0:T(8,128)(2,1)S(1)}, u32[]{:S(2)}, u32[]{:S(2)}) %collective-permute-start) | collective-permute-done | bytes 557088 | tf_op jit(solution)/shard_map/ppermute | solution.py:222
  29.7 3.4 %pack.1 = (bf16[2,2,96,1024]{3,2,1,0:T(8,128)(2,1)S(1)}, bf16[2,2,96,1024]{3,2,1,0:T(8,128)(2,1)S(1)}, bf16[2,2,96,1024]{3,2,1,0:T(8,128)(2,1)S(1)}, bf16[2,2,96...) custom-call(s32[8]{0:T(128)S(1)} %dynamic-slice_bitcast_fusion.first, ...), custom_call_target="tpu_custom_call" | custom-call | flops 805306368 | bytes 16777216 | tf_op jit(solution)/shard_map/pack/pallas_call | solution.py:258
  33.2 1.5 collective-permute-start.3
  34.7 0.6 collective-permute-start.5
  35.3 2.5 %collective-permute-start.6 = (bf16[2,2,96,1024]{3,2,1,0:T(8,128)(2,1)S(1)}, bf16[2,2,96,1024]{3,2,1,0:T(8,128)(2,1)S(1)}, u32[]{:S(2)}, u32[]{:S(2)}) collective-permute-start(bf16[2,2,96,1024]{3,2,1,0:T(8,128)(2,1)S(1)} %get-tuple-element.32), channel_id=1, source_target_pairs={{0,32},{8,136},{16,48},{24,152},{32,0},{40,168},{48,16},{56,184},{... | collective-permute-start | bytes 2359304 | tf_op jit(solution)/shard_map/ppermute | solution.py:222
  37.8 2.9 %collective-permute-start.7 = (bf16[2,2,96,1024]{3,2,1,0:T(8,128)(2,1)S(1)}, bf16[2,2,96,1024]{3,2,1,0:T(8,128)(2,1)S(1)}, u32[]{:S(2)}, u32[]{:S(2)}) collective-permute-start(bf16[2,2,96,1024]{3,2,1,0:T(8,128)(2,1)S(1)} %get-tuple-element.33), channel_id=1, source_target_pairs={{0,40},{8,128},{16,56},{24,144},{32,8},{40,160},{48,24},{56,176},{... | collective-permute-start | bytes 2359304 | tf_op jit(solution)/shard_map/ppermute | solution.py:222
  40.7 1.1 collective-permute-start.8
  41.8 5.4 %collective-permute-done.4.refs_2_ = bf16[2,2,96,1024]{3,2,1,0:T(8,128)(2,1)S(1)} collective-permute-done((bf16[2,2,96,1024]{3,2,1,0:T(8,128)(2,1)S(1)}, bf16[2,2,96,1024]{3,2,1,0:T(8,128)(2,1)S(1)}, u32[]{:S(2)}, u32[]{:S(2)}) %collective-permute-start.4) | collective-permute-done | bytes 786464 | tf_op jit(solution)/shard_map/ppermute | solution.py:222
  47.2 2.2 %collective-permute-start.9 = (bf16[2,2,96,1024]{3,2,1,0:T(8,128)(2,1)S(1)}, bf16[2,2,96,1024]{3,2,1,0:T(8,128)(2,1)}, u32[]{:S(2)}, u32[]{:S(2)}) collective-permute-start(bf16[2,2,96,1024]{3,2,1,0:T(8,128)(2,1)S(1)} %get-tuple-element.35), channel_id=1, source_target_pairs={{0,56},{8,192},{16,8},{24,208},{32,24},{40,224},{48,40},{56,240},{... | collective-permute-start | bytes 2359304 | tf_op jit(solution)/shard_map/ppermute | solution.py:222
  49.4 1.1 copy-done.4
  50.4 1.2 plan.1.refs_9_.pick_ref
  51.6 1.1 copy-done
  52.7 3.4 %collective-permute-done.5.refs_3_ = bf16[2,2,96,1024]{3,2,1,0:T(8,128)(2,1)S(1)} collective-permute-done((bf16[2,2,96,1024]{3,2,1,0:T(8,128)(2,1)S(1)}, bf16[2,2,96,1024]{3,2,1,0:T(8,128)(2,1)S(1)}, u32[]{:S(2)}, u32[]{:S(2)}) %collective-permute-start.5) | collective-permute-done | bytes 786464 | tf_op jit(solution)/shard_map/ppermute | solution.py:222
  56.1 7.4 %collective-permute-done.6.refs_4_ = bf16[2,2,96,1024]{3,2,1,0:T(8,128)(2,1)S(1)} collective-permute-done((bf16[2,2,96,1024]{3,2,1,0:T(8,128)(2,1)S(1)}, bf16[2,2,96,1024]{3,2,1,0:T(8,128)(2,1)S(1)}, u32[]{:S(2)}, u32[]{:S(2)}) %collective-permute-start.6) | collective-permute-done | bytes 786464 | tf_op jit(solution)/shard_map/ppermute | solution.py:222
  63.6 10.2 %collective-permute-done.7.refs_5_ = bf16[2,2,96,1024]{3,2,1,0:T(8,128)(2,1)S(1)} collective-permute-done((bf16[2,2,96,1024]{3,2,1,0:T(8,128)(2,1)S(1)}, bf16[2,2,96,1024]{3,2,1,0:T(8,128)(2,1)S(1)}, u32[]{:S(2)}, u32[]{:S(2)}) %collective-permute-start.7) | collective-permute-done | bytes 786464 | tf_op jit(solution)/shard_map/ppermute | solution.py:222
  73.9 0.9 copy-done.10
  74.7 0.9 copy-done.11
  75.7 17.4 %expert.1 = (bf16[2,4,2,24,1024]{4,3,2,1,0:T(8,128)(2,1)}, bf16[2,4,2,24,1024]{4,3,2,1,0:T(8,128)(2,1)}, bf16[2,4,2,24,1024]{4,3,2,1,0:T(8,128)(2,1)}, bf16[2,4,...) custom-call(bf16[2,2,96,1024]{3,2,1,0:T(8,128)(2,1)} %copy-done.2, ...), custom_call_target="tpu_custom_call" | custom-call | flops 10871635968 | bytes 25165824 | tf_op jit(solution)/shard_map/expert/pallas_call | solution.py:288
  93.1 0.0 reduce-scatter.2.cloned.1.call-update
  93.1 0.1 collective-permute-start.10
  93.2 0.1 collective-permute-start.11
  93.3 2.1 %collective-permute-start.12 = (bf16[2,4,48,1024]{3,2,1,0:T(8,128)(2,1)}, bf16[2,4,48,1024]{3,2,1,0:T(8,128)(2,1)S(1)}, u32[]{:S(2)}, u32[]{:S(2)}) collective-permute-start(bf16[2,4,48,1024]{3,2,1,0:T(8,128)(2,1)} %bitcast.23), channel_id=1, source_target_pairs={{56,0},{192,8},{8,16},{208,24},{24,32},{224,40},{40,48},{240,56},{... | collective-permute-start | bytes 2359304 | tf_op jit(solution)/shard_map/ppermute | solution.py:231
  95.4 1.5 collective-permute-start.13
  96.9 0.5 collective-permute-start.14
  97.5 2.6 %collective-permute-start.15 = (bf16[2,4,48,1024]{3,2,1,0:T(8,128)(2,1)}, bf16[2,4,48,1024]{3,2,1,0:T(8,128)(2,1)S(1)}, u32[]{:S(2)}, u32[]{:S(2)}) collective-permute-start(bf16[2,4,48,1024]{3,2,1,0:T(8,128)(2,1)} %bitcast.20), channel_id=1, source_target_pairs={{16,0},{72,8},{32,16},{88,24},{48,32},{104,40},{0,48},{120,56},{80... | collective-permute-start | bytes 2359304 | tf_op jit(solution)/shard_map/ppermute | solution.py:231
  100.1 13.6 %collective-permute-done.11.refs_2_ = bf16[2,4,48,1024]{3,2,1,0:T(8,128)(2,1)S(1)} collective-permute-done((bf16[2,4,48,1024]{3,2,1,0:T(8,128)(2,1)}, bf16[2,4,48,1024]{3,2,1,0:T(8,128)(2,1)S(1)}, u32[]{:S(2)}, u32[]{:S(2)}) %collective-permute-start.11) | collective-permute-done | bytes 786464 | tf_op jit(solution)/shard_map/ppermute | solution.py:231
  113.7 1.6 collective-permute-start.16
  115.3 0.7 collective-permute-done.12.refs_3_
  116.0 13.6 %collective-permute-done.13.refs_4_ = bf16[2,4,48,1024]{3,2,1,0:T(8,128)(2,1)S(1)} collective-permute-done((bf16[2,4,48,1024]{3,2,1,0:T(8,128)(2,1)}, bf16[2,4,48,1024]{3,2,1,0:T(8,128)(2,1)S(1)}, u32[]{:S(2)}, u32[]{:S(2)}) %collective-permute-start.13) | collective-permute-done | bytes 786464 | tf_op jit(solution)/shard_map/ppermute | solution.py:231
  129.5 1.7 %collective-permute-done.14.refs_5_ = bf16[2,4,48,1024]{3,2,1,0:T(8,128)(2,1)S(1)} collective-permute-done((bf16[2,4,48,1024]{3,2,1,0:T(8,128)(2,1)}, bf16[2,4,48,1024]{3,2,1,0:T(8,128)(2,1)S(1)}, u32[]{:S(2)}, u32[]{:S(2)}) %collective-permute-start.14) | collective-permute-done | bytes 786464 | tf_op jit(solution)/shard_map/ppermute | solution.py:231
  131.3 0.9 collective-permute-done.15.refs_6_
  132.1 1.2 collective-permute-done.16.refs_7_
  133.4 2.5 %combine.1 = (f32[2,128,1024]{2,1,0:T(8,128)S(1)}, bf16[2,128,1024]{2,1,0:T(8,128)(2,1)S(1)}, bf16[2,128,1024]{2,1,0:T(8,128)(2,1)S(1)}, bf16[2,128,1024]{2,1,0:T(8,128)(2,1)S(1)}) custom-call(bf16[2,4,256,384]{3,2,1,0:T(8,128)(2,1)S(1)} %copy-done.1, bf16[2,4,48,1024]{3,2,1,0:T(8,128)(2,1)S(1)} %bitcast.14, ...), custom_call_target="tpu_custom_call" | custom-call | flops 1610612736 | bytes 10485760 | tf_op jit(solution)/shard_map/combine/pallas_call | solution.py:307
  135.9 2.1 %collective-permute-start.17 = (bf16[2,128,1024]{2,1,0:T(8,128)(2,1)S(1)}, bf16[2,128,1024]{2,1,0:T(8,128)(2,1)S(1)}, u32[]{:S(2)}, u32[]{:S(2)}) collective-permute-start(bf16[2,128,1024]{2,1,0:T(8,128)(2,1)S(1)} %get-tuple-element.47), channel_id=1, source_target_pairs={{64,0},{24,8},{80,16},{40,24},{96,32},{56,40},{112,48},{8,56},{128... | collective-permute-start | bytes 1572872 | tf_op jit(solution)/shard_map/ppermute | solution.py:231
  138.0 0.0 collective-permute-start.18
  138.0 0.6 collective-permute-start.19
  138.7 11.1 %collective-permute-done.17.refs_0_ = bf16[2,128,1024]{2,1,0:T(8,128)(2,1)S(1)} collective-permute-done((bf16[2,128,1024]{2,1,0:T(8,128)(2,1)S(1)}, bf16[2,128,1024]{2,1,0:T(8,128)(2,1)S(1)}, u32[]{:S(2)}, u32[]{:S(2)}) %collective-permute-start.17) | collective-permute-done | bytes 524320 | tf_op jit(solution)/shard_map/ppermute | solution.py:231
  149.7 3.5 %collective-permute-done.19.refs_2_ = bf16[2,128,1024]{2,1,0:T(8,128)(2,1)S(1)} collective-permute-done((bf16[2,128,1024]{2,1,0:T(8,128)(2,1)S(1)}, bf16[2,128,1024]{2,1,0:T(8,128)(2,1)S(1)}, u32[]{:S(2)}, u32[]{:S(2)}) %collective-permute-start.19) | collective-permute-done | bytes 524320 | tf_op jit(solution)/shard_map/ppermute | solution.py:231
  153.3 1.3 reduce-scatter.2.cloned.1.call-done
  154.5 2.2 %final.1 = (bf16[128,1024]{1,0:T(8,128)(2,1)}, bf16[128,1024]{1,0:T(8,128)(2,1)}, bf16[2,128,768]{2,1,0:T(8,128)(2,1)}, bf16[2,384,128]{2,1,0:T(8,128)(2,1)}) custom-call(bf16[2,192,768]{2,1,0:T(8,128)(2,1)} %bitcast.15, f32[2,128,1024]{2,1,0:T(8,128)S(1)} %get-tuple-element.46.own_ref, bf16[2,128,1024]{2,1,0:T(8,128)(2,1)S(1)} %collective-permute-done.17.refs_0_, ...), custom_call_target="tpu_custom_call" | custom-call | bytes 4194304 | tf_op jit(solution)/shard_map/final/pallas_call | solution.py:320
  (29 shorter events, 0.1 us)
Async XLA Ops:
  7.2 68.5 %all-gather.3.cloned.1.call-start = ((), (), s32[]{:S(2)}) async-start(), calls=%async_computation.2 | async-start | bytes 5308416 | tf_op jit(solution)/shard_map/all_gather | solution.py:252
  9.6 145.0 %reduce-scatter.2.cloned.1.call-start = ((), (), s32[]{:S(2)}) async-start(), calls=%async_computation.1 | async-start | bytes 5308416 | tf_op jit(solution)/shard_map/reduce_scatter | solution.py:301
  9.6 16.4 %collective-permute-start.2 = (bf16[272,1024]{1,0:T(8,128)(2,1)}, bf16[272,1024]{1,0:T(8,128)(2,1)S(1)}, u32[]{:S(2)}, u32[]{:S(2)}) collective-permute-start(bf16[272,1024]{1,0:T(8,128)(2,1)} %get-tuple-element.27.refs_0_), channel_id=1, source_target_pairs={{0,192},{8,56},{16,208},{24,8},{32,224},{40,24},{48,240},{56,40},{... | collective-permute-start | bytes 1671176 | tf_op jit(solution)/shard_map/ppermute | solution.py:222
  13.3 12.8 %collective-permute-start.1 = (bf16[272,1024]{1,0:T(8,128)(2,1)}, bf16[272,1024]{1,0:T(8,128)(2,1)S(1)}, u32[]{:S(2)}, u32[]{:S(2)}) collective-permute-start(bf16[272,1024]{1,0:T(8,128)(2,1)} %get-tuple-element.27.refs_0_), channel_id=1, source_target_pairs={{0,128},{8,40},{16,144},{24,56},{32,160},{40,8},{48,176},{56,24},{... | collective-permute-start | bytes 1671176 | tf_op jit(solution)/shard_map/ppermute | solution.py:222
  13.6 16.1 %collective-permute-start = (bf16[272,1024]{1,0:T(8,128)(2,1)}, bf16[272,1024]{1,0:T(8,128)(2,1)S(1)}, u32[]{:S(2)}, u32[]{:S(2)}) collective-permute-start(bf16[272,1024]{1,0:T(8,128)(2,1)} %get-tuple-element.27.refs_0_), channel_id=1, source_target_pairs={{0,64},{8,24},{16,80},{24,40},{32,96},{40,56},{48,112},{56,8},{64,... | collective-permute-start | bytes 1671176 | tf_op jit(solution)/shard_map/ppermute | solution.py:222
  33.2 42.5 %copy-start.2 = (bf16[2,2,96,1024]{3,2,1,0:T(8,128)(2,1)}, bf16[2,2,96,1024]{3,2,1,0:T(8,128)(2,1)S(1)}, u32[]{:S(2)}) copy-start(bf16[2,2,96,1024]{3,2,1,0:T(8,128)(2,1)S(1)} %get-tuple-element.28.refs_4_.refs_0_) | copy-start | bytes 2359300
  33.2 7.5 %collective-permute-start.3 = (bf16[2,2,96,1024]{3,2,1,0:T(8,128)(2,1)S(1)}, bf16[2,2,96,1024]{3,2,1,0:T(8,128)(2,1)S(1)}, u32[]{:S(2)}, u32[]{:S(2)}) collective-permute-start(bf16[2,2,96,1024]{3,2,1,0:T(8,128)(2,1)S(1)} %get-tuple-element.29), channel_id=1, source_target_pairs={{0,8},{8,0},{16,24},{24,16},{32,40},{40,32},{48,56},{56,48},{64,72... | collective-permute-start | bytes 2359304 | tf_op jit(solution)/shard_map/ppermute | solution.py:222
  34.7 12.5 %collective-permute-start.4 = (bf16[2,2,96,1024]{3,2,1,0:T(8,128)(2,1)S(1)}, bf16[2,2,96,1024]{3,2,1,0:T(8,128)(2,1)S(1)}, u32[]{:S(2)}, u32[]{:S(2)}) collective-permute-start(bf16[2,2,96,1024]{3,2,1,0:T(8,128)(2,1)S(1)} %get-tuple-element.30), channel_id=1, source_target_pairs={{0,16},{8,72},{16,32},{24,88},{32,48},{40,104},{48,0},{56,120},{64... | collective-permute-start | bytes 2359304 | tf_op jit(solution)/shard_map/ppermute | solution.py:222
  34.7 21.4 %collective-permute-start.5 = (bf16[2,2,96,1024]{3,2,1,0:T(8,128)(2,1)S(1)}, bf16[2,2,96,1024]{3,2,1,0:T(8,128)(2,1)S(1)}, u32[]{:S(2)}, u32[]{:S(2)}) collective-permute-start(bf16[2,2,96,1024]{3,2,1,0:T(8,128)(2,1)S(1)} %get-tuple-element.31), channel_id=1, source_target_pairs={{0,24},{8,64},{16,40},{24,80},{32,56},{40,96},{48,8},{56,112},{64,... | collective-permute-start | bytes 2359304 | tf_op jit(solution)/shard_map/ppermute | solution.py:222
  35.3 28.3 %collective-permute-start.6 = (bf16[2,2,96,1024]{3,2,1,0:T(8,128)(2,1)S(1)}, bf16[2,2,96,1024]{3,2,1,0:T(8,128)(2,1)S(1)}, u32[]{:S(2)}, u32[]{:S(2)}) collective-permute-start(bf16[2,2,96,1024]{3,2,1,0:T(8,128)(2,1)S(1)} %get-tuple-element.32), channel_id=1, source_target_pairs={{0,32},{8,136},{16,48},{24,152},{32,0},{40,168},{48,16},{56,184},{... | collective-permute-start | bytes 2359304 | tf_op jit(solution)/shard_map/ppermute | solution.py:222
  37.8 36.1 %collective-permute-start.7 = (bf16[2,2,96,1024]{3,2,1,0:T(8,128)(2,1)S(1)}, bf16[2,2,96,1024]{3,2,1,0:T(8,128)(2,1)S(1)}, u32[]{:S(2)}, u32[]{:S(2)}) collective-permute-start(bf16[2,2,96,1024]{3,2,1,0:T(8,128)(2,1)S(1)} %get-tuple-element.33), channel_id=1, source_target_pairs={{0,40},{8,128},{16,56},{24,144},{32,8},{40,160},{48,24},{56,176},{... | collective-permute-start | bytes 2359304 | tf_op jit(solution)/shard_map/ppermute | solution.py:222
  40.7 34.9 %copy-start.5 = (bf16[2,2,96,1024]{3,2,1,0:T(8,128)(2,1)}, bf16[2,2,96,1024]{3,2,1,0:T(8,128)(2,1)S(1)}, u32[]{:S(2)}) copy-start(bf16[2,2,96,1024]{3,2,1,0:T(8,128)(2,1)S(1)} %collective-permute-done.3.refs_1_) | copy-start | bytes 2359300
  40.7 33.1 %collective-permute-start.8 = (bf16[2,2,96,1024]{3,2,1,0:T(8,128)(2,1)S(1)}, bf16[2,2,96,1024]{3,2,1,0:T(8,128)(2,1)S(1)}, u32[]{:S(2)}, u32[]{:S(2)}) collective-permute-start(bf16[2,2,96,1024]{3,2,1,0:T(8,128)(2,1)S(1)} %get-tuple-element.34), channel_id=1, source_target_pairs={{0,48},{8,200},{16,0},{24,216},{32,16},{40,232},{48,32},{56,248},{... | collective-permute-start | bytes 2359304 | tf_op jit(solution)/shard_map/ppermute | solution.py:222
  47.2 26.7 %copy-start.6 = (bf16[2,2,96,1024]{3,2,1,0:T(8,128)(2,1)}, bf16[2,2,96,1024]{3,2,1,0:T(8,128)(2,1)S(1)}, u32[]{:S(2)}) copy-start(bf16[2,2,96,1024]{3,2,1,0:T(8,128)(2,1)S(1)} %collective-permute-done.4.refs_2_) | copy-start | bytes 2359300
  47.2 28.5 %collective-permute-start.9 = (bf16[2,2,96,1024]{3,2,1,0:T(8,128)(2,1)S(1)}, bf16[2,2,96,1024]{3,2,1,0:T(8,128)(2,1)}, u32[]{:S(2)}, u32[]{:S(2)}) collective-permute-start(bf16[2,2,96,1024]{3,2,1,0:T(8,128)(2,1)S(1)} %get-tuple-element.35), channel_id=1, source_target_pairs={{0,56},{8,192},{16,8},{24,208},{32,24},{40,224},{48,40},{56,240},{... | collective-permute-start | bytes 2359304 | tf_op jit(solution)/shard_map/ppermute | solution.py:222
  49.4 1.1 copy-start.4
  51.6 1.1 copy-start
  56.1 17.7 %copy-start.8 = (bf16[2,2,96,1024]{3,2,1,0:T(8,128)(2,1)}, bf16[2,2,96,1024]{3,2,1,0:T(8,128)(2,1)S(1)}, u32[]{:S(2)}) copy-start(bf16[2,2,96,1024]{3,2,1,0:T(8,128)(2,1)S(1)} %collective-permute-done.5.refs_3_) | copy-start | bytes 2359300
  63.6 10.3 %copy-start.9 = (bf16[2,2,96,1024]{3,2,1,0:T(8,128)(2,1)}, bf16[2,2,96,1024]{3,2,1,0:T(8,128)(2,1)S(1)}, u32[]{:S(2)}) copy-start(bf16[2,2,96,1024]{3,2,1,0:T(8,128)(2,1)S(1)} %collective-permute-done.6.refs_4_) | copy-start | bytes 2359300
  73.8 0.9 copy-start.10
  74.7 0.9 copy-start.11
  93.1 20.6 %copy-start.7 = (bf16[2,4,2,24,1024]{4,3,2,1,0:T(8,128)(2,1)S(1)}, bf16[2,4,2,24,1024]{4,3,2,1,0:T(8,128)(2,1)}, u32[]{:S(2)}) copy-start(bf16[2,4,2,24,1024]{4,3,2,1,0:T(8,128)(2,1)} %get-tuple-element.45) | copy-start | bytes 2359300
  93.1 40.3 %copy-start.1 = (bf16[2,4,256,384]{3,2,1,0:T(8,128)(2,1)S(1)}, bf16[2,4,256,384]{3,2,1,0:T(8,128)(2,1)}, u32[]{:S(2)}) copy-start(bf16[2,4,256,384]{3,2,1,0:T(8,128)(2,1)} %copy-done) | copy-start | bytes 4718596
  93.1 40.3 %copy-start.3 = (bf16[2,4,2,24,1024]{4,3,2,1,0:T(8,128)(2,1)S(1)}, bf16[2,4,2,24,1024]{4,3,2,1,0:T(8,128)(2,1)}, u32[]{:S(2)}) copy-start(bf16[2,4,2,24,1024]{4,3,2,1,0:T(8,128)(2,1)} %get-tuple-element.38) | copy-start | bytes 2359300
  93.1 4.4 %collective-permute-start.10 = (bf16[2,4,48,1024]{3,2,1,0:T(8,128)(2,1)}, bf16[2,4,48,1024]{3,2,1,0:T(8,128)(2,1)S(1)}, u32[]{:S(2)}, u32[]{:S(2)}) collective-permute-start(bf16[2,4,48,1024]{3,2,1,0:T(8,128)(2,1)} %bitcast.25), channel_id=1, source_target_pairs={{8,0},{0,8},{24,16},{16,24},{40,32},{32,40},{56,48},{48,56},{72,64... | collective-permute-start | bytes 2359304 | tf_op jit(solution)/shard_map/ppermute | solution.py:231
  93.2 20.4 %collective-permute-start.11 = (bf16[2,4,48,1024]{3,2,1,0:T(8,128)(2,1)}, bf16[2,4,48,1024]{3,2,1,0:T(8,128)(2,1)S(1)}, u32[]{:S(2)}, u32[]{:S(2)}) collective-permute-start(bf16[2,4,48,1024]{3,2,1,0:T(8,128)(2,1)} %bitcast.24), channel_id=1, source_target_pairs={{48,0},{200,8},{0,16},{216,24},{16,32},{232,40},{32,48},{248,56},{... | collective-permute-start | bytes 2359304 | tf_op jit(solution)/shard_map/ppermute | solution.py:231
  93.3 22.7 %collective-permute-start.12 = (bf16[2,4,48,1024]{3,2,1,0:T(8,128)(2,1)}, bf16[2,4,48,1024]{3,2,1,0:T(8,128)(2,1)S(1)}, u32[]{:S(2)}, u32[]{:S(2)}) collective-permute-start(bf16[2,4,48,1024]{3,2,1,0:T(8,128)(2,1)} %bitcast.23), channel_id=1, source_target_pairs={{56,0},{192,8},{8,16},{208,24},{24,32},{224,40},{40,48},{240,56},{... | collective-permute-start | bytes 2359304 | tf_op jit(solution)/shard_map/ppermute | solution.py:231
  95.4 34.1 %collective-permute-start.13 = (bf16[2,4,48,1024]{3,2,1,0:T(8,128)(2,1)}, bf16[2,4,48,1024]{3,2,1,0:T(8,128)(2,1)S(1)}, u32[]{:S(2)}, u32[]{:S(2)}) collective-permute-start(bf16[2,4,48,1024]{3,2,1,0:T(8,128)(2,1)} %bitcast.22), channel_id=1, source_target_pairs={{32,0},{136,8},{48,16},{152,24},{0,32},{168,40},{16,48},{184,56},{... | collective-permute-start | bytes 2359304 | tf_op jit(solution)/shard_map/ppermute | solution.py:231
  96.9 34.3 %collective-permute-start.14 = (bf16[2,4,48,1024]{3,2,1,0:T(8,128)(2,1)}, bf16[2,4,48,1024]{3,2,1,0:T(8,128)(2,1)S(1)}, u32[]{:S(2)}, u32[]{:S(2)}) collective-permute-start(bf16[2,4,48,1024]{3,2,1,0:T(8,128)(2,1)} %bitcast.21), channel_id=1, source_target_pairs={{40,0},{128,8},{56,16},{144,24},{8,32},{160,40},{24,48},{176,56},{... | collective-permute-start | bytes 2359304 | tf_op jit(solution)/shard_map/ppermute | solution.py:231
  97.5 34.6 %collective-permute-start.15 = (bf16[2,4,48,1024]{3,2,1,0:T(8,128)(2,1)}, bf16[2,4,48,1024]{3,2,1,0:T(8,128)(2,1)S(1)}, u32[]{:S(2)}, u32[]{:S(2)}) collective-permute-start(bf16[2,4,48,1024]{3,2,1,0:T(8,128)(2,1)} %bitcast.20), channel_id=1, source_target_pairs={{16,0},{72,8},{32,16},{88,24},{48,32},{104,40},{0,48},{120,56},{80... | collective-permute-start | bytes 2359304 | tf_op jit(solution)/shard_map/ppermute | solution.py:231
  113.7 19.7 %collective-permute-start.16 = (bf16[2,4,48,1024]{3,2,1,0:T(8,128)(2,1)S(1)}, bf16[2,4,48,1024]{3,2,1,0:T(8,128)(2,1)S(1)}, u32[]{:S(2)}, u32[]{:S(2)}) collective-permute-start(bf16[2,4,48,1024]{3,2,1,0:T(8,128)(2,1)S(1)} %bitcast.19), channel_id=1, source_target_pairs={{24,0},{64,8},{40,16},{80,24},{56,32},{96,40},{8,48},{112,56},{88,... | collective-permute-start | bytes 2359304 | tf_op jit(solution)/shard_map/ppermute | solution.py:231
  135.9 13.8 %collective-permute-start.17 = (bf16[2,128,1024]{2,1,0:T(8,128)(2,1)S(1)}, bf16[2,128,1024]{2,1,0:T(8,128)(2,1)S(1)}, u32[]{:S(2)}, u32[]{:S(2)}) collective-permute-start(bf16[2,128,1024]{2,1,0:T(8,128)(2,1)S(1)} %get-tuple-element.47), channel_id=1, source_target_pairs={{64,0},{24,8},{80,16},{40,24},{96,32},{56,40},{112,48},{8,56},{128... | collective-permute-start | bytes 1572872 | tf_op jit(solution)/shard_map/ppermute | solution.py:231
  138.0 11.7 %collective-permute-start.18 = (bf16[2,128,1024]{2,1,0:T(8,128)(2,1)S(1)}, bf16[2,128,1024]{2,1,0:T(8,128)(2,1)S(1)}, u32[]{:S(2)}, u32[]{:S(2)}) collective-permute-start(bf16[2,128,1024]{2,1,0:T(8,128)(2,1)S(1)} %get-tuple-element.48), channel_id=1, source_target_pairs={{128,0},{40,8},{144,16},{56,24},{160,32},{8,40},{176,48},{24,56},{... | collective-permute-start | bytes 1572872 | tf_op jit(solution)/shard_map/ppermute | solution.py:231
  138.0 15.3 %collective-permute-start.19 = (bf16[2,128,1024]{2,1,0:T(8,128)(2,1)S(1)}, bf16[2,128,1024]{2,1,0:T(8,128)(2,1)S(1)}, u32[]{:S(2)}, u32[]{:S(2)}) collective-permute-start(bf16[2,128,1024]{2,1,0:T(8,128)(2,1)S(1)} %get-tuple-element.49), channel_id=1, source_target_pairs={{192,0},{56,8},{208,16},{8,24},{224,32},{24,40},{240,48},{40,56},{... | collective-permute-start | bytes 1572872 | tf_op jit(solution)/shard_map/ppermute | solution.py:231
Sparse Core Ops, SparseCore 0:
  9.8 63.5 all-gather.2
  93.2 61.2 reduce-scatter.1

commit v7 on v6

--- a/solution.py
+++ b/solution.py
@@ -128,12 +128,15 @@
         out[0] = (parts[:tok] + parts[tok:]).astype(out.dtype)
 
 
-def final_kernel(sum_ref, own_ref, *refs):
-    others, outs, (lift_ref, down_ref) = refs[: SIDE - 1], refs[SIDE - 1 : -2], refs[-2:]
+def split_kernel(sum_ref, lift_ref, down_ref):
     for e in range(lift_ref.shape[0]):
         lift_ref[e] = sum_ref[e, :128]
         for row, col in down_pieces():
             down_ref[e, row : row + 64] = sum_ref[e, 128:, col : col + 128]
+
+
+def total_kernel(own_ref, *refs):
+    others, outs = refs[: SIDE - 1], refs[SIDE - 1 :]
     for which, out in enumerate(outs):
         total = own_ref[which]
         for ref in others:
@@ -317,19 +320,23 @@
     )(picks, *parts)
     sums = list(sums[:1]) + [restore(x, target) for x, target in zip(sums[1:], shared)]
     token_shape = jax.ShapeDtypeStruct((tok, width), BF)
-    return call(
-        final_kernel,
-        "final",
-        [
-            token_shape,
-            token_shape,
-            jax.ShapeDtypeStruct(lift_weights.shape, BF),
-            jax.ShapeDtypeStruct(down_weights.shape, BF),
-        ],
-        in_specs=[vm] * (SIDE + 1),
-        out_specs=[vm] * 4,
-        nbytes=4 << 20,
-    )(offchip(summed), *sums)
+    layer_output, token_grads = call(
+        total_kernel,
+        "total",
+        [token_shape, token_shape],
+        in_specs=[vm] * SIDE,
+        out_specs=[vm] * 2,
+        nbytes=3 << 20,
+    )(*sums)
+    lift_grads, down_grads = call(
+        split_kernel,
+        "split",
+        [jax.ShapeDtypeStruct(lift_weights.shape, BF), jax.ShapeDtypeStruct(down_weights.shape, BF)],
+        in_specs=[vm],
+        out_specs=[vm] * 2,
+        nbytes=1 << 20,
+    )(offchip(summed))
+    return (layer_output, token_grads, lift_grads, down_grads)
 
 
 def solution(mesh):

time: 164 us -> 164 us (level)
  transfers between devices with their start and end apart: 22 -> 22, of which waited for: 15 -> 15; matrix products, arithmetic and copies ran while one was open for 0% -> 0% of each run, Pallas kernels for 4% -> 5%
where the time goes in v7:
time: 164 us; the launch traced here: 163 us
  waiting for transfers between devices  87.8 us (54%)
  Pallas kernels  29.7 us (18%)
  starting transfers between devices  26.9 us (16%)
  between operations  14.2 us (9%)
  local copies, waits for them, and re-layouts  4.68 us (3%)
    ppermute x10, waiting for transfers between devices, restore(): return lax.ppermute(x, 'expert', [(target(n), n) for n in everyone])  46.3 us
    ppermute x10, waiting for transfers between devices, permute(): return lax.ppermute(x, 'expert', [(n, target(n)) for n in everyone])  41.2 us
    pallas_call x1, Pallas kernels, shards(): call(functools.partial(expert_kernel, count), 'expert', [back_shape] * co...  17.4 us
    ppermute x10, starting transfers between devices, permute(): return lax.ppermute(x, 'expert', [(n, target(n)) for n in everyone])  15.5 us
    ppermute x10, starting transfers between devices, restore(): return lax.ppermute(x, 'expert', [(target(n), n) for n in everyone])  11.3 us
    unnamed x24, local copies, waits for them, and re-layouts  3.99 us
    pallas_call x1, Pallas kernels, shards(): call(pack_kernel, 'pack', [pltpu.VMEM(chunk_shape.shape, BF)] * count, in...  3.45 us
  transfers between devices with their start and end apart: 22, of which 15 were waited for; matrix products, arithmetic and copies ran while one was open for 0% of the time, Pallas kernels for 5%

profile of v7, /device:TPU:1, one launch (start us, length us, event | category | flops | bytes accessed | tf_op | source)
XLA Modules:
  0.0 163.3 jit_solution(12214529105061412358)
XLA Ops:
  7.2 0.0 all-gather.3.cloned.1.call-start
  7.2 2.3 %head.1 = (bf16[2,192,768]{2,1,0:T(8,128)(2,1)}, bf16[272,1024]{1,0:T(8,128)(2,1)}) custom-call(s32[8,128]{1,0:T(8,128)} %bitcast.16, f32[8,128]{1,0:T(8,128)} %bitcast.17, bf16[128,1024]{1,0:T(8,128)(2,1)} %tokens_ref.1, bf16[128,1024]{1,0:T(8,128)(2,1)} %cot_ref.1, bf16[2,128,768]{2,1,0:T(8,128)(2,1)} %lift_ref.1, bf16[2,384,128]{2,1,0:T(8,128)(2,1)} %down_ref.1), custom_call_target="tpu_custom_call" | custom-call | bytes 2097152 | tf_op jit(solution)/shard_map/head/pallas_call | solution.py:243
  9.6 0.0 reduce-scatter.2.cloned.1.call-start
  9.6 3.6 %collective-permute-start.2 = (bf16[272,1024]{1,0:T(8,128)(2,1)}, bf16[272,1024]{1,0:T(8,128)(2,1)S(1)}, u32[]{:S(2)}, u32[]{:S(2)}) collective-permute-start(bf16[272,1024]{1,0:T(8,128)(2,1)} %get-tuple-element.31.refs_0_), channel_id=1, source_target_pairs={{0,192},{8,56},{16,208},{24,8},{32,224},{40,24},{48,240},{56,40},{... | collective-permute-start | bytes 1671176 | tf_op jit(solution)/shard_map/ppermute | solution.py:225
  13.3 0.3 collective-permute-start.1
  13.6 0.7 collective-permute-start
  14.3 0.7 dynamic-slice_bitcast_fusion.first_ref
  15.0 11.0 %collective-permute-done.2.refs_3_ = bf16[272,1024]{1,0:T(8,128)(2,1)S(1)} collective-permute-done((bf16[272,1024]{1,0:T(8,128)(2,1)}, bf16[272,1024]{1,0:T(8,128)(2,1)S(1)}, u32[]{:S(2)}, u32[]{:S(2)}) %collective-permute-start.2) | collective-permute-done | bytes 557088 | tf_op jit(solution)/shard_map/ppermute | solution.py:225
  26.0 3.7 %collective-permute-done.refs_1_ = bf16[272,1024]{1,0:T(8,128)(2,1)S(1)} collective-permute-done((bf16[272,1024]{1,0:T(8,128)(2,1)}, bf16[272,1024]{1,0:T(8,128)(2,1)S(1)}, u32[]{:S(2)}, u32[]{:S(2)}) %collective-permute-start) | collective-permute-done | bytes 557088 | tf_op jit(solution)/shard_map/ppermute | solution.py:225
  29.7 3.4 %pack.1 = (bf16[2,2,96,1024]{3,2,1,0:T(8,128)(2,1)S(1)}, bf16[2,2,96,1024]{3,2,1,0:T(8,128)(2,1)S(1)}, bf16[2,2,96,1024]{3,2,1,0:T(8,128)(2,1)S(1)}, bf16[2,2,96...) custom-call(s32[8]{0:T(128)S(1)} %dynamic-slice_bitcast_fusion.first, ...), custom_call_target="tpu_custom_call" | custom-call | flops 805306368 | bytes 16777216 | tf_op jit(solution)/shard_map/pack/pallas_call | solution.py:261
  33.2 1.5 collective-permute-start.3
  34.7 0.6 collective-permute-start.5
  35.3 2.5 %collective-permute-start.6 = (bf16[2,2,96,1024]{3,2,1,0:T(8,128)(2,1)S(1)}, bf16[2,2,96,1024]{3,2,1,0:T(8,128)(2,1)S(1)}, u32[]{:S(2)}, u32[]{:S(2)}) collective-permute-start(bf16[2,2,96,1024]{3,2,1,0:T(8,128)(2,1)S(1)} %get-tuple-element.36), channel_id=1, source_target_pairs={{0,32},{8,136},{16,48},{24,152},{32,0},{40,168},{48,16},{56,184},{... | collective-permute-start | bytes 2359304 | tf_op jit(solution)/shard_map/ppermute | solution.py:225
  37.8 2.9 %collective-permute-start.7 = (bf16[2,2,96,1024]{3,2,1,0:T(8,128)(2,1)S(1)}, bf16[2,2,96,1024]{3,2,1,0:T(8,128)(2,1)S(1)}, u32[]{:S(2)}, u32[]{:S(2)}) collective-permute-start(bf16[2,2,96,1024]{3,2,1,0:T(8,128)(2,1)S(1)} %get-tuple-element.37), channel_id=1, source_target_pairs={{0,40},{8,128},{16,56},{24,144},{32,8},{40,160},{48,24},{56,176},{... | collective-permute-start | bytes 2359304 | tf_op jit(solution)/shard_map/ppermute | solution.py:225
  40.7 1.1 collective-permute-start.8
  41.8 5.4 %collective-permute-done.4.refs_2_ = bf16[2,2,96,1024]{3,2,1,0:T(8,128)(2,1)S(1)} collective-permute-done((bf16[2,2,96,1024]{3,2,1,0:T(8,128)(2,1)S(1)}, bf16[2,2,96,1024]{3,2,1,0:T(8,128)(2,1)S(1)}, u32[]{:S(2)}, u32[]{:S(2)}) %collective-permute-start.4) | collective-permute-done | bytes 786464 | tf_op jit(solution)/shard_map/ppermute | solution.py:225
  47.2 2.2 %collective-permute-start.9 = (bf16[2,2,96,1024]{3,2,1,0:T(8,128)(2,1)S(1)}, bf16[2,2,96,1024]{3,2,1,0:T(8,128)(2,1)}, u32[]{:S(2)}, u32[]{:S(2)}) collective-permute-start(bf16[2,2,96,1024]{3,2,1,0:T(8,128)(2,1)S(1)} %get-tuple-element.39), channel_id=1, source_target_pairs={{0,56},{8,192},{16,8},{24,208},{32,24},{40,224},{48,40},{56,240},{... | collective-permute-start | bytes 2359304 | tf_op jit(solution)/shard_map/ppermute | solution.py:225
  49.4 1.1 copy-done.4
  50.4 1.2 plan.1.refs_9_.pick_ref
  51.6 1.1 copy-done
  52.7 3.4 %collective-permute-done.5.refs_3_ = bf16[2,2,96,1024]{3,2,1,0:T(8,128)(2,1)S(1)} collective-permute-done((bf16[2,2,96,1024]{3,2,1,0:T(8,128)(2,1)S(1)}, bf16[2,2,96,1024]{3,2,1,0:T(8,128)(2,1)S(1)}, u32[]{:S(2)}, u32[]{:S(2)}) %collective-permute-start.5) | collective-permute-done | bytes 786464 | tf_op jit(solution)/shard_map/ppermute | solution.py:225
  56.1 7.4 %collective-permute-done.6.refs_4_ = bf16[2,2,96,1024]{3,2,1,0:T(8,128)(2,1)S(1)} collective-permute-done((bf16[2,2,96,1024]{3,2,1,0:T(8,128)(2,1)S(1)}, bf16[2,2,96,1024]{3,2,1,0:T(8,128)(2,1)S(1)}, u32[]{:S(2)}, u32[]{:S(2)}) %collective-permute-start.6) | collective-permute-done | bytes 786464 | tf_op jit(solution)/shard_map/ppermute | solution.py:225
  63.6 10.3 %collective-permute-done.7.refs_5_ = bf16[2,2,96,1024]{3,2,1,0:T(8,128)(2,1)S(1)} collective-permute-done((bf16[2,2,96,1024]{3,2,1,0:T(8,128)(2,1)S(1)}, bf16[2,2,96,1024]{3,2,1,0:T(8,128)(2,1)S(1)}, u32[]{:S(2)}, u32[]{:S(2)}) %collective-permute-start.7) | collective-permute-done | bytes 786464 | tf_op jit(solution)/shard_map/ppermute | solution.py:225
  73.9 0.8 copy-done.10
  74.7 0.9 copy-done.11
  75.7 17.4 %expert.1 = (bf16[2,4,2,24,1024]{4,3,2,1,0:T(8,128)(2,1)}, bf16[2,4,2,24,1024]{4,3,2,1,0:T(8,128)(2,1)}, bf16[2,4,2,24,1024]{4,3,2,1,0:T(8,128)(2,1)}, bf16[2,4,...) custom-call(bf16[2,2,96,1024]{3,2,1,0:T(8,128)(2,1)} %copy-done.2, ...), custom_call_target="tpu_custom_call" | custom-call | flops 10871635968 | bytes 25165824 | tf_op jit(solution)/shard_map/expert/pallas_call | solution.py:291
  93.1 0.1 collective-permute-start.10
  93.2 0.1 collective-permute-start.11
  93.3 2.1 %collective-permute-start.12 = (bf16[2,4,48,1024]{3,2,1,0:T(8,128)(2,1)}, bf16[2,4,48,1024]{3,2,1,0:T(8,128)(2,1)S(1)}, u32[]{:S(2)}, u32[]{:S(2)}) collective-permute-start(bf16[2,4,48,1024]{3,2,1,0:T(8,128)(2,1)} %bitcast.23), channel_id=1, source_target_pairs={{56,0},{192,8},{8,16},{208,24},{24,32},{224,40},{40,48},{240,56},{... | collective-permute-start | bytes 2359304 | tf_op jit(solution)/shard_map/ppermute | solution.py:234
  95.5 1.5 collective-permute-start.13
  97.0 0.5 collective-permute-start.14
  97.5 2.6 %collective-permute-start.15 = (bf16[2,4,48,1024]{3,2,1,0:T(8,128)(2,1)}, bf16[2,4,48,1024]{3,2,1,0:T(8,128)(2,1)S(1)}, u32[]{:S(2)}, u32[]{:S(2)}) collective-permute-start(bf16[2,4,48,1024]{3,2,1,0:T(8,128)(2,1)} %bitcast.20), channel_id=1, source_target_pairs={{16,0},{72,8},{32,16},{88,24},{48,32},{104,40},{0,48},{120,56},{80... | collective-permute-start | bytes 2359304 | tf_op jit(solution)/shard_map/ppermute | solution.py:234
  100.1 13.6 %collective-permute-done.11.refs_2_ = bf16[2,4,48,1024]{3,2,1,0:T(8,128)(2,1)S(1)} collective-permute-done((bf16[2,4,48,1024]{3,2,1,0:T(8,128)(2,1)}, bf16[2,4,48,1024]{3,2,1,0:T(8,128)(2,1)S(1)}, u32[]{:S(2)}, u32[]{:S(2)}) %collective-permute-start.11) | collective-permute-done | bytes 786464 | tf_op jit(solution)/shard_map/ppermute | solution.py:234
  113.7 1.6 %collective-permute-start.16 = (bf16[2,4,48,1024]{3,2,1,0:T(8,128)(2,1)S(1)}, bf16[2,4,48,1024]{3,2,1,0:T(8,128)(2,1)S(1)}, u32[]{:S(2)}, u32[]{:S(2)}) collective-permute-start(bf16[2,4,48,1024]{3,2,1,0:T(8,128)(2,1)S(1)} %bitcast.19), channel_id=1, source_target_pairs={{24,0},{64,8},{40,16},{80,24},{56,32},{96,40},{8,48},{112,56},{88,... | collective-permute-start | bytes 2359304 | tf_op jit(solution)/shard_map/ppermute | solution.py:234
  115.3 0.7 collective-permute-done.12.refs_3_
  116.0 13.6 %collective-permute-done.13.refs_4_ = bf16[2,4,48,1024]{3,2,1,0:T(8,128)(2,1)S(1)} collective-permute-done((bf16[2,4,48,1024]{3,2,1,0:T(8,128)(2,1)}, bf16[2,4,48,1024]{3,2,1,0:T(8,128)(2,1)S(1)}, u32[]{:S(2)}, u32[]{:S(2)}) %collective-permute-start.13) | collective-permute-done | bytes 786464 | tf_op jit(solution)/shard_map/ppermute | solution.py:234
  129.6 1.7 %collective-permute-done.14.refs_5_ = bf16[2,4,48,1024]{3,2,1,0:T(8,128)(2,1)S(1)} collective-permute-done((bf16[2,4,48,1024]{3,2,1,0:T(8,128)(2,1)}, bf16[2,4,48,1024]{3,2,1,0:T(8,128)(2,1)S(1)}, u32[]{:S(2)}, u32[]{:S(2)}) %collective-permute-start.14) | collective-permute-done | bytes 786464 | tf_op jit(solution)/shard_map/ppermute | solution.py:234
  131.3 0.9 collective-permute-done.15.refs_6_
  132.1 1.2 collective-permute-done.16.refs_7_
  133.4 2.5 %combine.1 = (f32[2,128,1024]{2,1,0:T(8,128)S(1)}, bf16[2,128,1024]{2,1,0:T(8,128)(2,1)S(1)}, bf16[2,128,1024]{2,1,0:T(8,128)(2,1)S(1)}, bf16[2,128,1024]{2,1,0:T(8,128)(2,1)S(1)}) custom-call(bf16[2,4,256,384]{3,2,1,0:T(8,128)(2,1)S(1)} %copy-done.1, bf16[2,4,48,1024]{3,2,1,0:T(8,128)(2,1)S(1)} %bitcast.14, ...), custom_call_target="tpu_custom_call" | custom-call | flops 1610612736 | bytes 10485760 | tf_op jit(solution)/shard_map/combine/pallas_call | solution.py:310
  135.9 2.1 %collective-permute-start.17 = (bf16[2,128,1024]{2,1,0:T(8,128)(2,1)S(1)}, bf16[2,128,1024]{2,1,0:T(8,128)(2,1)S(1)}, u32[]{:S(2)}, u32[]{:S(2)}) collective-permute-start(bf16[2,128,1024]{2,1,0:T(8,128)(2,1)S(1)} %get-tuple-element.50), channel_id=1, source_target_pairs={{64,0},{24,8},{80,16},{40,24},{96,32},{56,40},{112,48},{8,56},{128... | collective-permute-start | bytes 1572872 | tf_op jit(solution)/shard_map/ppermute | solution.py:234
  138.0 0.0 collective-permute-start.18
  138.0 0.6 collective-permute-start.19
  138.7 11.1 %collective-permute-done.17.refs_0_ = bf16[2,128,1024]{2,1,0:T(8,128)(2,1)S(1)} collective-permute-done((bf16[2,128,1024]{2,1,0:T(8,128)(2,1)S(1)}, bf16[2,128,1024]{2,1,0:T(8,128)(2,1)S(1)}, u32[]{:S(2)}, u32[]{:S(2)}) %collective-permute-start.17) | collective-permute-done | bytes 524320 | tf_op jit(solution)/shard_map/ppermute | solution.py:234
  149.7 3.5 %collective-permute-done.19.refs_2_ = bf16[2,128,1024]{2,1,0:T(8,128)(2,1)S(1)} collective-permute-done((bf16[2,128,1024]{2,1,0:T(8,128)(2,1)S(1)}, bf16[2,128,1024]{2,1,0:T(8,128)(2,1)S(1)}, u32[]{:S(2)}, u32[]{:S(2)}) %collective-permute-start.19) | collective-permute-done | bytes 524320 | tf_op jit(solution)/shard_map/ppermute | solution.py:234
  153.3 0.9 total.1
  154.2 0.3 reduce-scatter.2.cloned.1.call-done
  154.6 1.9 %split.1 = (bf16[2,128,768]{2,1,0:T(8,128)(2,1)}, bf16[2,384,128]{2,1,0:T(8,128)(2,1)}) custom-call(bf16[2,192,768]{2,1,0:T(8,128)(2,1)} %bitcast.15), custom_call_target="tpu_custom_call" | custom-call | bytes 1048576 | tf_op jit(solution)/shard_map/split/pallas_call | solution.py:331
  (30 shorter events, 0.1 us)
Async XLA Ops:
  7.2 68.5 %all-gather.3.cloned.1.call-start = ((), (), s32[]{:S(2)}) async-start(), calls=%async_computation.2 | async-start | bytes 5308416 | tf_op jit(solution)/shard_map/all_gather | solution.py:255
  9.6 145.0 %reduce-scatter.2.cloned.1.call-start = ((), (), s32[]{:S(2)}) async-start(), calls=%async_computation.1 | async-start | bytes 5308416 | tf_op jit(solution)/shard_map/reduce_scatter | solution.py:304
  9.6 16.4 %collective-permute-start.2 = (bf16[272,1024]{1,0:T(8,128)(2,1)}, bf16[272,1024]{1,0:T(8,128)(2,1)S(1)}, u32[]{:S(2)}, u32[]{:S(2)}) collective-permute-start(bf16[272,1024]{1,0:T(8,128)(2,1)} %get-tuple-element.31.refs_0_), channel_id=1, source_target_pairs={{0,192},{8,56},{16,208},{24,8},{32,224},{40,24},{48,240},{56,40},{... | collective-permute-start | bytes 1671176 | tf_op jit(solution)/shard_map/ppermute | solution.py:225
  13.3 12.8 %collective-permute-start.1 = (bf16[272,1024]{1,0:T(8,128)(2,1)}, bf16[272,1024]{1,0:T(8,128)(2,1)S(1)}, u32[]{:S(2)}, u32[]{:S(2)}) collective-permute-start(bf16[272,1024]{1,0:T(8,128)(2,1)} %get-tuple-element.31.refs_0_), channel_id=1, source_target_pairs={{0,128},{8,40},{16,144},{24,56},{32,160},{40,8},{48,176},{56,24},{... | collective-permute-start | bytes 1671176 | tf_op jit(solution)/shard_map/ppermute | solution.py:225
  13.6 16.1 %collective-permute-start = (bf16[272,1024]{1,0:T(8,128)(2,1)}, bf16[272,1024]{1,0:T(8,128)(2,1)S(1)}, u32[]{:S(2)}, u32[]{:S(2)}) collective-permute-start(bf16[272,1024]{1,0:T(8,128)(2,1)} %get-tuple-element.31.refs_0_), channel_id=1, source_target_pairs={{0,64},{8,24},{16,80},{24,40},{32,96},{40,56},{48,112},{56,8},{64,... | collective-permute-start | bytes 1671176 | tf_op jit(solution)/shard_map/ppermute | solution.py:225
  33.2 42.5 %copy-start.2 = (bf16[2,2,96,1024]{3,2,1,0:T(8,128)(2,1)}, bf16[2,2,96,1024]{3,2,1,0:T(8,128)(2,1)S(1)}, u32[]{:S(2)}) copy-start(bf16[2,2,96,1024]{3,2,1,0:T(8,128)(2,1)S(1)} %get-tuple-element.32.refs_4_.refs_0_) | copy-start | bytes 2359300
  33.2 7.5 %collective-permute-start.3 = (bf16[2,2,96,1024]{3,2,1,0:T(8,128)(2,1)S(1)}, bf16[2,2,96,1024]{3,2,1,0:T(8,128)(2,1)S(1)}, u32[]{:S(2)}, u32[]{:S(2)}) collective-permute-start(bf16[2,2,96,1024]{3,2,1,0:T(8,128)(2,1)S(1)} %get-tuple-element.33), channel_id=1, source_target_pairs={{0,8},{8,0},{16,24},{24,16},{32,40},{40,32},{48,56},{56,48},{64,72... | collective-permute-start | bytes 2359304 | tf_op jit(solution)/shard_map/ppermute | solution.py:225
  34.7 12.5 %collective-permute-start.4 = (bf16[2,2,96,1024]{3,2,1,0:T(8,128)(2,1)S(1)}, bf16[2,2,96,1024]{3,2,1,0:T(8,128)(2,1)S(1)}, u32[]{:S(2)}, u32[]{:S(2)}) collective-permute-start(bf16[2,2,96,1024]{3,2,1,0:T(8,128)(2,1)S(1)} %get-tuple-element.34), channel_id=1, source_target_pairs={{0,16},{8,72},{16,32},{24,88},{32,48},{40,104},{48,0},{56,120},{64... | collective-permute-start | bytes 2359304 | tf_op jit(solution)/shard_map/ppermute | solution.py:225
  34.7 21.4 %collective-permute-start.5 = (bf16[2,2,96,1024]{3,2,1,0:T(8,128)(2,1)S(1)}, bf16[2,2,96,1024]{3,2,1,0:T(8,128)(2,1)S(1)}, u32[]{:S(2)}, u32[]{:S(2)}) collective-permute-start(bf16[2,2,96,1024]{3,2,1,0:T(8,128)(2,1)S(1)} %get-tuple-element.35), channel_id=1, source_target_pairs={{0,24},{8,64},{16,40},{24,80},{32,56},{40,96},{48,8},{56,112},{64,... | collective-permute-start | bytes 2359304 | tf_op jit(solution)/shard_map/ppermute | solution.py:225
  35.3 28.3 %collective-permute-start.6 = (bf16[2,2,96,1024]{3,2,1,0:T(8,128)(2,1)S(1)}, bf16[2,2,96,1024]{3,2,1,0:T(8,128)(2,1)S(1)}, u32[]{:S(2)}, u32[]{:S(2)}) collective-permute-start(bf16[2,2,96,1024]{3,2,1,0:T(8,128)(2,1)S(1)} %get-tuple-element.36), channel_id=1, source_target_pairs={{0,32},{8,136},{16,48},{24,152},{32,0},{40,168},{48,16},{56,184},{... | collective-permute-start | bytes 2359304 | tf_op jit(solution)/shard_map/ppermute | solution.py:225
  37.8 36.1 %collective-permute-start.7 = (bf16[2,2,96,1024]{3,2,1,0:T(8,128)(2,1)S(1)}, bf16[2,2,96,1024]{3,2,1,0:T(8,128)(2,1)S(1)}, u32[]{:S(2)}, u32[]{:S(2)}) collective-permute-start(bf16[2,2,96,1024]{3,2,1,0:T(8,128)(2,1)S(1)} %get-tuple-element.37), channel_id=1, source_target_pairs={{0,40},{8,128},{16,56},{24,144},{32,8},{40,160},{48,24},{56,176},{... | collective-permute-start | bytes 2359304 | tf_op jit(solution)/shard_map/ppermute | solution.py:225
  40.7 34.9 %copy-start.5 = (bf16[2,2,96,1024]{3,2,1,0:T(8,128)(2,1)}, bf16[2,2,96,1024]{3,2,1,0:T(8,128)(2,1)S(1)}, u32[]{:S(2)}) copy-start(bf16[2,2,96,1024]{3,2,1,0:T(8,128)(2,1)S(1)} %collective-permute-done.3.refs_1_) | copy-start | bytes 2359300
  40.7 33.1 %collective-permute-start.8 = (bf16[2,2,96,1024]{3,2,1,0:T(8,128)(2,1)S(1)}, bf16[2,2,96,1024]{3,2,1,0:T(8,128)(2,1)S(1)}, u32[]{:S(2)}, u32[]{:S(2)}) collective-permute-start(bf16[2,2,96,1024]{3,2,1,0:T(8,128)(2,1)S(1)} %get-tuple-element.38), channel_id=1, source_target_pairs={{0,48},{8,200},{16,0},{24,216},{32,16},{40,232},{48,32},{56,248},{... | collective-permute-start | bytes 2359304 | tf_op jit(solution)/shard_map/ppermute | solution.py:225
  47.2 26.7 %copy-start.6 = (bf16[2,2,96,1024]{3,2,1,0:T(8,128)(2,1)}, bf16[2,2,96,1024]{3,2,1,0:T(8,128)(2,1)S(1)}, u32[]{:S(2)}) copy-start(bf16[2,2,96,1024]{3,2,1,0:T(8,128)(2,1)S(1)} %collective-permute-done.4.refs_2_) | copy-start | bytes 2359300
  47.2 28.5 %collective-permute-start.9 = (bf16[2,2,96,1024]{3,2,1,0:T(8,128)(2,1)S(1)}, bf16[2,2,96,1024]{3,2,1,0:T(8,128)(2,1)}, u32[]{:S(2)}, u32[]{:S(2)}) collective-permute-start(bf16[2,2,96,1024]{3,2,1,0:T(8,128)(2,1)S(1)} %get-tuple-element.39), channel_id=1, source_target_pairs={{0,56},{8,192},{16,8},{24,208},{32,24},{40,224},{48,40},{56,240},{... | collective-permute-start | bytes 2359304 | tf_op jit(solution)/shard_map/ppermute | solution.py:225
  49.4 1.1 copy-start.4
  51.6 1.1 copy-start
  56.1 17.7 %copy-start.8 = (bf16[2,2,96,1024]{3,2,1,0:T(8,128)(2,1)}, bf16[2,2,96,1024]{3,2,1,0:T(8,128)(2,1)S(1)}, u32[]{:S(2)}) copy-start(bf16[2,2,96,1024]{3,2,1,0:T(8,128)(2,1)S(1)} %collective-permute-done.5.refs_3_) | copy-start | bytes 2359300
  63.6 10.3 %copy-start.9 = (bf16[2,2,96,1024]{3,2,1,0:T(8,128)(2,1)}, bf16[2,2,96,1024]{3,2,1,0:T(8,128)(2,1)S(1)}, u32[]{:S(2)}) copy-start(bf16[2,2,96,1024]{3,2,1,0:T(8,128)(2,1)S(1)} %collective-permute-done.6.refs_4_) | copy-start | bytes 2359300
  73.8 0.9 copy-start.10
  74.7 0.9 copy-start.11
  93.1 20.6 %copy-start.7 = (bf16[2,4,2,24,1024]{4,3,2,1,0:T(8,128)(2,1)S(1)}, bf16[2,4,2,24,1024]{4,3,2,1,0:T(8,128)(2,1)}, u32[]{:S(2)}) copy-start(bf16[2,4,2,24,1024]{4,3,2,1,0:T(8,128)(2,1)} %get-tuple-element.48) | copy-start | bytes 2359300
  93.1 40.3 %copy-start.1 = (bf16[2,4,256,384]{3,2,1,0:T(8,128)(2,1)S(1)}, bf16[2,4,256,384]{3,2,1,0:T(8,128)(2,1)}, u32[]{:S(2)}) copy-start(bf16[2,4,256,384]{3,2,1,0:T(8,128)(2,1)} %copy-done) | copy-start | bytes 4718596
  93.1 40.3 %copy-start.3 = (bf16[2,4,2,24,1024]{4,3,2,1,0:T(8,128)(2,1)S(1)}, bf16[2,4,2,24,1024]{4,3,2,1,0:T(8,128)(2,1)}, u32[]{:S(2)}) copy-start(bf16[2,4,2,24,1024]{4,3,2,1,0:T(8,128)(2,1)} %get-tuple-element.41) | copy-start | bytes 2359300
  93.1 4.4 %collective-permute-start.10 = (bf16[2,4,48,1024]{3,2,1,0:T(8,128)(2,1)}, bf16[2,4,48,1024]{3,2,1,0:T(8,128)(2,1)S(1)}, u32[]{:S(2)}, u32[]{:S(2)}) collective-permute-start(bf16[2,4,48,1024]{3,2,1,0:T(8,128)(2,1)} %bitcast.25), channel_id=1, source_target_pairs={{8,0},{0,8},{24,16},{16,24},{40,32},{32,40},{56,48},{48,56},{72,64... | collective-permute-start | bytes 2359304 | tf_op jit(solution)/shard_map/ppermute | solution.py:234
  93.2 20.4 %collective-permute-start.11 = (bf16[2,4,48,1024]{3,2,1,0:T(8,128)(2,1)}, bf16[2,4,48,1024]{3,2,1,0:T(8,128)(2,1)S(1)}, u32[]{:S(2)}, u32[]{:S(2)}) collective-permute-start(bf16[2,4,48,1024]{3,2,1,0:T(8,128)(2,1)} %bitcast.24), channel_id=1, source_target_pairs={{48,0},{200,8},{0,16},{216,24},{16,32},{232,40},{32,48},{248,56},{... | collective-permute-start | bytes 2359304 | tf_op jit(solution)/shard_map/ppermute | solution.py:234
  93.3 22.7 %collective-permute-start.12 = (bf16[2,4,48,1024]{3,2,1,0:T(8,128)(2,1)}, bf16[2,4,48,1024]{3,2,1,0:T(8,128)(2,1)S(1)}, u32[]{:S(2)}, u32[]{:S(2)}) collective-permute-start(bf16[2,4,48,1024]{3,2,1,0:T(8,128)(2,1)} %bitcast.23), channel_id=1, source_target_pairs={{56,0},{192,8},{8,16},{208,24},{24,32},{224,40},{40,48},{240,56},{... | collective-permute-start | bytes 2359304 | tf_op jit(solution)/shard_map/ppermute | solution.py:234
  95.5 34.1 %collective-permute-start.13 = (bf16[2,4,48,1024]{3,2,1,0:T(8,128)(2,1)}, bf16[2,4,48,1024]{3,2,1,0:T(8,128)(2,1)S(1)}, u32[]{:S(2)}, u32[]{:S(2)}) collective-permute-start(bf16[2,4,48,1024]{3,2,1,0:T(8,128)(2,1)} %bitcast.22), channel_id=1, source_target_pairs={{32,0},{136,8},{48,16},{152,24},{0,32},{168,40},{16,48},{184,56},{... | collective-permute-start | bytes 2359304 | tf_op jit(solution)/shard_map/ppermute | solution.py:234
  97.0 34.3 %collective-permute-start.14 = (bf16[2,4,48,1024]{3,2,1,0:T(8,128)(2,1)}, bf16[2,4,48,1024]{3,2,1,0:T(8,128)(2,1)S(1)}, u32[]{:S(2)}, u32[]{:S(2)}) collective-permute-start(bf16[2,4,48,1024]{3,2,1,0:T(8,128)(2,1)} %bitcast.21), channel_id=1, source_target_pairs={{40,0},{128,8},{56,16},{144,24},{8,32},{160,40},{24,48},{176,56},{... | collective-permute-start | bytes 2359304 | tf_op jit(solution)/shard_map/ppermute | solution.py:234
  97.5 34.6 %collective-permute-start.15 = (bf16[2,4,48,1024]{3,2,1,0:T(8,128)(2,1)}, bf16[2,4,48,1024]{3,2,1,0:T(8,128)(2,1)S(1)}, u32[]{:S(2)}, u32[]{:S(2)}) collective-permute-start(bf16[2,4,48,1024]{3,2,1,0:T(8,128)(2,1)} %bitcast.20), channel_id=1, source_target_pairs={{16,0},{72,8},{32,16},{88,24},{48,32},{104,40},{0,48},{120,56},{80... | collective-permute-start | bytes 2359304 | tf_op jit(solution)/shard_map/ppermute | solution.py:234
  113.7 19.7 %collective-permute-start.16 = (bf16[2,4,48,1024]{3,2,1,0:T(8,128)(2,1)S(1)}, bf16[2,4,48,1024]{3,2,1,0:T(8,128)(2,1)S(1)}, u32[]{:S(2)}, u32[]{:S(2)}) collective-permute-start(bf16[2,4,48,1024]{3,2,1,0:T(8,128)(2,1)S(1)} %bitcast.19), channel_id=1, source_target_pairs={{24,0},{64,8},{40,16},{80,24},{56,32},{96,40},{8,48},{112,56},{88,... | collective-permute-start | bytes 2359304 | tf_op jit(solution)/shard_map/ppermute | solution.py:234
  135.9 13.8 %collective-permute-start.17 = (bf16[2,128,1024]{2,1,0:T(8,128)(2,1)S(1)}, bf16[2,128,1024]{2,1,0:T(8,128)(2,1)S(1)}, u32[]{:S(2)}, u32[]{:S(2)}) collective-permute-start(bf16[2,128,1024]{2,1,0:T(8,128)(2,1)S(1)} %get-tuple-element.50), channel_id=1, source_target_pairs={{64,0},{24,8},{80,16},{40,24},{96,32},{56,40},{112,48},{8,56},{128... | collective-permute-start | bytes 1572872 | tf_op jit(solution)/shard_map/ppermute | solution.py:234
  138.0 11.7 %collective-permute-start.18 = (bf16[2,128,1024]{2,1,0:T(8,128)(2,1)S(1)}, bf16[2,128,1024]{2,1,0:T(8,128)(2,1)S(1)}, u32[]{:S(2)}, u32[]{:S(2)}) collective-permute-start(bf16[2,128,1024]{2,1,0:T(8,128)(2,1)S(1)} %get-tuple-element.51), channel_id=1, source_target_pairs={{128,0},{40,8},{144,16},{56,24},{160,32},{8,40},{176,48},{24,56},{... | collective-permute-start | bytes 1572872 | tf_op jit(solution)/shard_map/ppermute | solution.py:234
  138.0 15.3 %collective-permute-start.19 = (bf16[2,128,1024]{2,1,0:T(8,128)(2,1)S(1)}, bf16[2,128,1024]{2,1,0:T(8,128)(2,1)S(1)}, u32[]{:S(2)}, u32[]{:S(2)}) collective-permute-start(bf16[2,128,1024]{2,1,0:T(8,128)(2,1)S(1)} %get-tuple-element.52), channel_id=1, source_target_pairs={{192,0},{56,8},{208,16},{8,24},{224,32},{24,40},{240,48},{40,56},{... | collective-permute-start | bytes 1572872 | tf_op jit(solution)/shard_map/ppermute | solution.py:234
Sparse Core Ops, SparseCore 0:
  9.8 63.5 all-gather.2
  93.3 61.2 reduce-scatter.1
